TPU v7x, 256 devices: a whole 4x4x8 slice. The times are simulated.
256 devices in a mesh: image: 16 (over x, y_lo, core), space: 16 (over z, y_hi).
Axes of the slice: x: 4, y: 4 (y_hi: 2, y_lo: 2; y = y_hi * 2 + y_lo), z: 8, core: 2. Of those that a mesh axis runs over, the one named last changes fastest.
Arguments:
- coords: float32 [32, 3, 131072], P('image', None, 'space'), may hold values from -16 to 16
- ref_coords: float32 [3, 131072], P(None, 'space'), may hold values from -4 to 4
- restraint: float32 [131072], P('space'), may hold values from 0.5 to 5
- atom_types: int32 [131072], P('space'), may hold values from 0 to 63
- well_table: float32 [64], replicated, may hold values from 0.3 to 1.5
- radius_table: float32 [64], replicated, may hold values from 0.4 to 1
- tile_lists: int32 [32, 4, 1024], P('image', None, 'space'), may hold values from 0 to 79
- halo_index: int32 [32, 2, 16384], P('image', None, 'space'), may hold values from 0 to 8191
Outputs:
- neb_force: float32 [32, 3, 131072], P('image', None, 'space')
- energies: float32 [32], P('image')
All inputs are finite; a program needn't handle non-finite values.
Results may differ from a plain program's by a relative error of at most 0.0001.
Values sent between devices are 32-bit elements; how exact they have to be, the bound alone decides.
No kernel may reach another device: no remote copies, remote signals or barrier semaphores. Data moves between devices by JAX's collectives and lax.ppermute only.
A program may use at most 64 MiB of HBM per device.

v0:
```python
import jax
import jax.numpy as jnp
from jax import lax
from jax.sharding import PartitionSpec as P

TILE = 128


soft_core = 1.0
spring_k = 2.0
small_eps = 1e-06


def extended_2(x, sides, width):
    for axis, dim in sides:
        devices, length = (lax.axis_size(axis), x.shape[dim])
        up = [(i, (i + 1) % devices) for i in range(devices - 1)]
        down = [(j, i) for i, j in up]
        last = lax.slice_in_dim(x, length - width, length, axis=dim)
        leading = lax.slice_in_dim(x, 0, width, axis=dim)
        before = lax.ppermute(last, axis, up)
        after = lax.ppermute(leading, axis, down)
        x = jnp.concatenate([before, x, after], axis=dim)
    return x


def pair_terms(own, partner):
    delta = own[:3, ..., :, None] - partner[:3, ..., None, :]
    dist_sq = jnp.sum(delta * delta, axis=0)
    reach = own[4, ..., :, None] + partner[4, ..., None, :]
    reach_sq = reach * reach
    ratio = reach_sq / (dist_sq + soft_core * reach_sq)
    cubed = ratio * ratio * ratio
    strength = own[3, ..., :, None] * partner[3, ..., None, :]
    energy = jnp.sum(4.0 * strength * (cubed * cubed - cubed), axis=(-2, -1))
    coeff = 24.0 * strength * (2.0 * cubed * cubed - cubed) * ratio / reach_sq
    force = jnp.sum(coeff[None] * delta, axis=-1)
    return (force, energy)


def image_total(values):
    return jnp.sum(values, axis=(1, 2))


def body(
    coords, ref_coords, restraint, atom_types, well_table, radius_table, tile_lists, halo_index
):
    img_local, _, atoms_local = coords.shape
    tiles_local = atoms_local // TILE
    kinds = well_table.shape[0]
    table = jnp.stack([well_table, radius_table])
    onehot = (atom_types[None, :] == jnp.arange(kinds, dtype=jnp.int32)[:, None]).astype(
        jnp.float32
    )
    params = jnp.dot(table, onehot, precision=lax.Precision.HIGHEST)
    feats = jnp.concatenate(
        [coords, jnp.broadcast_to(params[None], (img_local, 2, atoms_local))], axis=1
    )
    pick_atoms = jax.vmap(lambda source, index: source[:, index])
    pick_tiles = jax.vmap(lambda source, index: source[:, index, :])
    wide = extended_2(feats, (("space", 2),), atoms_local)
    lower = pick_atoms(wide[:, :, :atoms_local], halo_index[:, 0])
    upper = pick_atoms(wide[:, :, 2 * atoms_local :], halo_index[:, 1])
    extended = jnp.concatenate([feats, lower, upper], axis=2).reshape(img_local, 5, -1, TILE)
    own = feats.reshape(img_local, 5, tiles_local, TILE).transpose(1, 0, 2, 3)

    def add_partner(carry, index):
        partner = pick_tiles(extended, index).transpose(1, 0, 2, 3)
        force, energy = pair_terms(own, partner)
        return ((carry[0] + force, carry[1] + jnp.sum(energy, axis=1)), None)

    start = (
        jnp.zeros((3, img_local, tiles_local, TILE), jnp.float32),
        jnp.zeros((img_local,), jnp.float32),
    )
    (pair_force, pair_energy), _ = lax.scan(
        add_partner, start, jnp.transpose(tile_lists, (1, 0, 2))
    )
    pair_force = pair_force.transpose(1, 0, 2, 3).reshape(img_local, 3, atoms_local)
    offset = coords - ref_coords[None]
    forces = pair_force - restraint[None, None] * offset
    local_energy = 0.5 * pair_energy + 0.5 * image_total(restraint[None, None] * offset * offset)
    rims = extended_2(coords, (("image", 0),), 1)
    ahead = rims[2:] - coords
    behind = coords - rims[:-2]
    ahead_sq, behind_sq = lax.psum(
        (image_total(ahead * ahead), image_total(behind * behind)), "space"
    )
    ahead_len = jnp.sqrt(ahead_sq + small_eps)[:, None, None]
    behind_len = jnp.sqrt(behind_sq + small_eps)[:, None, None]
    tangent = ahead / ahead_len + behind / behind_len
    tan_sq, force_tan, energy_sum = lax.psum(
        (image_total(tangent * tangent), image_total(forces * tangent), local_energy), "space"
    )
    tan_len = jnp.sqrt(tan_sq + small_eps)[:, None, None]
    unit = tangent / tan_len
    along = force_tan[:, None, None] / tan_len
    banded = forces - along * unit + spring_k * (ahead_len - behind_len) * unit
    total_images = img_local * lax.axis_size("image")
    order = lax.axis_index("image") * img_local + jnp.arange(img_local, dtype=jnp.int32)
    ends = ((order == 0) | (order == total_images - 1))[:, None, None]
    neb_force = jnp.where(ends, forces, banded)
    energies = energy_sum / (atoms_local * lax.axis_size("space"))
    return (neb_force, energies)


def solution(mesh):
    in_specs = (
        P("image", None, "space"),
        P(None, "space"),
        P("space"),
        P("space"),
        P(),
        P(),
        P("image", None, "space"),
        P("image", None, "space"),
    )
    out_specs = (P("image", None, "space"), P("image"))
    return jax.shard_map(body, mesh=mesh, in_specs=in_specs, out_specs=out_specs, check_vma=False)
```

profile of v0, /device:TPU:6, one launch (start us, length us, event | category | flops | bytes accessed | tf_op | source)
XLA Modules:
  0.0 312.5 jit_solution(17228161440838271168)
XLA Ops:
  4.6 6.1 %collective-permute-start = (f32[2,5,8192]{2,0,1:T(2,128)S(1)}, f32[2,5,8192]{2,0,1:T(2,128)S(1)}, u32[]{:S(2)}, u32[]{:S(2)}) collective-permute-start(f32[2,5,8192]{2,0,1:T(2,128)S(1)} %pad_maximum_fusion.1), channel_id=1, source_target_pairs={{0,1},{1,2},{2,3},{3,4},{4,5},{5,6},{6,7},{7,8},{8,9},{9,10},{10,1... | collective-permute-start | bytes 983048 | tf_op jit(solution)/shard_map/ppermute | solution.py:21
  11.9 2.6 collective-permute-start.2
  14.5 1.9 collective-permute-start.3
  18.3 3.1 %collective-permute-done.3 = f32[1,3,8192]{2,0,1:T(1,128)S(1)} collective-permute-done((f32[1,3,8192]{2,0,1:T(1,128)S(1)}, f32[1,3,8192]{2,0,1:T(1,128)S(1)}, u32[]{:S(2)}, u32[]{:S(2)}) %collective-permute-start.3) | collective-permute-done | bytes 98336 | tf_op jit(solution)/shard_map/ppermute | solution.py:21
  21.5 1.8 multiply_reduce_fusion.3
  23.2 43.9 %all-reduce.1 = (f32[2]{0:T(128)S(1)}, f32[2]{0:T(128)S(1)}) all-reduce(f32[2]{0:T(128)S(1)} %get-tuple-element.86, f32[2]{0:T(128)S(1)} %get-tuple-element.85), channel_id=1, replica_groups=mesh['image'=16,'space'=16] {'space'}, use_global_device_ids=true, to_apply=%region_8.9 | all-reduce | flops 4 | bytes 32 | tf_op jit(solution)/shard_map/psum | solution.py:86
  67.2 4.6 %copy.32 = f32[2,5,8192]{1,2,0:T(8,128)} copy(f32[2,5,8192]{2,0,1:T(2,128)S(1)} %collective-permute-done.1) | data formatting | bytes 655360 | tf_op jit(solution)/shard_map/ppermute | solution.py:22
  71.8 20.5 %gather_fusion.2 = f32[2048,5]{1,0:T(8,128)S(1)} fusion(f32[2,5,8192]{1,2,0:T(8,128)} %copy.32, s32[2048]{0:T(1024)S(1)} %bitcast.49), kind=kCustom, calls=%fused_computation.2 | custom fusion | bytes 98304 | tf_op jit(solution)/shard_map/vmap()/gather | solution.py:59
  92.7 4.7 %copy.30 = f32[2,5,8192]{1,2,0:T(8,128)} copy(f32[2,5,8192]{2,0,1:T(2,128)S(1)} %collective-permute-done) | data formatting | bytes 655360 | tf_op jit(solution)/shard_map/ppermute | solution.py:21
  97.4 20.5 %gather_fusion.1 = f32[2048,5]{1,0:T(8,128)S(1)} fusion(f32[2,5,8192]{1,2,0:T(8,128)} %copy.30, s32[2048]{0:T(1024)S(1)} %bitcast.48), kind=kCustom, calls=%fused_computation.1 | custom fusion | bytes 98304 | tf_op jit(solution)/shard_map/vmap()/gather | solution.py:59
  119.1 154.2 %while.13 = (s32[]{:T(128)}, f32[3,2,64,128]{3,2,1,0:T(8,128)S(1)}, f32[2]{0:T(128)S(1)}, f32[5,2,64,128]{3,2,1,0:T(8,128)S(1)}, s32[4,2,64]{2,1,0:T(2,128)S(1)}...) while((s32[]{:T(128)}, f32[3,2,64,128]{3,2,1,0:T(8,128)S(1)}, f32[2]{0:T(128)S(1)}, ...), condition=%wide.region_4.0_spmd.clone, body=%wide.region_0.4_spmd.clone.sunk | while | flops 75547648 | bytes 37751944 | solution.py:76
  120.4 11.6 %fusion.37 = f32[2,64,128,128]{3,2,1,0:T(8,128)} fusion(f32[3,2,64,128]{3,2,1,0:T(8,128)S(1)} %copy.38, f32[3,2,64,128]{3,2,1,0:T(8,128)S(1)} %slice.76), kind=kLoop, calls=%fused_computation.5.clone.1 | loop fusion | flops 16777216 | bytes 8781824 | tf_op jit(solution)/shard_map/while/body/eval_jaxpr/reduce_sum | solution.py:29
  132.0 10.0 %fusion.38 = (f32[2]{0:T(128)S(1)}, f32[2,64,128,128]{3,2,1,0:T(8,128)S(1)}) fusion(f32[2,64,128]{2,1,0:T(8,128)S(1)} %bitcast.54, f32[2,64,128]{2,1,0:T(8,128)S(1)} %get-tuple-element.165, f32[2,64,128,128]{3,2,1,0:T(8,128)} %fusion.37, f32[2,64,128]{2,1,0:T(8,128)S(1)} %bitcast.55, f32[2,64,128]{2,1,0:T(8,128)S(1)} %get-tuple-element.167), kind=kLoop, calls=%fused_computation.17.clone.1 | loop fusion | flops 39845888 | bytes 17039368 | tf_op jit(solution)/shard_map/while/body/eval_jaxpr/reduce_sum | solution.py:70
  142.0 15.5 %fusion.39 = f32[3,2,64,128]{3,2,1,0:T(8,128)S(1)} fusion(f32[2,64,128,128]{3,2,1,0:T(8,128)S(1)} %get-tuple-element.168, f32[3,2,64,128]{3,2,1,0:T(8,128)S(1)} %copy.38, f32[3,2,64,128]{3,2,1,0:T(8,128)S(1)} %slice.76), kind=kLoop, calls=%fused_computation.6.clone.1 | loop fusion | flops 18825216 | bytes 8978432 | tf_op jit(solution)/shard_map/while/body/eval_jaxpr/reduce_sum | solution.py:37
  159.0 11.6 %fusion.37 = f32[2,64,128,128]{3,2,1,0:T(8,128)} fusion(f32[3,2,64,128]{3,2,1,0:T(8,128)S(1)} %copy.38, f32[3,2,64,128]{3,2,1,0:T(8,128)S(1)} %slice.76), kind=kLoop, calls=%fused_computation.5.clone.1 | loop fusion | flops 16777216 | bytes 8781824 | tf_op jit(solution)/shard_map/while/body/eval_jaxpr/reduce_sum | solution.py:29
  170.6 10.0 %fusion.38 = (f32[2]{0:T(128)S(1)}, f32[2,64,128,128]{3,2,1,0:T(8,128)S(1)}) fusion(f32[2,64,128]{2,1,0:T(8,128)S(1)} %bitcast.54, f32[2,64,128]{2,1,0:T(8,128)S(1)} %get-tuple-element.165, f32[2,64,128,128]{3,2,1,0:T(8,128)} %fusion.37, f32[2,64,128]{2,1,0:T(8,128)S(1)} %bitcast.55, f32[2,64,128]{2,1,0:T(8,128)S(1)} %get-tuple-element.167), kind=kLoop, calls=%fused_computation.17.clone.1 | loop fusion | flops 39845888 | bytes 17039368 | tf_op jit(solution)/shard_map/while/body/eval_jaxpr/reduce_sum | solution.py:70
  180.6 15.5 %fusion.39 = f32[3,2,64,128]{3,2,1,0:T(8,128)S(1)} fusion(f32[2,64,128,128]{3,2,1,0:T(8,128)S(1)} %get-tuple-element.168, f32[3,2,64,128]{3,2,1,0:T(8,128)S(1)} %copy.38, f32[3,2,64,128]{3,2,1,0:T(8,128)S(1)} %slice.76), kind=kLoop, calls=%fused_computation.6.clone.1 | loop fusion | flops 18825216 | bytes 8978432 | tf_op jit(solution)/shard_map/while/body/eval_jaxpr/reduce_sum | solution.py:37
  197.5 11.6 %fusion.37 = f32[2,64,128,128]{3,2,1,0:T(8,128)} fusion(f32[3,2,64,128]{3,2,1,0:T(8,128)S(1)} %copy.38, f32[3,2,64,128]{3,2,1,0:T(8,128)S(1)} %slice.76), kind=kLoop, calls=%fused_computation.5.clone.1 | loop fusion | flops 16777216 | bytes 8781824 | tf_op jit(solution)/shard_map/while/body/eval_jaxpr/reduce_sum | solution.py:29
  209.1 10.0 %fusion.38 = (f32[2]{0:T(128)S(1)}, f32[2,64,128,128]{3,2,1,0:T(8,128)S(1)}) fusion(f32[2,64,128]{2,1,0:T(8,128)S(1)} %bitcast.54, f32[2,64,128]{2,1,0:T(8,128)S(1)} %get-tuple-element.165, f32[2,64,128,128]{3,2,1,0:T(8,128)} %fusion.37, f32[2,64,128]{2,1,0:T(8,128)S(1)} %bitcast.55, f32[2,64,128]{2,1,0:T(8,128)S(1)} %get-tuple-element.167), kind=kLoop, calls=%fused_computation.17.clone.1 | loop fusion | flops 39845888 | bytes 17039368 | tf_op jit(solution)/shard_map/while/body/eval_jaxpr/reduce_sum | solution.py:70
  219.1 15.5 %fusion.39 = f32[3,2,64,128]{3,2,1,0:T(8,128)S(1)} fusion(f32[2,64,128,128]{3,2,1,0:T(8,128)S(1)} %get-tuple-element.168, f32[3,2,64,128]{3,2,1,0:T(8,128)S(1)} %copy.38, f32[3,2,64,128]{3,2,1,0:T(8,128)S(1)} %slice.76), kind=kLoop, calls=%fused_computation.6.clone.1 | loop fusion | flops 18825216 | bytes 8978432 | tf_op jit(solution)/shard_map/while/body/eval_jaxpr/reduce_sum | solution.py:37
  236.1 11.6 %fusion.37 = f32[2,64,128,128]{3,2,1,0:T(8,128)} fusion(f32[3,2,64,128]{3,2,1,0:T(8,128)S(1)} %copy.38, f32[3,2,64,128]{3,2,1,0:T(8,128)S(1)} %slice.76), kind=kLoop, calls=%fused_computation.5.clone.1 | loop fusion | flops 16777216 | bytes 8781824 | tf_op jit(solution)/shard_map/while/body/eval_jaxpr/reduce_sum | solution.py:29
  247.7 10.0 %fusion.38 = (f32[2]{0:T(128)S(1)}, f32[2,64,128,128]{3,2,1,0:T(8,128)S(1)}) fusion(f32[2,64,128]{2,1,0:T(8,128)S(1)} %bitcast.54, f32[2,64,128]{2,1,0:T(8,128)S(1)} %get-tuple-element.165, f32[2,64,128,128]{3,2,1,0:T(8,128)} %fusion.37, f32[2,64,128]{2,1,0:T(8,128)S(1)} %bitcast.55, f32[2,64,128]{2,1,0:T(8,128)S(1)} %get-tuple-element.167), kind=kLoop, calls=%fused_computation.17.clone.1 | loop fusion | flops 39845888 | bytes 17039368 | tf_op jit(solution)/shard_map/while/body/eval_jaxpr/reduce_sum | solution.py:70
  257.6 15.5 %fusion.39 = f32[3,2,64,128]{3,2,1,0:T(8,128)S(1)} fusion(f32[2,64,128,128]{3,2,1,0:T(8,128)S(1)} %get-tuple-element.168, f32[3,2,64,128]{3,2,1,0:T(8,128)S(1)} %copy.38, f32[3,2,64,128]{3,2,1,0:T(8,128)S(1)} %slice.76), kind=kLoop, calls=%fused_computation.6.clone.1 | loop fusion | flops 18825216 | bytes 8978432 | tf_op jit(solution)/shard_map/while/body/eval_jaxpr/reduce_sum | solution.py:37
  274.3 36.6 %all-reduce = (f32[2]{0:T(128)S(1)}, f32[2]{0:T(128)S(1)}, f32[2]{0:T(128)S(1)}) all-reduce(f32[2]{0:T(128)S(1)} %get-tuple-element.84, f32[2]{0:T(128)S(1)} %get-tuple-element.83, f32[2]{0:T(128)S(1)} %add_multiply_fusion.1), channel_id=1, replica_groups=mesh['image'=16,'space'=16] {'space'}, use_global_device_ids=true, to_apply=%region_12.13 | all-reduce | flops 6 | bytes 48 | tf_op jit(solution)/shard_map/psum | solution.py:92
  (71 shorter events, 16.6 us)
Async XLA Ops:
  3.3 63.9 %collective-permute-start.1 = (f32[2,5,8192]{2,0,1:T(2,128)S(1)}, f32[2,5,8192]{2,0,1:T(2,128)S(1)}, u32[]{:S(2)}, u32[]{:S(2)}) collective-permute-start(f32[2,5,8192]{2,0,1:T(2,128)S(1)} %pad_maximum_fusion.1), channel_id=1, source_target_pairs={{1,0},{2,1},{3,2},{4,3},{5,4},{6,5},{7,6},{8,7},{9,8},{10,9},{11,1... | collective-permute-start | bytes 983048 | tf_op jit(solution)/shard_map/ppermute | solution.py:22
  4.6 88.1 %collective-permute-start = (f32[2,5,8192]{2,0,1:T(2,128)S(1)}, f32[2,5,8192]{2,0,1:T(2,128)S(1)}, u32[]{:S(2)}, u32[]{:S(2)}) collective-permute-start(f32[2,5,8192]{2,0,1:T(2,128)S(1)} %pad_maximum_fusion.1), channel_id=1, source_target_pairs={{0,1},{1,2},{2,3},{3,4},{4,5},{5,6},{6,7},{7,8},{8,9},{9,10},{10,1... | collective-permute-start | bytes 983048 | tf_op jit(solution)/shard_map/ppermute | solution.py:21
  11.9 6.4 %collective-permute-start.2 = (f32[1,3,8192]{2,0,1:T(1,128)S(1)}, f32[1,3,8192]{2,0,1:T(1,128)S(1)}, u32[]{:S(2)}, u32[]{:S(2)}) collective-permute-start(f32[1,3,8192]{2,0,1:T(1,128)S(1)} %get-tuple-element.112), channel_id=1, source_target_pairs={{16,0},{32,16},{48,32},{64,48},{80,64},{96,80},{112,96},{128,112},... | collective-permute-start | bytes 294920 | tf_op jit(solution)/shard_map/ppermute | solution.py:22
  14.5 6.9 %collective-permute-start.3 = (f32[1,3,8192]{2,0,1:T(1,128)S(1)}, f32[1,3,8192]{2,0,1:T(1,128)S(1)}, u32[]{:S(2)}, u32[]{:S(2)}) collective-permute-start(f32[1,3,8192]{2,0,1:T(1,128)S(1)} %get-tuple-element.111), channel_id=1, source_target_pairs={{0,16},{16,32},{32,48},{48,64},{64,80},{80,96},{96,112},{112,128},... | collective-permute-start | bytes 294920 | tf_op jit(solution)/shard_map/ppermute | solution.py:21
  71.8 46.4 %copy-start = (f32[2,3,8192]{2,0,1:T(2,128)S(1)}, f32[2,3,8192]{2,0,1:T(2,128)}, u32[]{:S(2)}) copy-start(f32[2,3,8192]{2,0,1:T(2,128)} %param.10) | copy-start | bytes 589828
  119.0 154.3 %copy-start.1 = (f32[3,8192]{1,0:T(4,128)S(1)}, f32[3,8192]{1,0:T(4,128)}, u32[]{:S(2)}) copy-start(f32[3,8192]{1,0:T(4,128)} %param.11) | copy-start | bytes 294916
  119.1 154.3 %copy-start.2 = (f32[8192]{0:T(1024)S(1)}, f32[8192]{0:T(1024)}, u32[]{:S(2)}) copy-start(f32[8192]{0:T(1024)} %param.12) | copy-start | bytes 98308
where the time goes:
time: 316 us; the launch traced here: 312 us
  other arithmetic  155 us (49%)
  blocking collectives  80.6 us (26%)
  local copies, waits for them, and re-layouts  59.2 us (19%)
  starting transfers between devices  11.9 us (4%)
    reduce_sum x4, other arithmetic, pair_terms(): force = jnp.sum(coeff[None] * delta, axis=-1)  62 us
    reduce_sum x4, other arithmetic, pair_terms(): dist_sq = jnp.sum(delta * delta, axis=0)  46.4 us
    psum x1, blocking collectives, body(): lax.psum((image_total(ahead * ahead), image_total(behind * behind)), 'spa...  43.9 us
    gather x4, local copies, waits for them, and re-layouts, body(): pick_atoms = jax.vmap(lambda source, index: source[:, index])  41.7 us
    reduce_sum x4, other arithmetic, add_partner(): return ((carry[0] + force, carry[1] + jnp.sum(energy, axis=1)), None)  39.8 us
    psum x1, blocking collectives, body(): lax.psum((image_total(tangent * tangent), image_total(forces * tangent),...  36.6 us
    ppermute x2, starting transfers between devices, extended_2(): before = lax.ppermute(last, axis, up)  7.99 us
  transfers between devices with their start and end apart: 4, of which 1 were waited for; matrix products, arithmetic and copies ran while one was open for 10% of the time, Pallas kernels for 0%

commit v1 on v0

v1 whole, which is shorter than its diff:
```python
import jax
import jax.numpy as jnp
from jax import lax
from jax.experimental import pallas as pl
from jax.experimental.pallas import tpu as pltpu
from jax.sharding import PartitionSpec as P

TILE = 128
PARTNERS = 4
UNROLL = 8
spring_k = 2.0
small_eps = 1e-06
f32, bf16 = jnp.float32, jnp.bfloat16
GROUPS = ((0, 0), (0, 1), (1, 0), (0, 2), (2, 0), (1, 1))
VMEM = pl.BlockSpec(memory_space=pltpu.VMEM)
SMEM = pl.BlockSpec(memory_space=pltpu.SMEM)


def lanes(tile):
    return pl.ds(pl.multiple_of(tile * TILE, TILE), TILE)


def pieces(v):
    first = v.astype(bf16).astype(f32)
    rest = v - first
    second = rest.astype(bf16).astype(f32)
    return first, second, (rest - second).astype(bf16).astype(f32)


def rows_of(shape):
    return lax.broadcasted_iota(jnp.int32, shape, 0)


def streamed_features(x3, depth, radius):
    row = rows_of((8, TILE))
    squares = x3 * x3
    rr = radius * radius
    norm = squares[0:1] + squares[1:2] + squares[2:3] + rr
    cut = pieces(jnp.concatenate([x3, radius, norm, norm, rr, rr], axis=0))
    ones = [jnp.where((row == 5) | (row == 7), 1.0, c) for c in cut]
    streamed = jnp.concatenate([ones[a] for a, _ in GROUPS], axis=0).astype(bf16)
    streamed = jnp.concatenate([streamed, jnp.zeros((80, TILE), bf16)], axis=0)
    moved = jnp.concatenate([depth, depth * x3], axis=0)
    p1, p2, p3 = pieces(jnp.concatenate([moved, moved], axis=0))
    weights = jnp.concatenate(
        [jnp.where(row < 4, p1, p2), jnp.where(row < 4, p3, 0.0)], axis=0
    ).astype(bf16)
    return cut, streamed, weights


def held_features(cut):
    row = rows_of((8, TILE))
    blocks = []
    for a, b in GROUPS:
        own = 1.0 if (a, b) in ((0, 0), (0, 1), (0, 2)) else 0.0
        other = 1.0 if (a, b) in ((0, 0), (1, 0), (2, 0)) else 0.0
        scale_d = jnp.where(row < 3, -2.0, jnp.where(row == 3, 2.0, jnp.where(row == 5, own, 0.0)))
        scale_r = jnp.where(row == 3, 2.0, jnp.where(row == 7, own, 0.0))
        dist = cut[b] * scale_d + jnp.where(row == 4, other, 0.0)
        reach = cut[b] * scale_r + jnp.where(row == 6, other, 0.0)
        blocks.append(jnp.concatenate([dist, reach], axis=1))
    held = jnp.concatenate(blocks, axis=0).astype(bf16)
    return jnp.concatenate([held, jnp.zeros((80, 2 * TILE), bf16)], axis=0)


def pair_kernel(
    lists, sides, coords, below, above, types, tables, hidx, ref, restr, prev, nxt,
    force, sums,
    halo_x, depth_s, radius_s, a_s, b_s, p_s, acc_s,
):
    images = coords.shape[0]
    own_tiles = types.shape[0]
    halo_tiles = halo_x.shape[2]
    side_tiles = halo_tiles // 2
    take = lambda src, idx: jnp.take_along_axis(src, idx, axis=1, mode="promise_in_bounds")
    wells = jnp.broadcast_to(tables[0:1], (8, TILE))
    radii = jnp.broadcast_to(tables[1:2], (8, TILE))
    for b in range(own_tiles // 8):
        kind = types[8 * b : 8 * b + 8]
        for m in range(images):
            depth_s[m, 8 * b : 8 * b + 8] = take(wells, kind)
            radius_s[m, 8 * b : 8 * b + 8] = take(radii, kind)

    for side, source in enumerate((below, above)):
        low, high = [], []
        for m in range(images):
            idx = jnp.concatenate(
                [hidx[m, side : side + 1, q * TILE : (q + 1) * TILE] for q in range(side_tiles)],
                axis=0,
            )
            low.append(idx & (TILE - 1))
            high.append(idx >> 7)

        def gather_row(r, carry):
            chunk = source[:, lanes(r)]
            out = []
            for m in range(images):
                hit = high[m] == r
                for c, row in enumerate((3 * m, 3 * m + 1, 3 * m + 2, 3 * images)):
                    wide = jnp.broadcast_to(chunk[row : row + 1], (8, TILE))
                    out.append(jnp.where(hit, take(wide, low[m]), carry[4 * m + c]))
            return tuple(out)

        zero = jnp.zeros((8, TILE), f32)
        found = lax.fori_loop(0, own_tiles, gather_row, (zero,) * (4 * images), unroll=4)
        inside = sides[side].astype(f32)
        for m in range(images):
            for c in range(3):
                halo_x[m, c, side * side_tiles : (side + 1) * side_tiles] = found[4 * m + c]
            kind = found[4 * m + 3].astype(jnp.int32)
            spot = slice(own_tiles + side * side_tiles, own_tiles + (side + 1) * side_tiles)
            depth_s[m, spot] = take(wells, kind) * inside
            radius_s[m, spot] = take(radii, kind)

    eye = (rows_of((TILE, TILE)) == lax.broadcasted_iota(jnp.int32, (TILE, TILE), 1)).astype(bf16)

    def store_tiles(m, first, made):
        for n in range(0, len(made), 2):
            pair = jnp.concatenate([made[n][1], made[n + 1][1]], axis=0)
            turned = lax.dot_general(
                eye, pair, (((1,), (1,)), ((), ())), preferred_element_type=f32
            ).astype(bf16)
            for h in range(2):
                a_s[m, first + n + h] = turned[:, h * TILE : (h + 1) * TILE]
                p_s[m, first + n + h] = made[n + h][2]

    centers = []
    for m in range(images):
        total = coords[m, :, 0:TILE]
        for t in range(1, own_tiles):
            total = total + coords[m, :, t * TILE : (t + 1) * TILE]
        center = jnp.sum(total, axis=1, keepdims=True) * (1.0 / (own_tiles * TILE))
        center = jnp.broadcast_to(center, (3, TILE))
        centers.append(center)

        def build_own(n, carry):
            made = []
            for h in range(4):
                t = 4 * n + h
                x3 = coords[m, :, lanes(t)] - center
                made.append(streamed_features(x3, depth_s[m, pl.ds(t, 1)], radius_s[m, pl.ds(t, 1)]))
                b_s[m, t] = held_features(made[-1][0])
            store_tiles(m, 4 * n, made)
            return carry

        lax.fori_loop(0, own_tiles // 4, build_own, 0)

        def build_halo(n, carry):
            made = []
            for h in range(4):
                t = 4 * n + h
                x3 = jnp.concatenate([halo_x[m, c, pl.ds(t, 1)] for c in range(3)], axis=0) - center
                q = own_tiles + t
                made.append(streamed_features(x3, depth_s[m, pl.ds(q, 1)], radius_s[m, pl.ds(q, 1)]))
            store_tiles(m, own_tiles + 4 * n, made)
            return carry

        lax.fori_loop(0, halo_tiles // 4, build_halo, 0)

    acc_s[...] = jnp.zeros_like(acc_s)
    for m in range(images):
        center = centers[m]

        def one_tile(t, carry):
            held = b_s[m, t]
            acc = jnp.zeros((16, 2 * TILE), f32)
            for k in range(PARTNERS):
                p = lists[m, k, t]
                both = jnp.dot(a_s[m, p], held, preferred_element_type=f32)
                reach = both[:, TILE:]
                inv = pltpu.reciprocal(both[:, :TILE], approx=True)
                ratio = reach * inv
                cubed = ratio * ratio * ratio
                sixth = cubed * cubed
                energy = sixth - cubed
                coeff = (energy + sixth) * inv
                high = coeff.astype(bf16)
                low = (coeff - high.astype(f32)).astype(bf16)
                left = jnp.concatenate([high, low], axis=0)
                right = jnp.concatenate([energy.astype(bf16), jnp.zeros((TILE, TILE), bf16)], axis=0)
                weights = p_s[m, p]
                acc += jnp.dot(
                    jnp.concatenate([weights, weights], axis=1),
                    jnp.concatenate([left, right], axis=1),
                    preferred_element_type=f32,
                )
            depth = depth_s[m, pl.ds(t, 1)]
            at = lanes(t)
            x = coords[m, :, at]
            joined = acc[0:4] + acc[4:8] + acc[8:12]
            moved = (x - center) * joined[0:1, :TILE] - joined[1:4, :TILE]
            offset = x - ref[:, at]
            pull = restr[:, at] * offset
            total = 24.0 * depth * moved - pull
            force[m, :, at] = total
            if m == 0:
                before, after = prev[:, at], coords[1, :, at]
            else:
                before, after = coords[0, :, at], nxt[:, at]
            ahead, behind = after - x, x - before
            both_ways, bend = ahead + behind, ahead - behind
            acc_s[m, 0] += both_ways * both_ways
            acc_s[m, 1] += both_ways * bend
            acc_s[m, 2] += bend * bend
            acc_s[m, 3] += total * both_ways
            acc_s[m, 4] += total * bend
            acc_s[m, 5] += 0.5 * pull * offset
            acc_s[m, 5, 0:1] += 2.0 * depth * joined[0:1, TILE:]
            return carry

        lax.fori_loop(0, own_tiles, one_tile, 0, unroll=UNROLL)

    line = [jnp.sum(acc_s[m, n], axis=0, keepdims=True) for m in range(images) for n in range(6)]
    line = line + [jnp.zeros_like(line[0])] * (16 - len(line))
    row, lane = rows_of((16, 16)), lax.broadcasted_iota(jnp.int32, (16, 16), 1)
    totals = jnp.sum(jnp.concatenate(line, axis=0), axis=1, keepdims=True)
    totals = jnp.sum(jnp.where(row == lane, totals, 0.0), axis=0, keepdims=True)
    sums[...] = jnp.broadcast_to(totals, (16, 16))


def band_kernel(ends, shares, force, coords, prev, nxt, out, energies):
    total = jnp.sum(shares[...], axis=0, keepdims=True)
    atoms = 16 * coords.shape[2]
    for m in range(coords.shape[0]):
        s_sq, cross, b_sq, f_s, f_b, energy = [
            total[:, 6 * m + n : 6 * m + n + 1] for n in range(6)
        ]
        energies[m] = (energy / atoms)[0, 0]
        base = 0.25 * (s_sq + b_sq) + small_eps
        ahead_sq, behind_sq = base + 0.5 * cross, base - 0.5 * cross
        ahead_len, behind_len = jnp.sqrt(ahead_sq), jnp.sqrt(behind_sq)
        inverse_sum = 1.0 / ahead_len + 1.0 / behind_len
        alpha = 0.5 * inverse_sum
        beta = -0.5 * cross / (ahead_sq * behind_sq * inverse_sum)
        tan_sq = alpha * alpha * s_sq + 2.0 * alpha * beta * cross + beta * beta * b_sq
        tan_len = jnp.sqrt(jnp.maximum(tan_sq, 0.0) + small_eps)
        along = (alpha * f_s + beta * f_b) / tan_len
        stretch = cross / (ahead_len + behind_len)
        gain = (spring_k * stretch - along) / tan_len
        gain = jnp.where(ends[m] == 1, 0.0, gain)
        for_s, for_b = gain * alpha, gain * beta
        for_s = jnp.broadcast_to(for_s, (3, TILE))
        for_b = jnp.broadcast_to(for_b, (3, TILE))
        for t in range(coords.shape[2] // TILE):
            at = slice(t * TILE, (t + 1) * TILE)
            x = coords[m, :, at]
            before = prev[:, at] if m == 0 else coords[0, :, at]
            after = nxt[:, at] if m == 1 else coords[1, :, at]
            ahead, behind = after - x, x - before
            out[m, :, at] = force[m, :, at] + for_s * (ahead + behind) + for_b * (ahead - behind)


def ring(axis, step):
    n = lax.axis_size(axis)
    return [(i, (i + step) % n) for i in range(n)]


def body(
    coords, ref_coords, restraint, atom_types, well_table, radius_table, tile_lists, halo_index
):
    images, _, atoms = coords.shape
    tiles = atoms // TILE
    halo_tiles = 2 * halo_index.shape[2] // TILE
    slab, slabs = lax.axis_index("space"), lax.axis_size("space")
    feats = jnp.concatenate(
        [coords.reshape(3 * images, atoms), atom_types.astype(f32)[None]], axis=0
    )
    below = lax.ppermute(feats, "space", ring("space", 1))
    above = lax.ppermute(feats, "space", ring("space", -1))
    prev = lax.ppermute(coords[images - 1], "image", ring("image", 1))
    nxt = lax.ppermute(coords[0], "image", ring("image", -1))
    sides = jnp.stack([slab > 0, slab < slabs - 1]).astype(jnp.int32)
    tables = jnp.pad(
        jnp.stack([well_table, radius_table]), ((0, 0), (0, TILE - well_table.shape[0]))
    )
    tiles_ext = tiles + halo_tiles
    force, sums = pl.pallas_call(
        pair_kernel,
        out_shape=(
            jax.ShapeDtypeStruct((images, 3, atoms), f32),
            jax.ShapeDtypeStruct((16, 16), f32),
        ),
        in_specs=[SMEM, SMEM] + [VMEM] * 10,
        out_specs=(VMEM, VMEM),
        scratch_shapes=[
            pltpu.VMEM((images, 3, halo_tiles, TILE), f32),
            pltpu.VMEM((images, tiles_ext, TILE), f32),
            pltpu.VMEM((images, tiles_ext, TILE), f32),
            pltpu.VMEM((images, tiles_ext, TILE, TILE), bf16),
            pltpu.VMEM((images, tiles, TILE, 2 * TILE), bf16),
            pltpu.VMEM((images, tiles_ext, 16, TILE), bf16),
            pltpu.VMEM((images, 6, 3, TILE), f32),
        ],
        compiler_params=pltpu.CompilerParams(vmem_limit_bytes=40 << 20),
        name="pair",
    )(
        tile_lists, sides, coords, below, above, atom_types.reshape(tiles, TILE), tables,
        halo_index, ref_coords, restraint[None], prev, nxt,
    )
    shares = lax.all_to_all(sums, "space", 0, 0, tiled=True)
    image = lax.axis_index("image") * images + jnp.arange(images, dtype=jnp.int32)
    ends = ((image == 0) | (image == images * lax.axis_size("image") - 1)).astype(jnp.int32)
    return pl.pallas_call(
        band_kernel,
        out_shape=(
            jax.ShapeDtypeStruct((images, 3, atoms), f32),
            jax.ShapeDtypeStruct((images,), f32),
        ),
        in_specs=[SMEM] + [VMEM] * 5,
        out_specs=(VMEM, SMEM),
        name="band",
    )(ends, shares, force, coords, prev, nxt)


def solution(mesh):
    in_specs = (
        P("image", None, "space"),
        P(None, "space"),
        P("space"),
        P("space"),
        P(),
        P(),
        P("image", None, "space"),
        P("image", None, "space"),
    )
    out_specs = (P("image", None, "space"), P("image"))
    return jax.shard_map(body, mesh=mesh, in_specs=in_specs, out_specs=out_specs, check_vma=False)
```

time: 316 us -> 84.3 us (0.27); the launches traced: 312 us -> 83.9 us
  other arithmetic: 155 us -> 1.41 us
  blocking collectives: 80.6 us -> 0 us
  local copies, waits for them, and re-layouts: 59.2 us -> 4.31 us
  Pallas kernels: 0 us -> 39.3 us
  waiting for transfers between devices: 3.14 us -> 20.1 us
  starting transfers between devices: 11.9 us -> 18.1 us
    reduce_sum x14 -> x0, other arithmetic: 151 us -> none  [the longest x4 62 us: pair_terms(): force = jnp.sum(coeff[None] * delta, axis=-1)]
    psum x2 -> x0, blocking collectives: 80.6 us -> none  [the longest x1 43.9 us: body(): lax.psum((image_total(ahead * ahead), image_total(behind * behind)), 'spa...]
    gather x12 -> x0, local copies, waits for them, and re-layouts: 46.1 us -> none  [the longest x4 41.7 us: body(): pick_atoms = jax.vmap(lambda source, index: source[:, index])]
    pallas_call x0 -> x2, Pallas kernels: none -> 39.3 us  [the longest x1 36.9 us: body(): pl.pallas_call(pair_kernel, out_shape=(jax.ShapeDtypeStruct((images, 3, a...]
    all_to_all x0 -> x1, waiting for transfers between devices: none -> 9.5 us  [body(): shares = lax.all_to_all(sums, 'space', 0, 0, tiled=True)]
    ppermute x2 -> x0, local copies, waits for them, and re-layouts: 9.3 us -> none  [the longest x1 4.65 us: extended_2(): before = lax.ppermute(last, axis, up)]
    all_to_all x0 -> x1, starting transfers between devices: none -> 8.95 us  [body(): shares = lax.all_to_all(sums, 'space', 0, 0, tiled=True)]
    ppermute x4, waiting for transfers between devices: 3.14 us -> 10.6 us  [the longest x1 4.37 us: body(): below = lax.ppermute(feats, 'space', ring('space', 1))]
  transfers between devices with their start and end apart: 4 -> 5, of which waited for: 1 -> 5; matrix products, arithmetic and copies ran while one was open for 10% -> 1% of each run, Pallas kernels for 0% -> 0%
where the time goes in v1:
time: 84.3 us; the launch traced here: 83.9 us
  Pallas kernels  39.3 us (47%)
  waiting for transfers between devices  20.1 us (24%)
  starting transfers between devices  18.1 us (21%)
  local copies, waits for them, and re-layouts  4.31 us (5%)
  other arithmetic  1.41 us (2%)
    pallas_call x1, Pallas kernels, body(): pl.pallas_call(pair_kernel, out_shape=(jax.ShapeDtypeStruct((images, 3, a...  36.9 us
    all_to_all x1, waiting for transfers between devices, body(): shares = lax.all_to_all(sums, 'space', 0, 0, tiled=True)  9.5 us
    all_to_all x1, starting transfers between devices, body(): shares = lax.all_to_all(sums, 'space', 0, 0, tiled=True)  8.95 us
    ppermute x1, starting transfers between devices, body(): above = lax.ppermute(feats, 'space', ring('space', -1))  8.56 us
    ppermute x1, waiting for transfers between devices, body(): below = lax.ppermute(feats, 'space', ring('space', 1))  4.37 us
    ppermute x1, waiting for transfers between devices, body(): prev = lax.ppermute(coords[images - 1], 'image', ring('image', 1))  2.86 us
    pallas_call x1, Pallas kernels, body(): pl.pallas_call(band_kernel, out_shape=(jax.ShapeDtypeStruct((images, 3, a...  2.4 us
    unnamed x25, local copies, waits for them, and re-layouts  2.39 us
  transfers between devices with their start and end apart: 5, of which 5 were waited for; matrix products, arithmetic and copies ran while one was open for 1% of the time, Pallas kernels for 0%

profile of v1, /device:TPU:6, one launch (start us, length us, event | category | flops | bytes accessed | tf_op | source)
XLA Modules:
  0.0 83.9 jit_solution(8640662373775702477)
XLA Ops:
  0.6 0.8 convert_element_type.13
  1.4 1.1 %copy.25.coords = f32[2,3,8192]{2,1,0:T(4,128)S(1)} copy(f32[2,3,8192]{2,0,1:T(2,128)} %param.8) | data formatting | bytes 393216 | tf_op args[0]
  2.5 0.1 reshape.12
  2.6 0.1 pad_maximum_fusion
  2.6 0.0 copy-start.5
  2.6 8.6 %collective-permute-start.1 = (f32[7,8192]{1,0:T(8,128)S(1)}, f32[7,8192]{1,0:T(8,128)S(1)}, u32[]{:S(2)}, u32[]{:S(2)}) collective-permute-start(f32[7,8192]{1,0:T(8,128)S(1)} %pad_maximum_fusion), channel_id=1, source_target_pairs={{0,15},{1,0},{2,1},{3,2},{4,3},{5,4},{6,5},{7,6},{8,7},{9,8},{10,9... | collective-permute-start | bytes 688136 | tf_op jit(solution)/shard_map/ppermute | solution.py:269
  11.2 0.0 copy-start.7
  11.3 0.0 copy-start.4
  11.3 0.2 collective-permute-start.3
  11.5 0.4 collective-permute-start.2
  11.9 0.0 copy-start.8
  11.9 0.1 add_convert_fusion.sides
  12.0 2.0 %collective-permute-done.3.nxt = f32[3,8192]{1,0:T(4,128)S(1)} collective-permute-done((f32[3,8192]{1,0:T(4,128)S(1)}, f32[3,8192]{1,0:T(4,128)S(1)}, u32[]{:S(2)}, u32[]{:S(2)}) %collective-permute-start.3) | collective-permute-done | bytes 98336 | tf_op jit(solution)/shard_map/ppermute | solution.py:271
  14.0 2.9 %collective-permute-done.2.prev = f32[3,8192]{1,0:T(4,128)S(1)} collective-permute-done((f32[3,8192]{1,0:T(4,128)S(1)}, f32[3,8192]{1,0:T(4,128)S(1)}, u32[]{:S(2)}, u32[]{:S(2)}) %collective-permute-start.2) | collective-permute-done | bytes 98336 | tf_op jit(solution)/shard_map/ppermute | solution.py:270
  16.9 1.3 %collective-permute-done.1.above = f32[7,8192]{1,0:T(8,128)S(1)} collective-permute-done((f32[7,8192]{1,0:T(8,128)S(1)}, f32[7,8192]{1,0:T(8,128)S(1)}, u32[]{:S(2)}, u32[]{:S(2)}) %collective-permute-start.1) | collective-permute-done | bytes 229408 | tf_op jit(solution)/shard_map/ppermute | solution.py:269
  18.2 4.4 %collective-permute-done.below = f32[7,8192]{1,0:T(8,128)S(1)} collective-permute-done((f32[7,8192]{1,0:T(8,128)S(1)}, f32[7,8192]{1,0:T(8,128)S(1)}, u32[]{:S(2)}, u32[]{:S(2)}) %collective-permute-start) | collective-permute-done | bytes 229408 | tf_op jit(solution)/shard_map/ppermute | solution.py:268
  22.6 36.9 %pair.1 = (f32[2,3,8192]{2,1,0:T(4,128)S(1)}, f32[16,16]{1,0:T(8,128)}) custom-call(s32[2,4,64]{2,1,0:T(4,128)S(1)} %copy-done.8, s32[2]{0:T(128)S(1)} %add_convert_fusion.sides, f32[2,3,8192]{2,1,0:T(4,128)S(1)} %copy.25.coords, f32[7,8192]{1,0:T(8,128)S(1)} %collective-permute-done.below, f32[7,8192]{1,0:T(8,128)S(1)} %collective-permute-done.1.above, ...), custom_call_target="tpu_custom_call" | custom-call | tf_op jit(solution)/shard_map/pair/pallas_call | solution.py:277
  59.5 0.7 copy-done.3
  60.2 8.9 %all-to-all-start = ((f32[16,1,16]{2,1,0:T(1,128)}), f32[16,1,16]{2,1,0:T(1,128)S(1)}, u32[]{:S(2)}, u32[]{:S(2)}) async-start(f32[16,1,16]{2,1,0:T(1,128)} %bitcast.10), calls=%async_computation | async-start | bytes 16384 | tf_op jit(solution)/shard_map/all_to_all | solution.py:300
  69.1 0.5 or_convert_fusion.ends
  69.7 9.5 %all-to-all-done = f32[16,1,16]{2,1,0:T(1,128)S(1)} async-done(((f32[16,1,16]{2,1,0:T(1,128)}), f32[16,1,16]{2,1,0:T(1,128)S(1)}, u32[]{:S(2)}, u32[]{:S(2)}) %all-to-all-start) | async-done | bytes 1056 | tf_op jit(solution)/shard_map/all_to_all | solution.py:300
  79.2 0.6 copy-done.9
  79.7 2.4 %band.1 = (f32[2,3,8192]{2,1,0:T(4,128)}, f32[2]{0:T(128)}) custom-call(s32[2]{0:T(128)} %or_convert_fusion.ends, f32[16,16]{1,0:T(8,128)} %bitcast.18, f32[2,3,8192]{2,1,0:T(4,128)} %copy-done.3, f32[2,3,8192]{2,1,0:T(4,128)} %copy-done, f32[3,8192]{1,0:T(4,128)} %copy-done.2, f32[3,8192]{1,0:T(4,128)} %copy-done.1), custom_call_target="tpu_custom_call" | custom-call | tf_op jit(solution)/shard_map/band/pallas_call | solution.py:303
  82.2 1.8 %copy.28 = f32[2,3,8192]{2,0,1:T(2,128)} copy(f32[2,3,8192]{2,1,0:T(4,128)} %get-tuple-element.10) | data formatting | bytes 393216 | tf_op jit(solution)/shard_map/band/pallas_call | solution.py:303
  (21 shorter events, 0.1 us)
Async XLA Ops:
  2.5 20.1 %copy-start = (f32[2,3,8192]{2,1,0:T(4,128)}, f32[2,3,8192]{2,1,0:T(4,128)S(1)}, u32[]{:S(2)}) copy-start(f32[2,3,8192]{2,1,0:T(4,128)S(1)} %copy.25.coords) | copy-start | bytes 589828
  2.6 20.0 %copy-start.5 = (f32[3,8192]{1,0:T(4,128)S(1)}, f32[3,8192]{1,0:T(4,128)}, u32[]{:S(2)}) copy-start(f32[3,8192]{1,0:T(4,128)} %ref.1) | copy-start | bytes 294916
  2.6 15.6 %collective-permute-start.1 = (f32[7,8192]{1,0:T(8,128)S(1)}, f32[7,8192]{1,0:T(8,128)S(1)}, u32[]{:S(2)}, u32[]{:S(2)}) collective-permute-start(f32[7,8192]{1,0:T(8,128)S(1)} %pad_maximum_fusion), channel_id=1, source_target_pairs={{0,15},{1,0},{2,1},{3,2},{4,3},{5,4},{6,5},{7,6},{8,7},{9,8},{10,9... | collective-permute-start | bytes 688136 | tf_op jit(solution)/shard_map/ppermute | solution.py:269
  11.2 11.4 %collective-permute-start = (f32[7,8192]{1,0:T(8,128)S(1)}, f32[7,8192]{1,0:T(8,128)S(1)}, u32[]{:S(2)}, u32[]{:S(2)}) collective-permute-start(f32[7,8192]{1,0:T(8,128)S(1)} %pad_maximum_fusion), channel_id=1, source_target_pairs={{0,1},{1,2},{2,3},{3,4},{4,5},{5,6},{6,7},{7,8},{8,9},{9,10},{10,1... | collective-permute-start | bytes 688136 | tf_op jit(solution)/shard_map/ppermute | solution.py:268
  11.2 0.7 copy-start.10
  11.2 0.7 copy-start.11
  11.2 11.4 %copy-start.6 = (f32[8192]{0:T(1024)S(1)}, f32[8192]{0:T(1024)}, u32[]{:S(2)}) copy-start(f32[8192]{0:T(1024)} %param.10) | copy-start | bytes 98308
  11.2 11.4 %copy-start.7 = (s32[2,2,1024]{2,1,0:T(2,128)S(1)}, s32[2,2,1024]{2,1,0:T(2,128)}, u32[]{:S(2)}) copy-start(s32[2,2,1024]{2,1,0:T(2,128)} %hidx.1) | copy-start | bytes 49156
  11.3 11.3 %copy-start.4 = (s32[8192]{0:T(1024)S(1)}, s32[8192]{0:T(1024)}, u32[]{:S(2)}) copy-start(s32[8192]{0:T(1024)} %param.11) | copy-start | bytes 98308
  11.3 2.7 %collective-permute-start.3 = (f32[3,8192]{1,0:T(4,128)S(1)}, f32[3,8192]{1,0:T(4,128)S(1)}, u32[]{:S(2)}, u32[]{:S(2)}) collective-permute-start(f32[3,8192]{1,0:T(4,128)S(1)} %get-tuple-element.12), channel_id=1, source_target_pairs={{0,240},{16,0},{32,16},{48,32},{64,48},{80,64},{96,80},{112,96},{1... | collective-permute-start | bytes 294920 | tf_op jit(solution)/shard_map/ppermute | solution.py:271
  11.5 5.4 %collective-permute-start.2 = (f32[3,8192]{1,0:T(4,128)S(1)}, f32[3,8192]{1,0:T(4,128)S(1)}, u32[]{:S(2)}, u32[]{:S(2)}) collective-permute-start(f32[3,8192]{1,0:T(4,128)S(1)} %get-tuple-element.13), channel_id=1, source_target_pairs={{0,16},{16,32},{32,48},{48,64},{64,80},{80,96},{96,112},{112,128},... | collective-permute-start | bytes 294920 | tf_op jit(solution)/shard_map/ppermute | solution.py:270
  11.9 10.7 %copy-start.8 = (s32[2,4,64]{2,1,0:T(4,128)S(1)}, s32[2,4,64]{2,1,0:T(4,128)}, u32[]{:S(2)}) copy-start(s32[2,4,64]{2,1,0:T(4,128)} %lists.1) | copy-start | bytes 6148
  14.0 45.5 %copy-start.1 = (f32[3,8192]{1,0:T(4,128)}, f32[3,8192]{1,0:T(4,128)S(1)}, u32[]{:S(2)}) copy-start(f32[3,8192]{1,0:T(4,128)S(1)} %collective-permute-done.3.nxt) | copy-start | bytes 294916
  16.9 42.6 %copy-start.2 = (f32[3,8192]{1,0:T(4,128)}, f32[3,8192]{1,0:T(4,128)S(1)}, u32[]{:S(2)}) copy-start(f32[3,8192]{1,0:T(4,128)S(1)} %collective-permute-done.2.prev) | copy-start | bytes 294916
  59.5 0.7 copy-start.3
  60.2 19.0 %all-to-all-start = ((f32[16,1,16]{2,1,0:T(1,128)}), f32[16,1,16]{2,1,0:T(1,128)S(1)}, u32[]{:S(2)}, u32[]{:S(2)}) async-start(f32[16,1,16]{2,1,0:T(1,128)} %bitcast.10), calls=%async_computation | async-start | bytes 16384 | tf_op jit(solution)/shard_map/all_to_all | solution.py:300
  79.2 0.6 copy-start.9

commit v2 on v1

v2 whole, which is shorter than its diff:
```python
import jax
import jax.numpy as jnp
from jax import lax
from jax.experimental import pallas as pl
from jax.experimental.pallas import tpu as pltpu
from jax.sharding import PartitionSpec as P

TILE = 128
PARTNERS = 4
UNROLL = 8
spring_k = 2.0
small_eps = 1e-06
f32, bf16 = jnp.float32, jnp.bfloat16
GROUPS = ((0, 0), (0, 1), (1, 0), (0, 2), (2, 0), (1, 1))
VMEM = pl.BlockSpec(memory_space=pltpu.VMEM)
SMEM = pl.BlockSpec(memory_space=pltpu.SMEM)


def lanes(tile):
    return pl.ds(pl.multiple_of(tile * TILE, TILE), TILE)


def pieces(v):
    first = v.astype(bf16).astype(f32)
    rest = v - first
    second = rest.astype(bf16).astype(f32)
    return first, second, (rest - second).astype(bf16).astype(f32)


def rows_of(shape):
    return lax.broadcasted_iota(jnp.int32, shape, 0)


def streamed_features(x3, depth, radius):
    row = rows_of((8, TILE))
    squares = x3 * x3
    rr = radius * radius
    norm = squares[0:1] + squares[1:2] + squares[2:3] + rr
    cut = pieces(jnp.concatenate([x3, radius, norm, norm, rr, rr], axis=0))
    ones = [jnp.where((row == 5) | (row == 7), 1.0, c) for c in cut]
    streamed = jnp.concatenate([ones[a] for a, _ in GROUPS], axis=0).astype(bf16)
    streamed = jnp.concatenate([streamed, jnp.zeros((80, TILE), bf16)], axis=0)
    moved = jnp.concatenate([depth, depth * x3], axis=0)
    p1, p2, p3 = pieces(jnp.concatenate([moved, moved], axis=0))
    weights = jnp.concatenate(
        [jnp.where(row < 4, p1, p2), jnp.where(row < 4, p3, 0.0)], axis=0
    ).astype(bf16)
    return cut, streamed, weights


def held_features(cut):
    row = rows_of((8, TILE))
    blocks = []
    for a, b in GROUPS:
        own = 1.0 if (a, b) in ((0, 0), (0, 1), (0, 2)) else 0.0
        other = 1.0 if (a, b) in ((0, 0), (1, 0), (2, 0)) else 0.0
        scale_d = jnp.where(row < 3, -2.0, jnp.where(row == 3, 2.0, jnp.where(row == 5, own, 0.0)))
        scale_r = jnp.where(row == 3, 2.0, jnp.where(row == 7, own, 0.0))
        dist = cut[b] * scale_d + jnp.where(row == 4, other, 0.0)
        reach = cut[b] * scale_r + jnp.where(row == 6, other, 0.0)
        blocks.append(jnp.concatenate([dist, reach], axis=1))
    held = jnp.concatenate(blocks, axis=0).astype(bf16)
    return jnp.concatenate([held, jnp.zeros((80, 2 * TILE), bf16)], axis=0)


def store_tiles(a_out, p_out, first, made):
    eye = (rows_of((TILE, TILE)) == lax.broadcasted_iota(jnp.int32, (TILE, TILE), 1)).astype(bf16)
    for n in range(0, len(made), 2):
        pair = jnp.concatenate([made[n][1], made[n + 1][1]], axis=0)
        turned = lax.dot_general(
            eye, pair, (((1,), (1,)), ((), ())), preferred_element_type=f32
        ).astype(bf16)
        for h in range(2):
            a_out[first + n + h] = turned[:, h * TILE : (h + 1) * TILE]
            p_out[first + n + h] = made[n + h][2]


def take(src, idx):
    return jnp.take_along_axis(src, idx, axis=1, mode="promise_in_bounds")


def pair_sums(order, count, lists, a, b, p, join, own_tiles, tiles_ext):
    def step(n, carry):
        for h in range(UNROLL):
            u = order[n * UNROLL + h]
            m = u // own_tiles
            t = u - m * own_tiles
            held = b[u]
            acc = jnp.zeros((16, 2 * TILE), f32)
            for k in range(PARTNERS):
                q = m * tiles_ext + lists[m, k, t]
                both = jnp.dot(a[q], held, preferred_element_type=f32)
                reach = both[:, TILE:]
                inv = pltpu.reciprocal(both[:, :TILE], approx=True)
                ratio = reach * inv
                cubed = ratio * ratio * ratio
                sixth = cubed * cubed
                energy = sixth - cubed
                coeff = (energy + sixth) * inv
                high = coeff.astype(bf16)
                low = (coeff - high.astype(f32)).astype(bf16)
                left = jnp.concatenate([high, low], axis=0)
                right = jnp.concatenate([energy.astype(bf16), jnp.zeros((TILE, TILE), bf16)], axis=0)
                weights = p[q]
                acc += jnp.dot(
                    jnp.concatenate([weights, weights], axis=1),
                    jnp.concatenate([left, right], axis=1),
                    preferred_element_type=f32,
                )
            joined = acc[0:4] + acc[4:8] + acc[8:12]
            join[u] = jnp.concatenate([joined[:, :TILE], joined[:, TILE:]], axis=0)
        return carry

    lax.fori_loop(0, (count + UNROLL - 1) // UNROLL, step, 0)


def own_kernel(
    lists, place, coords, types, tables,
    a, b, p, join, center, order, count,
    near, depth_s, radius_s,
):
    images = coords.shape[1]
    own_tiles = types.shape[0]
    tiles_ext = a.shape[0] // images
    wells = jnp.broadcast_to(tables[0:1], (8, TILE))
    radii = jnp.broadcast_to(tables[1:2], (8, TILE))
    for n in range(own_tiles // 8):
        kind = types[8 * n : 8 * n + 8]
        depth_s[8 * n : 8 * n + 8] = take(wells, kind)
        radius_s[8 * n : 8 * n + 8] = take(radii, kind)
    for c in range(3):
        total = coords[c, :, 0:TILE]
        for t in range(1, own_tiles):
            total = total + coords[c, :, t * TILE : (t + 1) * TILE]
        middle = jnp.sum(total, axis=1, keepdims=True) * (1.0 / (own_tiles * TILE))
        for m in range(images):
            center[m, c : c + 1] = jnp.broadcast_to(middle[m : m + 1], (1, TILE))

    n_near, n_far = jnp.int32(0), jnp.int32(0)
    for m in range(images):
        middle = center[m, 0:3]

        def build(n, carry):
            n_near, n_far = carry
            made = []
            for h in range(8):
                t = 8 * n + h
                u = m * own_tiles + t
                x3 = jnp.concatenate([coords[c, m : m + 1, lanes(t)] for c in range(3)], axis=0)
                made.append(
                    streamed_features(x3 - middle, depth_s[pl.ds(t, 1)], radius_s[pl.ds(t, 1)])
                )
                b[u] = held_features(made[-1][0])
                last = lists[m, 0, t]
                for k in range(1, PARTNERS):
                    last = jnp.maximum(last, lists[m, k, t])
                inside = (last < own_tiles).astype(jnp.int32)
                near[n_near] = u
                order[n_far] = u
                n_near = n_near + inside
                n_far = n_far + (1 - inside)
            store_tiles(a, p, m * tiles_ext + 8 * n, made)
            return n_near, n_far

        n_near, n_far = lax.fori_loop(0, own_tiles // 8, build, (n_near, n_far))
    last_near = near[jnp.maximum(n_near - 1, 0)]
    last_far = order[jnp.maximum(n_far - 1, 0)]
    for h in range(UNROLL):
        near[n_near + h] = last_near
        order[n_far + h] = last_far
    count[0] = n_far
    pair_sums(near, n_near, lists, a, b, p, join, own_tiles, tiles_ext)


def rest_kernel(
    lists, place, order, count, coords, below, above, types, tables, hidx, ref, restr, prev, nxt,
    center, b, a_in, p_in, join_in,
    force, sums, a, p, join,
    halo_x, depth_s, radius_s, own_depth,
):
    images = coords.shape[1]
    own_tiles = types.shape[0]
    tiles_ext = a.shape[0] // images
    halo_tiles = tiles_ext - own_tiles
    side_tiles = halo_tiles // 2
    wells = jnp.broadcast_to(tables[0:1], (8, TILE))
    radii = jnp.broadcast_to(tables[1:2], (8, TILE))
    for n in range(own_tiles // 8):
        own_depth[8 * n : 8 * n + 8] = take(wells, types[8 * n : 8 * n + 8])

    for side, source in enumerate((below, above)):
        low, high = [], []
        for m in range(images):
            idx = jnp.concatenate(
                [hidx[m, side : side + 1, q * TILE : (q + 1) * TILE] for q in range(side_tiles)],
                axis=0,
            )
            low.append(idx & (TILE - 1))
            high.append(idx >> 7)

        def gather_row(r, carry):
            out = []
            for m in range(images):
                hit = high[m] == r
                for c in range(4):
                    wide = jnp.broadcast_to(source[c, m : m + 1, lanes(r)], (8, TILE))
                    out.append(jnp.where(hit, take(wide, low[m]), carry[4 * m + c]))
            return tuple(out)

        zero = jnp.zeros((8, TILE), f32)
        found = lax.fori_loop(0, own_tiles, gather_row, (zero,) * (4 * images), unroll=8)
        inside = place[side].astype(f32)
        spot = slice(side * side_tiles, (side + 1) * side_tiles)
        for m in range(images):
            for c in range(3):
                halo_x[m, c, spot] = found[4 * m + c]
            kind = found[4 * m + 3].astype(jnp.int32)
            depth_s[m, spot] = take(wells, kind) * inside
            radius_s[m, spot] = take(radii, kind)

    for m in range(images):
        middle = center[m, 0:3]

        def build(n, carry):
            made = []
            for h in range(8):
                t = 8 * n + h
                x3 = jnp.concatenate([halo_x[m, c, pl.ds(t, 1)] for c in range(3)], axis=0)
                made.append(
                    streamed_features(
                        x3 - middle, depth_s[m, pl.ds(t, 1)], radius_s[m, pl.ds(t, 1)]
                    )
                )
            store_tiles(a, p, m * tiles_ext + own_tiles + 8 * n, made)
            return carry

        lax.fori_loop(0, halo_tiles // 8, build, 0)

    pair_sums(order, count[0], lists, a, b, p, join, own_tiles, tiles_ext)

    def finish(n, carry):
        carry = list(carry)
        for h in range(4):
            t = 4 * n + h
            at = lanes(t)
            depth = own_depth[pl.ds(t, 1)]
            stiff = restr[:, at]
            rows = [join[m * own_tiles + t] for m in range(images)]
            weight = jnp.concatenate([r[0:1] for r in rows], axis=0)
            carry[5] += 2.0 * depth * jnp.concatenate([r[4:5] for r in rows], axis=0)
            for c in range(3):
                x = coords[c, :, at]
                middle = jnp.concatenate([center[m, c : c + 1] for m in range(images)], axis=0)
                moved = jnp.concatenate([r[1 + c : 2 + c] for r in rows], axis=0)
                offset = x - ref[c : c + 1, at]
                pull = stiff * offset
                total = 24.0 * depth * ((x - middle) * weight - moved) - pull
                force[c, :, at] = total
                before = jnp.concatenate([prev[c, :, at], x[0:1]], axis=0)
                after = jnp.concatenate([x[1:2], nxt[c, :, at]], axis=0)
                ahead, behind = after - x, x - before
                both_ways, bend = ahead + behind, ahead - behind
                carry[0] += both_ways * both_ways
                carry[1] += both_ways * bend
                carry[2] += bend * bend
                carry[3] += total * both_ways
                carry[4] += total * bend
                carry[5] += 0.5 * pull * offset
        return tuple(carry)

    zero = jnp.zeros((images, TILE), f32)
    line = lax.fori_loop(0, own_tiles // 4, finish, (zero,) * 6)
    line = jnp.concatenate(list(line) + [jnp.zeros((16 - 6 * images, TILE), f32)], axis=0)
    row, lane = rows_of((16, 16)), lax.broadcasted_iota(jnp.int32, (16, 16), 1)
    totals = jnp.sum(line, axis=1, keepdims=True)
    totals = jnp.sum(jnp.where(row == lane, totals, 0.0), axis=0, keepdims=True)
    sums[...] = jnp.broadcast_to(totals, (16, 16))


def band_kernel(place, shares, force, coords, prev, nxt, out, energies):
    total = jnp.sum(shares[...], axis=0, keepdims=True)
    images, atoms = coords.shape[1], coords.shape[2]
    parts = []
    for m in range(images):
        s_sq, cross, b_sq, f_s, f_b, energy = [
            total[:, images * n + m : images * n + m + 1] for n in range(6)
        ]
        energies[m] = (energy / (16 * atoms))[0, 0]
        base = 0.25 * (s_sq + b_sq) + small_eps
        ahead_sq, behind_sq = base + 0.5 * cross, base - 0.5 * cross
        ahead_len, behind_len = jnp.sqrt(ahead_sq), jnp.sqrt(behind_sq)
        inverse_sum = 1.0 / ahead_len + 1.0 / behind_len
        alpha = 0.5 * inverse_sum
        beta = -0.5 * cross / (ahead_sq * behind_sq * inverse_sum)
        tan_sq = alpha * alpha * s_sq + 2.0 * alpha * beta * cross + beta * beta * b_sq
        tan_len = jnp.sqrt(jnp.maximum(tan_sq, 0.0) + small_eps)
        along = (alpha * f_s + beta * f_b) / tan_len
        stretch = cross / (ahead_len + behind_len)
        gain = (spring_k * stretch - along) / tan_len
        gain = jnp.where(place[2 + m] == 1, 0.0, gain)
        parts.append((gain * alpha, gain * beta))
    for_s = jnp.concatenate([jnp.broadcast_to(q[0], (1, TILE)) for q in parts], axis=0)
    for_b = jnp.concatenate([jnp.broadcast_to(q[1], (1, TILE)) for q in parts], axis=0)
    for t in range(atoms // TILE):
        at = slice(t * TILE, (t + 1) * TILE)
        for c in range(3):
            x = coords[c, :, at]
            before = jnp.concatenate([prev[c, :, at], x[0:1]], axis=0)
            after = jnp.concatenate([x[1:2], nxt[c, :, at]], axis=0)
            ahead, behind = after - x, x - before
            out[c, :, at] = force[c, :, at] + for_s * (ahead + behind) + for_b * (ahead - behind)


def ring(axis, step):
    n = lax.axis_size(axis)
    return [(i, (i + step) % n) for i in range(n)]


def shape(dims, dtype=f32):
    return jax.ShapeDtypeStruct(dims, dtype)


def params(mib, **more):
    return dict(compiler_params=pltpu.CompilerParams(vmem_limit_bytes=mib << 20), **more)


def body(
    coords, ref_coords, restraint, atom_types, well_table, radius_table, tile_lists, halo_index
):
    images, _, atoms = coords.shape
    tiles = atoms // TILE
    tiles_ext = tiles + 2 * halo_index.shape[2] // TILE
    slab, slabs = lax.axis_index("space"), lax.axis_size("space")
    coords = coords.transpose(1, 0, 2)
    types = atom_types.reshape(tiles, TILE)
    kinds = jnp.broadcast_to(atom_types.astype(f32), (1, images, atoms))
    feats = jnp.concatenate([coords, kinds], axis=0)
    below = lax.ppermute(feats, "space", ring("space", 1))
    above = lax.ppermute(feats, "space", ring("space", -1))
    prev = lax.ppermute(coords[:, images - 1 :], "image", ring("image", 1))
    nxt = lax.ppermute(coords[:, :1], "image", ring("image", -1))
    image, ranks = lax.axis_index("image"), lax.axis_size("image")
    place = [slab > 0, slab < slabs - 1, image == 0, image == ranks - 1]
    place = jnp.stack(place).astype(jnp.int32)
    tables = jnp.pad(
        jnp.stack([well_table, radius_table]), ((0, 0), (0, TILE - well_table.shape[0]))
    )
    own = images * tiles
    a, b, p, join, center, order, count = pl.pallas_call(
        own_kernel,
        out_shape=(
            shape((images * tiles_ext, TILE, TILE), bf16),
            shape((own, TILE, 2 * TILE), bf16),
            shape((images * tiles_ext, 16, TILE), bf16),
            shape((own, 8, TILE)),
            shape((images, 8, TILE)),
            shape((own + UNROLL,), jnp.int32),
            shape((1,), jnp.int32),
        ),
        in_specs=[SMEM] * 2 + [VMEM] * 3,
        out_specs=(VMEM,) * 5 + (SMEM,) * 2,
        scratch_shapes=[
            pltpu.SMEM((own + UNROLL,), jnp.int32),
            pltpu.VMEM((tiles, TILE), f32),
            pltpu.VMEM((tiles, TILE), f32),
        ],
        cost_estimate=pl.CostEstimate(flops=60 * 10**9, bytes_accessed=10**6, transcendentals=0),
        name="own",
        **params(16),
    )(tile_lists, place, coords, types, tables)
    force, sums, *_ = pl.pallas_call(
        rest_kernel,
        out_shape=(
            shape((3, images, atoms)),
            shape((16, 16)),
            shape(a.shape, bf16),
            shape(p.shape, bf16),
            shape(join.shape),
        ),
        in_specs=[SMEM] * 4 + [VMEM] * 15,
        out_specs=(VMEM,) * 5,
        input_output_aliases={16: 2, 17: 3, 18: 4},
        scratch_shapes=[
            pltpu.VMEM((images, 3, tiles_ext - tiles, TILE), f32),
            pltpu.VMEM((images, tiles_ext - tiles, TILE), f32),
            pltpu.VMEM((images, tiles_ext - tiles, TILE), f32),
            pltpu.VMEM((tiles, TILE), f32),
        ],
        name="rest",
        **params(16),
    )(
        tile_lists, place, order, count, coords, below, above, types, tables, halo_index,
        ref_coords, restraint[None], prev, nxt, center, b, a, p, join,
    )
    shares = lax.all_to_all(sums, "space", 0, 0, tiled=True)
    out, energies = pl.pallas_call(
        band_kernel,
        out_shape=(shape((3, images, atoms)), shape((images,))),
        in_specs=[SMEM] + [VMEM] * 5,
        out_specs=(VMEM, SMEM),
        name="band",
        **params(8),
    )(place, shares, force, coords, prev, nxt)
    return out.transpose(1, 0, 2), energies


def solution(mesh):
    in_specs = (
        P("image", None, "space"),
        P(None, "space"),
        P("space"),
        P("space"),
        P(),
        P(),
        P("image", None, "space"),
        P("image", None, "space"),
    )
    out_specs = (P("image", None, "space"), P("image"))
    return jax.shard_map(body, mesh=mesh, in_specs=in_specs, out_specs=out_specs, check_vma=False)
```

time: 84.3 us -> 72.2 us (0.86)
  waiting for transfers between devices: 20.1 us -> 0.01 us
  blocking collectives: 0 us -> 18.3 us
  starting transfers between devices: 18.1 us -> 9.15 us
  Pallas kernels: 39.3 us -> 37 us
  other arithmetic: 1.41 us -> 2.57 us
    all_to_all x0 -> x1, blocking collectives: none -> 18.3 us  [body(): shares = lax.all_to_all(sums, 'space', 0, 0, tiled=True)]
    all_to_all x1 -> x0, waiting for transfers between devices: 9.5 us -> none  [body(): shares = lax.all_to_all(sums, 'space', 0, 0, tiled=True)]
    all_to_all x1 -> x0, starting transfers between devices: 8.95 us -> none  [body(): shares = lax.all_to_all(sums, 'space', 0, 0, tiled=True)]
    ppermute x2, waiting for transfers between devices: 4.88 us -> 0.01 us  [the longest x1 0.01 us: body(): prev = lax.ppermute(coords[:, images - 1:], 'image', ring('image', 1))]
    ppermute x1, waiting for transfers between devices: 4.37 us -> 0.01 us  [body(): below = lax.ppermute(feats, 'space', ring('space', 1))]
    pallas_call x2 -> x3, Pallas kernels: 39.3 us -> 37 us  [the longest x1 18.9 us: body(): pl.pallas_call(own_kernel, out_shape=(shape((images * tiles_ext, TILE, TI...]
    pallas_call x1 -> x0, local copies, waits for them, and re-layouts: 1.78 us -> none  [body(): pl.pallas_call(band_kernel, out_shape=(jax.ShapeDtypeStruct((images, 3, a...]
    ppermute x1, waiting for transfers between devices: 1.34 us -> 0.01 us  [body(): above = lax.ppermute(feats, 'space', ring('space', -1))]
  transfers between devices with their start and end apart: 5 -> 4, of which waited for: 5 -> 0; matrix products, arithmetic and copies ran while one was open for 1% -> 3% of each run, Pallas kernels for 0% -> 26%
where the time goes in v2:
time: 72.2 us; the launch traced here: 71.3 us
  Pallas kernels  37 us (51%)
  blocking collectives  18.3 us (25%)
  starting transfers between devices  9.15 us (13%)
  local copies, waits for them, and re-layouts  3.6 us (5%)
  other arithmetic  2.57 us (4%)
    pallas_call x1, Pallas kernels, body(): pl.pallas_call(own_kernel, out_shape=(shape((images * tiles_ext, TILE, TI...  18.9 us
    all_to_all x1, blocking collectives, body(): shares = lax.all_to_all(sums, 'space', 0, 0, tiled=True)  18.3 us
    pallas_call x1, Pallas kernels, body(): pl.pallas_call(rest_kernel, out_shape=(shape((3, images, atoms)), shape((...  16.2 us
    ppermute x1, starting transfers between devices, body(): above = lax.ppermute(feats, 'space', ring('space', -1))  8.56 us
    unnamed x12, local copies, waits for them, and re-layouts  2.38 us
    pallas_call x1, Pallas kernels, body(): pl.pallas_call(band_kernel, out_shape=(shape((3, images, atoms)), shape((...  1.87 us
  transfers between devices with their start and end apart: 4, of which 0 were waited for; matrix products, arithmetic and copies ran while one was open for 3% of the time, Pallas kernels for 26%

profile of v2, /device:TPU:6, one launch (start us, length us, event | category | flops | bytes accessed | tf_op | source)
XLA Modules:
  0.0 71.3 jit_solution(13657822356904844634)
XLA Ops:
  0.6 0.8 %convert_element_type.9 = f32[8192]{0:T(1024)S(1)} convert(s32[8192]{0:T(1024)} %param.11) | non-fusion elementwise | flops 8192 | bytes 65536 | tf_op jit(solution)/shard_map/convert_element_type | solution.py:336
  1.4 1.0 %pad_maximum_fusion = f32[4,2,8192]{2,1,0:T(2,128)S(1)} fusion(f32[1,2,8192]{2,1,0:T(2,128)S(1)} %broadcast_in_dim.6, f32[3,2,8192]{2,1,0:T(2,128)} %bitcast.14), kind=kLoop, calls=%fused_computation | loop fusion | flops 65536 | bytes 524288 | tf_op jit(solution)/shard_map/concatenate | solution.py:337
  2.5 8.6 %collective-permute-start.1 = (f32[4,2,8192]{2,1,0:T(2,128)S(1)}, f32[4,2,8192]{2,1,0:T(2,128)S(1)}, u32[]{:S(2)}, u32[]{:S(2)}) collective-permute-start(f32[4,2,8192]{2,1,0:T(2,128)S(1)} %pad_maximum_fusion), channel_id=1, source_target_pairs={{0,15},{1,0},{2,1},{3,2},{4,3},{5,4},{6,5},{7,6},{8,7},{9,8},{10,9... | collective-permute-start | bytes 786440 | tf_op jit(solution)/shard_map/ppermute | solution.py:339
  11.0 0.0 collective-permute-start
  11.0 1.2 %fusion = (f32[3,1,8192]{2,1,0:T(1,128)S(1)}, f32[3,1,8192]{2,1,0:T(1,128)S(1)}) fusion(f32[3,2,8192]{2,1,0:T(2,128)} %bitcast.15), kind=kLoop, calls=%fused_computation.3 | loop fusion | bytes 393216 | tf_op jit(solution)/shard_map/slice | solution.py:341
  12.2 0.2 collective-permute-start.3
  12.4 0.4 collective-permute-start.2
  12.8 0.7 select_maximum_fusion.tables
  13.5 0.1 add_convert_fusion.place
  13.6 0.0 copy-start
  13.6 0.9 %copy-done = f32[2,3,8192]{2,0,1:T(2,128)S(1)} copy-done((f32[2,3,8192]{2,0,1:T(2,128)S(1)}, f32[2,3,8192]{2,0,1:T(2,128)}, u32[]{:S(2)}) %copy-start) | copy-done | bytes 196632
  14.5 0.8 %copy-done.2 = s32[8192]{0:T(1024)S(1)} copy-done((s32[8192]{0:T(1024)S(1)}, s32[8192]{0:T(1024)}, u32[]{:S(2)}) %copy-start.2) | copy-done | bytes 32792
  15.3 0.7 copy-done.5
  16.0 18.9 %own.1 = (bf16[160,128,128]{2,1,0:T(8,128)(2,1)S(1)}, bf16[128,128,256]{2,1,0:T(8,128)(2,1)S(1)}, bf16[160,16,128]{2,1,0:T(8,128)(2,1)S(1)}, f32[128,8,128]{2,1,...) custom-call(s32[2,4,64]{2,1,0:T(4,128)S(1)} %copy-done.5, s32[4]{0:T(128)S(1)} %add_convert_fusion.place, ...), custom_call_target="tpu_custom_call" | custom-call | flops 60000002048 | bytes 1000000 | tf_op jit(solution)/shard_map/own/pallas_call | solution.py:349
  34.8 0.0 collective-permute-done.3.nxt
  34.9 0.0 collective-permute-done.2.prev
  34.9 0.0 collective-permute-done.1.above
  34.9 0.0 collective-permute-done.below
  34.9 0.0 copy-done.1
  34.9 0.0 copy-done.3
  34.9 0.0 copy-done.4
  34.9 16.2 %rest.1 = (f32[3,2,8192]{2,1,0:T(2,128)S(1)}, f32[16,16]{1,0:T(8,128)S(1)}, bf16[160,128,128]{2,1,0:T(8,128)(2,1)S(1)}, bf16[160,16,128]{2,1,0:T(8,128)(2,1)S(1)}, f32[128,8,128]{2,1,0:T(8,128)S(1)}) custom-call(s32[2,4,64]{2,1,0:T(4,128)S(1)} %copy-done.5, ...), custom_call_target="tpu_custom_call", output_to_operand_aliasing={{2}: (16, {}), {3}: (17, {}), {4}: (18, {})} | custom-call | tf_op jit(solution)/shard_map/rest/pallas_call | solution.py:371
  51.1 18.3 %all_to_all.11 = f32[16,1,16]{2,1,0:T(1,128)S(1)} all-to-all(f32[16,1,16]{2,1,0:T(1,128)S(1)} %bitcast.23), channel_id=1, replica_groups=mesh['image'=16,'space'=16] {'space'}, dimensions={0} | all-to-all | bytes 2048 | tf_op jit(solution)/shard_map/all_to_all | solution.py:395
  69.5 1.9 %band.1 = (f32[3,2,8192]{2,1,0:T(2,128)}, f32[2]{0:T(128)}) custom-call(s32[4]{0:T(128)S(1)} %add_convert_fusion.place, f32[16,16]{1,0:T(8,128)S(1)} %bitcast.22, f32[3,2,8192]{2,1,0:T(2,128)S(1)} %get-tuple-element.21.force, f32[3,2,8192]{2,1,0:T(2,128)S(1)} %bitcast.18, f32[3,1,8192]{2,1,0:T(1,128)S(1)} %collective-permute-done.2.prev, ...), custom_call_target="tpu_custom_call" | custom-call | tf_op jit(solution)/shard_map/band/pallas_call | solution.py:396
  (6 shorter events, 0.0 us)
Async XLA Ops:
  2.5 32.4 %collective-permute-start.1 = (f32[4,2,8192]{2,1,0:T(2,128)S(1)}, f32[4,2,8192]{2,1,0:T(2,128)S(1)}, u32[]{:S(2)}, u32[]{:S(2)}) collective-permute-start(f32[4,2,8192]{2,1,0:T(2,128)S(1)} %pad_maximum_fusion), channel_id=1, source_target_pairs={{0,15},{1,0},{2,1},{3,2},{4,3},{5,4},{6,5},{7,6},{8,7},{9,8},{10,9... | collective-permute-start | bytes 786440 | tf_op jit(solution)/shard_map/ppermute | solution.py:339
  11.0 23.8 %collective-permute-start = (f32[4,2,8192]{2,1,0:T(2,128)S(1)}, f32[4,2,8192]{2,1,0:T(2,128)S(1)}, u32[]{:S(2)}, u32[]{:S(2)}) collective-permute-start(f32[4,2,8192]{2,1,0:T(2,128)S(1)} %pad_maximum_fusion), channel_id=1, source_target_pairs={{0,1},{1,2},{2,3},{3,4},{4,5},{5,6},{6,7},{7,8},{8,9},{9,10},{10,1... | collective-permute-start | bytes 786440 | tf_op jit(solution)/shard_map/ppermute | solution.py:338
  12.2 22.6 %collective-permute-start.3 = (f32[3,1,8192]{2,1,0:T(1,128)S(1)}, f32[3,1,8192]{2,1,0:T(1,128)S(1)}, u32[]{:S(2)}, u32[]{:S(2)}) collective-permute-start(f32[3,1,8192]{2,1,0:T(1,128)S(1)} %get-tuple-element.24), channel_id=1, source_target_pairs={{0,240},{16,0},{32,16},{48,32},{64,48},{80,64},{96,80},{112,96},{1... | collective-permute-start | bytes 294920 | tf_op jit(solution)/shard_map/ppermute | solution.py:341
  12.4 22.4 %collective-permute-start.2 = (f32[3,1,8192]{2,1,0:T(1,128)S(1)}, f32[3,1,8192]{2,1,0:T(1,128)S(1)}, u32[]{:S(2)}, u32[]{:S(2)}) collective-permute-start(f32[3,1,8192]{2,1,0:T(1,128)S(1)} %get-tuple-element.25), channel_id=1, source_target_pairs={{0,16},{16,32},{32,48},{48,64},{64,80},{80,96},{96,112},{112,128},... | collective-permute-start | bytes 294920 | tf_op jit(solution)/shard_map/ppermute | solution.py:340
  13.6 0.9 %copy-start = (f32[2,3,8192]{2,0,1:T(2,128)S(1)}, f32[2,3,8192]{2,0,1:T(2,128)}, u32[]{:S(2)}) copy-start(f32[2,3,8192]{2,0,1:T(2,128)} %param.8) | copy-start | bytes 589828
  14.5 0.8 %copy-start.2 = (s32[8192]{0:T(1024)S(1)}, s32[8192]{0:T(1024)}, u32[]{:S(2)}) copy-start(s32[8192]{0:T(1024)} %param.11) | copy-start | bytes 98308
  15.3 0.7 copy-start.5
  16.0 18.9 %copy-start.1 = (f32[3,8192]{1,0:T(4,128)S(1)}, f32[3,8192]{1,0:T(4,128)}, u32[]{:S(2)}) copy-start(f32[3,8192]{1,0:T(4,128)} %ref.1) | copy-start | bytes 294916
  16.0 18.9 %copy-start.3 = (f32[8192]{0:T(1024)S(1)}, f32[8192]{0:T(1024)}, u32[]{:S(2)}) copy-start(f32[8192]{0:T(1024)} %param.10) | copy-start | bytes 98308
  16.0 19.0 %copy-start.4 = (s32[2,2,1024]{2,1,0:T(2,128)S(1)}, s32[2,2,1024]{2,1,0:T(2,128)}, u32[]{:S(2)}) copy-start(s32[2,2,1024]{2,1,0:T(2,128)} %hidx.1) | copy-start | bytes 49156

commit v3 on v2

--- a/solution.py
+++ b/solution.py
@@ -7,13 +7,14 @@
 
 TILE = 128
 PARTNERS = 4
-UNROLL = 8
+UNROLL = 16
 spring_k = 2.0
 small_eps = 1e-06
 f32, bf16 = jnp.float32, jnp.bfloat16
 GROUPS = ((0, 0), (0, 1), (1, 0), (0, 2), (2, 0), (1, 1))
 VMEM = pl.BlockSpec(memory_space=pltpu.VMEM)
 SMEM = pl.BlockSpec(memory_space=pltpu.SMEM)
+HBM = pl.BlockSpec(memory_space=pltpu.HBM)
 
 
 def lanes(tile):
@@ -79,7 +80,7 @@
     return jnp.take_along_axis(src, idx, axis=1, mode="promise_in_bounds")
 
 
-def pair_sums(order, count, lists, a, b, p, join, own_tiles, tiles_ext):
+def pair_sums(order, steps, lists, a, b, p, join, own_tiles, tiles_ext):
     def step(n, carry):
         for h in range(UNROLL):
             u = order[n * UNROLL + h]
@@ -111,23 +112,58 @@
             join[u] = jnp.concatenate([joined[:, :TILE], joined[:, TILE:]], axis=0)
         return carry
 
-    lax.fori_loop(0, (count + UNROLL - 1) // UNROLL, step, 0)
+    lax.fori_loop(0, steps, step, 0)
+
+
+def prep_kernel(
+    coords_in, types_in, well_in, radius_in, lists_in,
+    feats, first, last, depth, radius, tables, lists, place,
+    types, narrow, sem,
+):
+    images = feats.shape[1]
+    moves = (
+        (types_in, types), (well_in, narrow.at[0]), (radius_in, narrow.at[1]),
+        (coords_in, feats.at[0:3]), (lists_in, lists),
+    )
+    copies = [pltpu.make_async_copy(src, dst, sem.at[n]) for n, (src, dst) in enumerate(moves)]
+    for copy in copies:
+        copy.start()
+    slab, image = lax.axis_index("space"), lax.axis_index("image")
+    place[0] = (slab > 0).astype(jnp.int32)
+    place[1] = (slab < lax.axis_size("space") - 1).astype(jnp.int32)
+    place[2] = (image == 0).astype(jnp.int32)
+    place[3] = (image == lax.axis_size("image") - 1).astype(jnp.int32)
+    for copy in copies[:3]:
+        copy.wait()
+    for n in range(2):
+        tables[n : n + 1] = jnp.concatenate([narrow[n], jnp.zeros_like(narrow[n])], axis=1)
+    wells = jnp.broadcast_to(tables[0:1], (8, TILE))
+    radii = jnp.broadcast_to(tables[1:2], (8, TILE))
+    for n in range(types.shape[0] // 8):
+        kind = types[8 * n : 8 * n + 8]
+        depth[8 * n : 8 * n + 8] = take(wells, kind)
+        radius[8 * n : 8 * n + 8] = take(radii, kind)
+        kind = kind.astype(f32)
+        for h in range(8):
+            t = 8 * n + h
+            feats[3, :, t * TILE : (t + 1) * TILE] = jnp.broadcast_to(
+                kind[h : h + 1], (images, TILE)
+            )
+    for copy in copies[3:]:
+        copy.wait()
+    for c in range(3):
+        first[c] = feats[c, 0:1]
+        last[c] = feats[c, images - 1 : images]
 
 
 def own_kernel(
-    lists, place, coords, types, tables,
+    lists, place, coords, depth_s, radius_s,
     a, b, p, join, center, order, count,
-    near, depth_s, radius_s,
+    near,
 ):
     images = coords.shape[1]
-    own_tiles = types.shape[0]
+    own_tiles = depth_s.shape[0]
     tiles_ext = a.shape[0] // images
-    wells = jnp.broadcast_to(tables[0:1], (8, TILE))
-    radii = jnp.broadcast_to(tables[1:2], (8, TILE))
-    for n in range(own_tiles // 8):
-        kind = types[8 * n : 8 * n + 8]
-        depth_s[8 * n : 8 * n + 8] = take(wells, kind)
-        radius_s[8 * n : 8 * n + 8] = take(radii, kind)
     for c in range(3):
         total = coords[c, :, 0:TILE]
         for t in range(1, own_tiles):
@@ -163,30 +199,30 @@
             return n_near, n_far
 
         n_near, n_far = lax.fori_loop(0, own_tiles // 8, build, (n_near, n_far))
-    last_near = near[jnp.maximum(n_near - 1, 0)]
-    last_far = order[jnp.maximum(n_far - 1, 0)]
-    for h in range(UNROLL):
-        near[n_near + h] = last_near
-        order[n_far + h] = last_far
-    count[0] = n_far
-    pair_sums(near, n_near, lists, a, b, p, join, own_tiles, tiles_ext)
+    steps = n_near // UNROLL
+
+    def move(n, n_far):
+        order[n_far] = near[n]
+        return n_far + 1
+
+    n_far = lax.fori_loop(steps * UNROLL, n_near, move, n_far)
+    count[0] = n_far // UNROLL
+    pair_sums(near, steps, lists, a, b, p, join, own_tiles, tiles_ext)
 
 
 def rest_kernel(
-    lists, place, order, count, coords, below, above, types, tables, hidx, ref, restr, prev, nxt,
+    lists, place, order, count, coords, below, above, own_depth, tables, hidx, ref, restr, prev, nxt,
     center, b, a_in, p_in, join_in,
     force, sums, a, p, join,
-    halo_x, depth_s, radius_s, own_depth,
+    halo_x, depth_s, radius_s,
 ):
     images = coords.shape[1]
-    own_tiles = types.shape[0]
+    own_tiles = own_depth.shape[0]
     tiles_ext = a.shape[0] // images
     halo_tiles = tiles_ext - own_tiles
     side_tiles = halo_tiles // 2
     wells = jnp.broadcast_to(tables[0:1], (8, TILE))
     radii = jnp.broadcast_to(tables[1:2], (8, TILE))
-    for n in range(own_tiles // 8):
-        own_depth[8 * n : 8 * n + 8] = take(wells, types[8 * n : 8 * n + 8])
 
     for side, source in enumerate((below, above)):
         low, high = [], []
@@ -330,21 +366,36 @@
     images, _, atoms = coords.shape
     tiles = atoms // TILE
     tiles_ext = tiles + 2 * halo_index.shape[2] // TILE
-    slab, slabs = lax.axis_index("space"), lax.axis_size("space")
-    coords = coords.transpose(1, 0, 2)
-    types = atom_types.reshape(tiles, TILE)
-    kinds = jnp.broadcast_to(atom_types.astype(f32), (1, images, atoms))
-    feats = jnp.concatenate([coords, kinds], axis=0)
+    kinds = well_table.shape[0]
+    feats, first, last, depth, radius, tables, lists, place = pl.pallas_call(
+        prep_kernel,
+        out_shape=(
+            shape((4, images, atoms)),
+            shape((3, 1, atoms)),
+            shape((3, 1, atoms)),
+            shape((tiles, TILE)),
+            shape((tiles, TILE)),
+            shape((2, TILE)),
+            shape(tile_lists.shape, jnp.int32),
+            shape((4,), jnp.int32),
+        ),
+        in_specs=[HBM] * 5,
+        out_specs=(VMEM,) * 7 + (SMEM,),
+        scratch_shapes=[
+            pltpu.VMEM((tiles, TILE), jnp.int32),
+            pltpu.VMEM((2, 1, kinds), f32),
+            pltpu.SemaphoreType.DMA((5,)),
+        ],
+        name="prep",
+        **params(8),
+    )(
+        coords.transpose(1, 0, 2), atom_types.reshape(tiles, TILE), well_table[None],
+        radius_table[None], tile_lists,
+    )
     below = lax.ppermute(feats, "space", ring("space", 1))
     above = lax.ppermute(feats, "space", ring("space", -1))
-    prev = lax.ppermute(coords[:, images - 1 :], "image", ring("image", 1))
-    nxt = lax.ppermute(coords[:, :1], "image", ring("image", -1))
-    image, ranks = lax.axis_index("image"), lax.axis_size("image")
-    place = [slab > 0, slab < slabs - 1, image == 0, image == ranks - 1]
-    place = jnp.stack(place).astype(jnp.int32)
-    tables = jnp.pad(
-        jnp.stack([well_table, radius_table]), ((0, 0), (0, TILE - well_table.shape[0]))
-    )
+    prev = lax.ppermute(last, "image", ring("image", 1))
+    nxt = lax.ppermute(first, "image", ring("image", -1))
     own = images * tiles
     a, b, p, join, center, order, count = pl.pallas_call(
         own_kernel,
@@ -354,20 +405,18 @@
             shape((images * tiles_ext, 16, TILE), bf16),
             shape((own, 8, TILE)),
             shape((images, 8, TILE)),
-            shape((own + UNROLL,), jnp.int32),
+            shape((own,), jnp.int32),
             shape((1,), jnp.int32),
         ),
         in_specs=[SMEM] * 2 + [VMEM] * 3,
         out_specs=(VMEM,) * 5 + (SMEM,) * 2,
         scratch_shapes=[
-            pltpu.SMEM((own + UNROLL,), jnp.int32),
-            pltpu.VMEM((tiles, TILE), f32),
-            pltpu.VMEM((tiles, TILE), f32),
+            pltpu.SMEM((own,), jnp.int32),
         ],
         cost_estimate=pl.CostEstimate(flops=60 * 10**9, bytes_accessed=10**6, transcendentals=0),
         name="own",
         **params(16),
-    )(tile_lists, place, coords, types, tables)
+    )(lists, place, feats, depth, radius)
     force, sums, *_ = pl.pallas_call(
         rest_kernel,
         out_shape=(
@@ -384,12 +433,11 @@
             pltpu.VMEM((images, 3, tiles_ext - tiles, TILE), f32),
             pltpu.VMEM((images, tiles_ext - tiles, TILE), f32),
             pltpu.VMEM((images, tiles_ext - tiles, TILE), f32),
-            pltpu.VMEM((tiles, TILE), f32),
         ],
         name="rest",
         **params(16),
     )(
-        tile_lists, place, order, count, coords, below, above, types, tables, halo_index,
+        lists, place, order, count, feats, below, above, depth, tables, halo_index,
         ref_coords, restraint[None], prev, nxt, center, b, a, p, join,
     )
     shares = lax.all_to_all(sums, "space", 0, 0, tiled=True)
@@ -400,7 +448,7 @@
         out_specs=(VMEM, SMEM),
         name="band",
         **params(8),
-    )(place, shares, force, coords, prev, nxt)
+    )(place, shares, force, feats, prev, nxt)
     return out.transpose(1, 0, 2), energies
 
 

time: 72.2 us -> 68.7 us (0.952)
  other arithmetic: 2.57 us -> 0 us
  starting transfers between devices: 9.15 us -> 11.2 us
  blocking collectives: 18.3 us -> 17 us
  Pallas kernels: 37 us -> 35.8 us
    pallas_call x1, Pallas kernels: 18.9 us -> 14 us  [body(): pl.pallas_call(own_kernel, out_shape=(shape((images * tiles_ext, TILE, TI...]
    pallas_call x1, Pallas kernels: 16.2 us -> 18.9 us  [body(): pl.pallas_call(rest_kernel, out_shape=(shape((3, images, atoms)), shape((...]
    ppermute x2, starting transfers between devices: 0.59 us -> 2.64 us  [the longest x1 2.64 us: body(): nxt = lax.ppermute(first, 'image', ring('image', -1))]
    all_to_all x1, blocking collectives: 18.3 us -> 17 us  [body(): shares = lax.all_to_all(sums, 'space', 0, 0, tiled=True)]
    unnamed x12 -> x16, local copies, waits for them, and re-layouts: 2.38 us -> 3.68 us
    slice x1 -> x0, local copies, waits for them, and re-layouts: 1.19 us -> none  [body(): nxt = lax.ppermute(coords[:, :1], 'image', ring('image', -1))]
    concatenate x1 -> x0, other arithmetic: 1.05 us -> none  [body(): feats = jnp.concatenate([coords, kinds], axis=0)]
    pallas_call x0 -> x1, Pallas kernels: none -> 1.04 us  [body(): pl.pallas_call(prep_kernel, out_shape=(shape((4, images, atoms)), shape((...]
  transfers between devices with their start and end apart: 4 -> 4, of which waited for: 0 -> 0; matrix products, arithmetic and copies ran while one was open for 3% -> 0% of each run, Pallas kernels for 26% -> 20%
where the time goes in v3:
time: 68.7 us; the launch traced here: 68.4 us
  Pallas kernels  35.8 us (52%)
  blocking collectives  17 us (25%)
  starting transfers between devices  11.2 us (16%)
  local copies, waits for them, and re-layouts  3.68 us (5%)
  between operations  0.72 us (1%)
    pallas_call x1, Pallas kernels, body(): pl.pallas_call(rest_kernel, out_shape=(shape((3, images, atoms)), shape((...  18.9 us
    all_to_all x1, blocking collectives, body(): shares = lax.all_to_all(sums, 'space', 0, 0, tiled=True)  17 us
    pallas_call x1, Pallas kernels, body(): pl.pallas_call(own_kernel, out_shape=(shape((images * tiles_ext, TILE, TI...  14 us
    ppermute x1, starting transfers between devices, body(): above = lax.ppermute(feats, 'space', ring('space', -1))  8.56 us
    unnamed x16, local copies, waits for them, and re-layouts  3.68 us
    ppermute x1, starting transfers between devices, body(): nxt = lax.ppermute(first, 'image', ring('image', -1))  2.64 us
    pallas_call x1, Pallas kernels, body(): pl.pallas_call(band_kernel, out_shape=(shape((3, images, atoms)), shape((...  1.87 us
  transfers between devices with their start and end apart: 4, of which 0 were waited for; matrix products, arithmetic and copies ran while one was open for 0% of the time, Pallas kernels for 20%

profile of v3, /device:TPU:6, one launch (start us, length us, event | category | flops | bytes accessed | tf_op | source)
XLA Modules:
  0.0 68.4 jit_solution(12962741589968220702)
XLA Ops:
  0.6 0.0 copy-start
  0.6 0.9 %copy-done = f32[2,3,8192]{2,0,1:T(2,128)S(1)} copy-done((f32[2,3,8192]{2,0,1:T(2,128)S(1)}, f32[2,3,8192]{2,0,1:T(2,128)}, u32[]{:S(2)}) %copy-start) | copy-done | bytes 196632
  1.6 0.0 copy-start.3
  1.6 0.8 %copy-done.3 = s32[8192]{0:T(1024)S(1)} copy-done((s32[8192]{0:T(1024)S(1)}, s32[8192]{0:T(1024)}, u32[]{:S(2)}) %copy-start.3) | copy-done | bytes 32792
  2.3 0.0 copy-start.5
  2.3 0.7 %copy-done.5 = s32[2,4,64]{2,1,0:T(4,128)S(1)} copy-done((s32[2,4,64]{2,1,0:T(4,128)S(1)}, s32[2,4,64]{2,1,0:T(4,128)}, u32[]{:S(2)}) %copy-start.5) | copy-done | bytes 2072
  3.0 0.7 copy-done.6
  3.7 0.7 copy-done.7
  4.3 1.0 %prep.1 = (f32[4,2,8192]{2,1,0:T(2,128)S(1)}, f32[3,1,8192]{2,1,0:T(1,128)S(1)}, f32[3,1,8192]{2,1,0:T(1,128)S(1)}, f32[64,128]{1,0:T(8,128)S(1)}, f32[64,128]{1...) custom-call(f32[3,2,8192]{2,1,0:T(2,128)S(1)} %bitcast.10, s32[64,128]{1,0:T(8,128)S(1)} %bitcast.13, ...), custom_call_target="tpu_custom_call" | custom-call | tf_op jit(solution)/shard_map/prep/pallas_call | solution.py:370
  5.4 8.6 %collective-permute-start.1 = (f32[4,2,8192]{2,1,0:T(2,128)S(1)}, f32[4,2,8192]{2,1,0:T(2,128)S(1)}, u32[]{:S(2)}, u32[]{:S(2)}) collective-permute-start(f32[4,2,8192]{2,1,0:T(2,128)S(1)} %get-tuple-element.23.coords), channel_id=1, source_target_pairs={{0,15},{1,0},{2,1},{3,2},{4,3},{5,4},{6,5},{7,6},{8,7},{9,8},{10,9... | collective-permute-start | bytes 786440 | tf_op jit(solution)/shard_map/ppermute | solution.py:396
  13.9 0.0 collective-permute-start
  13.9 0.0 collective-permute-start.2
  13.9 2.6 %collective-permute-start.3 = (f32[3,1,8192]{2,1,0:T(1,128)S(1)}, f32[3,1,8192]{2,1,0:T(1,128)S(1)}, u32[]{:S(2)}, u32[]{:S(2)}) collective-permute-start(f32[3,1,8192]{2,1,0:T(1,128)S(1)} %get-tuple-element.30), channel_id=1, source_target_pairs={{0,240},{16,0},{32,16},{48,32},{64,48},{80,64},{96,80},{112,96},{1... | collective-permute-start | bytes 294920 | tf_op jit(solution)/shard_map/ppermute | solution.py:398
  16.6 14.0 %own.1 = (bf16[160,128,128]{2,1,0:T(8,128)(2,1)S(1)}, bf16[128,128,256]{2,1,0:T(8,128)(2,1)S(1)}, bf16[160,16,128]{2,1,0:T(8,128)(2,1)S(1)}, f32[128,8,128]{2,1,...) custom-call(s32[2,4,64]{2,1,0:T(4,128)S(1)} %get-tuple-element.22.lists, ...), custom_call_target="tpu_custom_call" | custom-call | flops 60000002048 | bytes 1000000 | tf_op jit(solution)/shard_map/own/pallas_call | solution.py:400
  30.6 0.0 collective-permute-done.2.prev
  30.6 0.0 collective-permute-done.3.nxt
  30.6 0.0 collective-permute-done.1.above
  30.6 0.0 collective-permute-done.below
  30.6 0.0 copy-done.1
  30.7 0.0 copy-done.2
  30.7 0.0 copy-done.4
  30.7 18.9 %rest.1 = (f32[3,2,8192]{2,1,0:T(2,128)S(1)}, f32[16,16]{1,0:T(8,128)S(1)}, bf16[160,128,128]{2,1,0:T(8,128)(2,1)S(1)}, bf16[160,16,128]{2,1,0:T(8,128)(2,1)S(1)}, f32[128,8,128]{2,1,0:T(8,128)S(1)}) custom-call(s32[2,4,64]{2,1,0:T(4,128)S(1)} %get-tuple-element.22.lists, ...), custom_call_target="tpu_custom_call", output_to_operand_aliasing={{2}: (16, {}), {3}: (17, {}), {4}: (18, {})} | custom-call | tf_op jit(solution)/shard_map/rest/pallas_call | solution.py:420
  49.6 17.0 %all_to_all.11 = f32[16,1,16]{2,1,0:T(1,128)S(1)} all-to-all(f32[16,1,16]{2,1,0:T(1,128)S(1)} %bitcast.14), channel_id=1, replica_groups=mesh['image'=16,'space'=16] {'space'}, dimensions={0} | all-to-all | bytes 2048 | tf_op jit(solution)/shard_map/all_to_all | solution.py:443
  66.6 1.9 %band.1 = (f32[3,2,8192]{2,1,0:T(2,128)}, f32[2]{0:T(128)}) custom-call(s32[4]{0:T(128)S(1)} %get-tuple-element.21.place, f32[16,16]{1,0:T(8,128)S(1)} %bitcast.12, f32[3,2,8192]{2,1,0:T(2,128)S(1)} %get-tuple-element.37.force, f32[4,2,8192]{2,1,0:T(2,128)S(1)} %get-tuple-element.23.coords, f32[3,1,8192]{2,1,0:T(1,128)S(1)} %collective-permute-done.2.prev, ...), custom_call_target="tpu_custom_call" | custom-call | tf_op jit(solution)/shard_map/band/pallas_call | solution.py:444
  (5 shorter events, 0.0 us)
Async XLA Ops:
  0.6 0.9 %copy-start = (f32[2,3,8192]{2,0,1:T(2,128)S(1)}, f32[2,3,8192]{2,0,1:T(2,128)}, u32[]{:S(2)}) copy-start(f32[2,3,8192]{2,0,1:T(2,128)} %param.8) | copy-start | bytes 589828
  1.6 0.8 %copy-start.3 = (s32[8192]{0:T(1024)S(1)}, s32[8192]{0:T(1024)}, u32[]{:S(2)}) copy-start(s32[8192]{0:T(1024)} %param.11) | copy-start | bytes 98308
  2.3 0.7 %copy-start.5 = (s32[2,4,64]{2,1,0:T(4,128)S(1)}, s32[2,4,64]{2,1,0:T(4,128)}, u32[]{:S(2)}) copy-start(s32[2,4,64]{2,1,0:T(4,128)} %lists_in.1) | copy-start | bytes 6148
  3.0 0.7 copy-start.6
  3.7 0.7 copy-start.7
  5.4 25.3 %collective-permute-start.1 = (f32[4,2,8192]{2,1,0:T(2,128)S(1)}, f32[4,2,8192]{2,1,0:T(2,128)S(1)}, u32[]{:S(2)}, u32[]{:S(2)}) collective-permute-start(f32[4,2,8192]{2,1,0:T(2,128)S(1)} %get-tuple-element.23.coords), channel_id=1, source_target_pairs={{0,15},{1,0},{2,1},{3,2},{4,3},{5,4},{6,5},{7,6},{8,7},{9,8},{10,9... | collective-permute-start | bytes 786440 | tf_op jit(solution)/shard_map/ppermute | solution.py:396
  13.9 16.7 %collective-permute-start = (f32[4,2,8192]{2,1,0:T(2,128)S(1)}, f32[4,2,8192]{2,1,0:T(2,128)S(1)}, u32[]{:S(2)}, u32[]{:S(2)}) collective-permute-start(f32[4,2,8192]{2,1,0:T(2,128)S(1)} %get-tuple-element.23.coords), channel_id=1, source_target_pairs={{0,1},{1,2},{2,3},{3,4},{4,5},{5,6},{6,7},{7,8},{8,9},{9,10},{10,1... | collective-permute-start | bytes 786440 | tf_op jit(solution)/shard_map/ppermute | solution.py:395
  13.9 16.7 %collective-permute-start.2 = (f32[3,1,8192]{2,1,0:T(1,128)S(1)}, f32[3,1,8192]{2,1,0:T(1,128)S(1)}, u32[]{:S(2)}, u32[]{:S(2)}) collective-permute-start(f32[3,1,8192]{2,1,0:T(1,128)S(1)} %get-tuple-element.29), channel_id=1, source_target_pairs={{0,16},{16,32},{32,48},{48,64},{64,80},{80,96},{96,112},{112,128},... | collective-permute-start | bytes 294920 | tf_op jit(solution)/shard_map/ppermute | solution.py:397
  13.9 16.7 %collective-permute-start.3 = (f32[3,1,8192]{2,1,0:T(1,128)S(1)}, f32[3,1,8192]{2,1,0:T(1,128)S(1)}, u32[]{:S(2)}, u32[]{:S(2)}) collective-permute-start(f32[3,1,8192]{2,1,0:T(1,128)S(1)} %get-tuple-element.30), channel_id=1, source_target_pairs={{0,240},{16,0},{32,16},{48,32},{64,48},{80,64},{96,80},{112,96},{1... | collective-permute-start | bytes 294920 | tf_op jit(solution)/shard_map/ppermute | solution.py:398
  16.6 14.1 %copy-start.1 = (f32[3,8192]{1,0:T(4,128)S(1)}, f32[3,8192]{1,0:T(4,128)}, u32[]{:S(2)}) copy-start(f32[3,8192]{1,0:T(4,128)} %ref.1) | copy-start | bytes 294916
  16.6 14.1 %copy-start.2 = (f32[8192]{0:T(1024)S(1)}, f32[8192]{0:T(1024)}, u32[]{:S(2)}) copy-start(f32[8192]{0:T(1024)} %param.10) | copy-start | bytes 98308
  16.6 14.1 %copy-start.4 = (s32[2,2,1024]{2,1,0:T(2,128)S(1)}, s32[2,2,1024]{2,1,0:T(2,128)}, u32[]{:S(2)}) copy-start(s32[2,2,1024]{2,1,0:T(2,128)} %hidx.1) | copy-start | bytes 49156

commit v4 on v3

--- a/solution.py
+++ b/solution.py
@@ -7,14 +7,14 @@
 
 TILE = 128
 PARTNERS = 4
-UNROLL = 16
+UNROLL = 32
+BUILD = 16
 spring_k = 2.0
 small_eps = 1e-06
 f32, bf16 = jnp.float32, jnp.bfloat16
 GROUPS = ((0, 0), (0, 1), (1, 0), (0, 2), (2, 0), (1, 1))
 VMEM = pl.BlockSpec(memory_space=pltpu.VMEM)
 SMEM = pl.BlockSpec(memory_space=pltpu.SMEM)
-HBM = pl.BlockSpec(memory_space=pltpu.HBM)
 
 
 def lanes(tile):
@@ -115,55 +115,45 @@
     lax.fori_loop(0, steps, step, 0)
 
 
-def prep_kernel(
-    coords_in, types_in, well_in, radius_in, lists_in,
-    feats, first, last, depth, radius, tables, lists, place,
-    types, narrow, sem,
-):
+def table(values):
+    wide = jnp.concatenate([values[...], jnp.zeros_like(values[...])], axis=1)
+    return jnp.broadcast_to(wide, (8, TILE))
+
+
+def prep_kernel(coords_in, types, feats, first, last, place):
     images = feats.shape[1]
-    moves = (
-        (types_in, types), (well_in, narrow.at[0]), (radius_in, narrow.at[1]),
-        (coords_in, feats.at[0:3]), (lists_in, lists),
-    )
-    copies = [pltpu.make_async_copy(src, dst, sem.at[n]) for n, (src, dst) in enumerate(moves)]
-    for copy in copies:
-        copy.start()
     slab, image = lax.axis_index("space"), lax.axis_index("image")
     place[0] = (slab > 0).astype(jnp.int32)
     place[1] = (slab < lax.axis_size("space") - 1).astype(jnp.int32)
     place[2] = (image == 0).astype(jnp.int32)
     place[3] = (image == lax.axis_size("image") - 1).astype(jnp.int32)
-    for copy in copies[:3]:
-        copy.wait()
-    for n in range(2):
-        tables[n : n + 1] = jnp.concatenate([narrow[n], jnp.zeros_like(narrow[n])], axis=1)
-    wells = jnp.broadcast_to(tables[0:1], (8, TILE))
-    radii = jnp.broadcast_to(tables[1:2], (8, TILE))
     for n in range(types.shape[0] // 8):
-        kind = types[8 * n : 8 * n + 8]
-        depth[8 * n : 8 * n + 8] = take(wells, kind)
-        radius[8 * n : 8 * n + 8] = take(radii, kind)
-        kind = kind.astype(f32)
+        kind = types[8 * n : 8 * n + 8].astype(f32)
         for h in range(8):
             t = 8 * n + h
             feats[3, :, t * TILE : (t + 1) * TILE] = jnp.broadcast_to(
                 kind[h : h + 1], (images, TILE)
             )
-    for copy in copies[3:]:
-        copy.wait()
     for c in range(3):
-        first[c] = feats[c, 0:1]
-        last[c] = feats[c, images - 1 : images]
+        rows = coords_in[c]
+        feats[c] = rows
+        first[c] = rows[0:1]
+        last[c] = rows[images - 1 : images]
 
 
 def own_kernel(
-    lists, place, coords, depth_s, radius_s,
-    a, b, p, join, center, order, count,
-    near,
+    lists, place, coords, types, well, radius,
+    a, b, p, join, center, depth_s, order, count,
+    near, radius_s,
 ):
     images = coords.shape[1]
-    own_tiles = depth_s.shape[0]
+    own_tiles = types.shape[0]
     tiles_ext = a.shape[0] // images
+    wells, radii = table(well), table(radius)
+    for n in range(own_tiles // 8):
+        kind = types[8 * n : 8 * n + 8]
+        depth_s[8 * n : 8 * n + 8] = take(wells, kind)
+        radius_s[8 * n : 8 * n + 8] = take(radii, kind)
     for c in range(3):
         total = coords[c, :, 0:TILE]
         for t in range(1, own_tiles):
@@ -179,8 +169,8 @@
         def build(n, carry):
             n_near, n_far = carry
             made = []
-            for h in range(8):
-                t = 8 * n + h
+            for h in range(BUILD):
+                t = BUILD * n + h
                 u = m * own_tiles + t
                 x3 = jnp.concatenate([coords[c, m : m + 1, lanes(t)] for c in range(3)], axis=0)
                 made.append(
@@ -195,10 +185,10 @@
                 order[n_far] = u
                 n_near = n_near + inside
                 n_far = n_far + (1 - inside)
-            store_tiles(a, p, m * tiles_ext + 8 * n, made)
+            store_tiles(a, p, m * tiles_ext + BUILD * n, made)
             return n_near, n_far
 
-        n_near, n_far = lax.fori_loop(0, own_tiles // 8, build, (n_near, n_far))
+        n_near, n_far = lax.fori_loop(0, own_tiles // BUILD, build, (n_near, n_far))
     steps = n_near // UNROLL
 
     def move(n, n_far):
@@ -211,7 +201,7 @@
 
 
 def rest_kernel(
-    lists, place, order, count, coords, below, above, own_depth, tables, hidx, ref, restr, prev, nxt,
+    lists, place, order, count, coords, below, above, own_depth, well, radius, hidx, ref, restr, prev, nxt,
     center, b, a_in, p_in, join_in,
     force, sums, a, p, join,
     halo_x, depth_s, radius_s,
@@ -221,8 +211,7 @@
     tiles_ext = a.shape[0] // images
     halo_tiles = tiles_ext - own_tiles
     side_tiles = halo_tiles // 2
-    wells = jnp.broadcast_to(tables[0:1], (8, TILE))
-    radii = jnp.broadcast_to(tables[1:2], (8, TILE))
+    wells, radii = table(well), table(radius)
 
     for side, source in enumerate((below, above)):
         low, high = [], []
@@ -259,18 +248,18 @@
 
         def build(n, carry):
             made = []
-            for h in range(8):
-                t = 8 * n + h
+            for h in range(BUILD):
+                t = BUILD * n + h
                 x3 = jnp.concatenate([halo_x[m, c, pl.ds(t, 1)] for c in range(3)], axis=0)
                 made.append(
                     streamed_features(
                         x3 - middle, depth_s[m, pl.ds(t, 1)], radius_s[m, pl.ds(t, 1)]
                     )
                 )
-            store_tiles(a, p, m * tiles_ext + own_tiles + 8 * n, made)
+            store_tiles(a, p, m * tiles_ext + own_tiles + BUILD * n, made)
             return carry
 
-        lax.fori_loop(0, halo_tiles // 8, build, 0)
+        lax.fori_loop(0, halo_tiles // BUILD, build, 0)
 
     pair_sums(order, count[0], lists, a, b, p, join, own_tiles, tiles_ext)
 
@@ -366,38 +355,28 @@
     images, _, atoms = coords.shape
     tiles = atoms // TILE
     tiles_ext = tiles + 2 * halo_index.shape[2] // TILE
-    kinds = well_table.shape[0]
-    feats, first, last, depth, radius, tables, lists, place = pl.pallas_call(
+    types = atom_types.reshape(tiles, TILE)
+    well, radius = well_table[None], radius_table[None]
+    feats, first, last, place = pl.pallas_call(
         prep_kernel,
         out_shape=(
             shape((4, images, atoms)),
             shape((3, 1, atoms)),
             shape((3, 1, atoms)),
-            shape((tiles, TILE)),
-            shape((tiles, TILE)),
-            shape((2, TILE)),
-            shape(tile_lists.shape, jnp.int32),
             shape((4,), jnp.int32),
         ),
-        in_specs=[HBM] * 5,
-        out_specs=(VMEM,) * 7 + (SMEM,),
-        scratch_shapes=[
-            pltpu.VMEM((tiles, TILE), jnp.int32),
-            pltpu.VMEM((2, 1, kinds), f32),
-            pltpu.SemaphoreType.DMA((5,)),
-        ],
+        in_specs=[VMEM] * 2,
+        out_specs=(VMEM,) * 3 + (SMEM,),
+        cost_estimate=pl.CostEstimate(flops=10**10, bytes_accessed=10**6, transcendentals=0),
         name="prep",
         **params(8),
-    )(
-        coords.transpose(1, 0, 2), atom_types.reshape(tiles, TILE), well_table[None],
-        radius_table[None], tile_lists,
-    )
+    )(coords.transpose(1, 0, 2), types)
     below = lax.ppermute(feats, "space", ring("space", 1))
     above = lax.ppermute(feats, "space", ring("space", -1))
     prev = lax.ppermute(last, "image", ring("image", 1))
     nxt = lax.ppermute(first, "image", ring("image", -1))
     own = images * tiles
-    a, b, p, join, center, order, count = pl.pallas_call(
+    a, b, p, join, center, depth, order, count = pl.pallas_call(
         own_kernel,
         out_shape=(
             shape((images * tiles_ext, TILE, TILE), bf16),
@@ -405,18 +384,20 @@
             shape((images * tiles_ext, 16, TILE), bf16),
             shape((own, 8, TILE)),
             shape((images, 8, TILE)),
+            shape((tiles, TILE)),
             shape((own,), jnp.int32),
             shape((1,), jnp.int32),
         ),
-        in_specs=[SMEM] * 2 + [VMEM] * 3,
-        out_specs=(VMEM,) * 5 + (SMEM,) * 2,
+        in_specs=[SMEM] * 2 + [VMEM] * 4,
+        out_specs=(VMEM,) * 6 + (SMEM,) * 2,
         scratch_shapes=[
             pltpu.SMEM((own,), jnp.int32),
+            pltpu.VMEM((tiles, TILE), f32),
         ],
         cost_estimate=pl.CostEstimate(flops=60 * 10**9, bytes_accessed=10**6, transcendentals=0),
         name="own",
         **params(16),
-    )(lists, place, feats, depth, radius)
+    )(tile_lists, place, feats, types, well, radius)
     force, sums, *_ = pl.pallas_call(
         rest_kernel,
         out_shape=(
@@ -426,9 +407,9 @@
             shape(p.shape, bf16),
             shape(join.shape),
         ),
-        in_specs=[SMEM] * 4 + [VMEM] * 15,
+        in_specs=[SMEM] * 4 + [VMEM] * 16,
         out_specs=(VMEM,) * 5,
-        input_output_aliases={16: 2, 17: 3, 18: 4},
+        input_output_aliases={17: 2, 18: 3, 19: 4},
         scratch_shapes=[
             pltpu.VMEM((images, 3, tiles_ext - tiles, TILE), f32),
             pltpu.VMEM((images, tiles_ext - tiles, TILE), f32),
@@ -437,7 +418,7 @@
         name="rest",
         **params(16),
     )(
-        lists, place, order, count, feats, below, above, depth, tables, halo_index,
+        tile_lists, place, order, count, feats, below, above, depth, well, radius, halo_index,
         ref_coords, restraint[None], prev, nxt, center, b, a, p, join,
     )
     shares = lax.all_to_all(sums, "space", 0, 0, tiled=True)

time: 68.7 us -> 63.8 us (0.929)
  Pallas kernels: 35.8 us -> 32.7 us
  local copies, waits for them, and re-layouts: 3.68 us -> 1.7 us
    pallas_call x1, Pallas kernels: 14 us -> 10.1 us  [body(): pl.pallas_call(own_kernel, out_shape=(shape((images * tiles_ext, TILE, TI...]
    unnamed x16, local copies, waits for them, and re-layouts: 3.68 us -> 1.7 us
    pallas_call x1, Pallas kernels: 18.9 us -> 20.2 us  [body(): pl.pallas_call(rest_kernel, out_shape=(shape((3, images, atoms)), shape((...]
  transfers between devices with their start and end apart: 4 -> 4, of which waited for: 0 -> 0; matrix products, arithmetic and copies ran while one was open for 0% -> 0% of each run, Pallas kernels for 20% -> 16%
where the time goes in v4:
time: 63.8 us; the launch traced here: 63.5 us
  Pallas kernels  32.7 us (51%)
  blocking collectives  16.9 us (26%)
  starting transfers between devices  11.2 us (18%)
  local copies, waits for them, and re-layouts  1.7 us (3%)
  between operations  0.9 us (1%)
    pallas_call x1, Pallas kernels, body(): pl.pallas_call(rest_kernel, out_shape=(shape((3, images, atoms)), shape((...  20.2 us
    all_to_all x1, blocking collectives, body(): shares = lax.all_to_all(sums, 'space', 0, 0, tiled=True)  16.9 us
    pallas_call x1, Pallas kernels, body(): pl.pallas_call(own_kernel, out_shape=(shape((images * tiles_ext, TILE, TI...  10.1 us
    ppermute x1, starting transfers between devices, body(): above = lax.ppermute(feats, 'space', ring('space', -1))  8.56 us
    ppermute x1, starting transfers between devices, body(): nxt = lax.ppermute(first, 'image', ring('image', -1))  2.64 us
    pallas_call x1, Pallas kernels, body(): pl.pallas_call(band_kernel, out_shape=(shape((3, images, atoms)), shape((...  1.84 us
    unnamed x16, local copies, waits for them, and re-layouts  1.7 us
  transfers between devices with their start and end apart: 4, of which 0 were waited for; matrix products, arithmetic and copies ran while one was open for 0% of the time, Pallas kernels for 16%

profile of v4, /device:TPU:6, one launch (start us, length us, event | category | flops | bytes accessed | tf_op | source)
XLA Modules:
  0.0 63.5 jit_solution(3297717327605361748)
XLA Ops:
  0.6 0.0 copy-start.6
  0.6 0.9 %copy-done.6 = f32[2,3,8192]{2,0,1:T(2,128)S(1)} copy-done((f32[2,3,8192]{2,0,1:T(2,128)S(1)}, f32[2,3,8192]{2,0,1:T(2,128)}, u32[]{:S(2)}) %copy-start.6) | copy-done | bytes 196632
  1.6 0.8 %copy-done.7 = s32[8192]{0:T(1024)S(1)} copy-done((s32[8192]{0:T(1024)S(1)}, s32[8192]{0:T(1024)}, u32[]{:S(2)}) %copy-start.7) | copy-done | bytes 32792
  2.3 0.6 %prep.1 = (f32[4,2,8192]{2,1,0:T(2,128)S(1)}, f32[3,1,8192]{2,1,0:T(1,128)S(1)}, f32[3,1,8192]{2,1,0:T(1,128)S(1)}, s32[4]{0:T(128)S(1)}) custom-call(f32[3,2,8192]{2,1,0:T(2,128)S(1)} %bitcast.17, s32[64,128]{1,0:T(8,128)S(1)} %bitcast.18), custom_call_target="tpu_custom_call" | custom-call | flops 10000000000 | bytes 1000000 | tf_op jit(solution)/shard_map/prep/pallas_call | solution.py:360
  3.0 8.6 %collective-permute-start.1 = (f32[4,2,8192]{2,1,0:T(2,128)S(1)}, f32[4,2,8192]{2,1,0:T(2,128)S(1)}, u32[]{:S(2)}, u32[]{:S(2)}) collective-permute-start(f32[4,2,8192]{2,1,0:T(2,128)S(1)} %get-tuple-element.19.coords), channel_id=1, source_target_pairs={{0,15},{1,0},{2,1},{3,2},{4,3},{5,4},{6,5},{7,6},{8,7},{9,8},{10,9... | collective-permute-start | bytes 786440 | tf_op jit(solution)/shard_map/ppermute | solution.py:375
  11.5 0.0 collective-permute-start
  11.5 0.0 collective-permute-start.2
  11.5 2.6 %collective-permute-start.3 = (f32[3,1,8192]{2,1,0:T(1,128)S(1)}, f32[3,1,8192]{2,1,0:T(1,128)S(1)}, u32[]{:S(2)}, u32[]{:S(2)}) collective-permute-start(f32[3,1,8192]{2,1,0:T(1,128)S(1)} %get-tuple-element.24), channel_id=1, source_target_pairs={{0,240},{16,0},{32,16},{48,32},{64,48},{80,64},{96,80},{112,96},{1... | collective-permute-start | bytes 294920 | tf_op jit(solution)/shard_map/ppermute | solution.py:377
  14.2 0.0 copy-done.3
  14.2 0.0 copy-done.4
  14.2 0.0 copy-done.5
  14.2 0.0 copy-start.1
  14.2 0.0 copy-start.2
  14.2 10.1 %own.1 = (bf16[160,128,128]{2,1,0:T(8,128)(2,1)S(1)}, bf16[128,128,256]{2,1,0:T(8,128)(2,1)S(1)}, bf16[160,16,128]{2,1,0:T(8,128)(2,1)S(1)}, f32[128,8,128]{2,1,...) custom-call(s32[2,4,64]{2,1,0:T(4,128)S(1)} %copy-done.3, ...), custom_call_target="tpu_custom_call" | custom-call | flops 60000002048 | bytes 1000000 | tf_op jit(solution)/shard_map/own/pallas_call | solution.py:379
  24.3 0.0 collective-permute-done.2.prev
  24.3 0.0 collective-permute-done.3.nxt
  24.3 0.0 collective-permute-done.1.above
  24.3 0.0 collective-permute-done.below
  24.4 0.0 copy-done
  24.4 0.0 copy-done.1
  24.4 0.0 copy-done.2
  24.4 20.2 %rest.1 = (f32[3,2,8192]{2,1,0:T(2,128)S(1)}, f32[16,16]{1,0:T(8,128)S(1)}, bf16[160,128,128]{2,1,0:T(8,128)(2,1)S(1)}, bf16[160,16,128]{2,1,0:T(8,128)(2,1)S(1)}, f32[128,8,128]{2,1,0:T(8,128)S(1)}) custom-call(s32[2,4,64]{2,1,0:T(4,128)S(1)} %copy-done.3, ...), custom_call_target="tpu_custom_call", output_to_operand_aliasing={{2}: (17, {}), {3}: (18, {}), {4}: (19, {})} | custom-call | tf_op jit(solution)/shard_map/rest/pallas_call | solution.py:401
  44.6 16.9 %all_to_all.11 = f32[16,1,16]{2,1,0:T(1,128)S(1)} all-to-all(f32[16,1,16]{2,1,0:T(1,128)S(1)} %bitcast.12), channel_id=1, replica_groups=mesh['image'=16,'space'=16] {'space'}, dimensions={0} | all-to-all | bytes 2048 | tf_op jit(solution)/shard_map/all_to_all | solution.py:424
  61.5 1.8 %band.1 = (f32[3,2,8192]{2,1,0:T(2,128)}, f32[2]{0:T(128)}) custom-call(s32[4]{0:T(128)S(1)} %get-tuple-element.18.place, f32[16,16]{1,0:T(8,128)S(1)} %bitcast.11, f32[3,2,8192]{2,1,0:T(2,128)S(1)} %get-tuple-element.31.force, f32[4,2,8192]{2,1,0:T(2,128)S(1)} %get-tuple-element.19.coords, f32[3,1,8192]{2,1,0:T(1,128)S(1)} %collective-permute-done.2.prev, ...), custom_call_target="tpu_custom_call" | custom-call | tf_op jit(solution)/shard_map/band/pallas_call | solution.py:425
  (5 shorter events, 0.0 us)
Async XLA Ops:
  0.6 0.9 %copy-start.6 = (f32[2,3,8192]{2,0,1:T(2,128)S(1)}, f32[2,3,8192]{2,0,1:T(2,128)}, u32[]{:S(2)}) copy-start(f32[2,3,8192]{2,0,1:T(2,128)} %param.8) | copy-start | bytes 589828
  1.6 0.8 %copy-start.7 = (s32[8192]{0:T(1024)S(1)}, s32[8192]{0:T(1024)}, u32[]{:S(2)}) copy-start(s32[8192]{0:T(1024)} %param.11) | copy-start | bytes 98308
  2.3 11.9 %copy-start.3 = (s32[2,4,64]{2,1,0:T(4,128)S(1)}, s32[2,4,64]{2,1,0:T(4,128)}, u32[]{:S(2)}) copy-start(s32[2,4,64]{2,1,0:T(4,128)} %lists.3) | copy-start | bytes 6148
  2.3 11.9 %copy-start.4 = (f32[64]{0:T(128)S(1)}, f32[64]{0:T(128)}, u32[]{:S(2)}) copy-start(f32[64]{0:T(128)} %param.12) | copy-start | bytes 772
  2.3 11.9 %copy-start.5 = (f32[64]{0:T(128)S(1)}, f32[64]{0:T(128)}, u32[]{:S(2)}) copy-start(f32[64]{0:T(128)} %param.13) | copy-start | bytes 772
  3.0 21.4 %collective-permute-start.1 = (f32[4,2,8192]{2,1,0:T(2,128)S(1)}, f32[4,2,8192]{2,1,0:T(2,128)S(1)}, u32[]{:S(2)}, u32[]{:S(2)}) collective-permute-start(f32[4,2,8192]{2,1,0:T(2,128)S(1)} %get-tuple-element.19.coords), channel_id=1, source_target_pairs={{0,15},{1,0},{2,1},{3,2},{4,3},{5,4},{6,5},{7,6},{8,7},{9,8},{10,9... | collective-permute-start | bytes 786440 | tf_op jit(solution)/shard_map/ppermute | solution.py:375
  11.5 12.8 %collective-permute-start = (f32[4,2,8192]{2,1,0:T(2,128)S(1)}, f32[4,2,8192]{2,1,0:T(2,128)S(1)}, u32[]{:S(2)}, u32[]{:S(2)}) collective-permute-start(f32[4,2,8192]{2,1,0:T(2,128)S(1)} %get-tuple-element.19.coords), channel_id=1, source_target_pairs={{0,1},{1,2},{2,3},{3,4},{4,5},{5,6},{6,7},{7,8},{8,9},{9,10},{10,1... | collective-permute-start | bytes 786440 | tf_op jit(solution)/shard_map/ppermute | solution.py:374
  11.5 12.8 %collective-permute-start.2 = (f32[3,1,8192]{2,1,0:T(1,128)S(1)}, f32[3,1,8192]{2,1,0:T(1,128)S(1)}, u32[]{:S(2)}, u32[]{:S(2)}) collective-permute-start(f32[3,1,8192]{2,1,0:T(1,128)S(1)} %get-tuple-element.23), channel_id=1, source_target_pairs={{0,16},{16,32},{32,48},{48,64},{64,80},{80,96},{96,112},{112,128},... | collective-permute-start | bytes 294920 | tf_op jit(solution)/shard_map/ppermute | solution.py:376
  11.5 12.8 %collective-permute-start.3 = (f32[3,1,8192]{2,1,0:T(1,128)S(1)}, f32[3,1,8192]{2,1,0:T(1,128)S(1)}, u32[]{:S(2)}, u32[]{:S(2)}) collective-permute-start(f32[3,1,8192]{2,1,0:T(1,128)S(1)} %get-tuple-element.24), channel_id=1, source_target_pairs={{0,240},{16,0},{32,16},{48,32},{64,48},{80,64},{96,80},{112,96},{1... | collective-permute-start | bytes 294920 | tf_op jit(solution)/shard_map/ppermute | solution.py:377
  14.2 10.2 %copy-start = (f32[3,8192]{1,0:T(4,128)S(1)}, f32[3,8192]{1,0:T(4,128)}, u32[]{:S(2)}) copy-start(f32[3,8192]{1,0:T(4,128)} %ref.1) | copy-start | bytes 294916
  14.2 10.2 %copy-start.1 = (f32[8192]{0:T(1024)S(1)}, f32[8192]{0:T(1024)}, u32[]{:S(2)}) copy-start(f32[8192]{0:T(1024)} %param.10) | copy-start | bytes 98308
  14.2 10.2 %copy-start.2 = (s32[2,2,1024]{2,1,0:T(2,128)S(1)}, s32[2,2,1024]{2,1,0:T(2,128)}, u32[]{:S(2)}) copy-start(s32[2,2,1024]{2,1,0:T(2,128)} %hidx.1) | copy-start | bytes 49156

commit v5 on v4

--- a/solution.py
+++ b/solution.py
@@ -299,11 +299,11 @@
     row, lane = rows_of((16, 16)), lax.broadcasted_iota(jnp.int32, (16, 16), 1)
     totals = jnp.sum(line, axis=1, keepdims=True)
     totals = jnp.sum(jnp.where(row == lane, totals, 0.0), axis=0, keepdims=True)
-    sums[...] = jnp.broadcast_to(totals, (16, 16))
+    sums[...] = totals
 
 
 def band_kernel(place, shares, force, coords, prev, nxt, out, energies):
-    total = jnp.sum(shares[...], axis=0, keepdims=True)
+    total = shares[...]
     images, atoms = coords.shape[1], coords.shape[2]
     parts = []
     for m in range(images):
@@ -402,7 +402,7 @@
         rest_kernel,
         out_shape=(
             shape((3, images, atoms)),
-            shape((16, 16)),
+            shape((1, 16)),
             shape(a.shape, bf16),
             shape(p.shape, bf16),
             shape(join.shape),
@@ -421,7 +421,13 @@
         tile_lists, place, order, count, feats, below, above, depth, well, radius, halo_index,
         ref_coords, restraint[None], prev, nxt, center, b, a, p, join,
     )
-    shares = lax.all_to_all(sums, "space", 0, 0, tiled=True)
+    shares = sums
+    for stride in (1, 4):
+        parts = [
+            lax.ppermute(shares, "space", [(i, i ^ (stride * d)) for i in range(16)])
+            for d in (1, 2, 3)
+        ]
+        shares = shares + (parts[0] + parts[1] + parts[2])
     out, energies = pl.pallas_call(
         band_kernel,
         out_shape=(shape((3, images, atoms)), shape((images,))),

time: 63.8 us -> 67.7 us (1.061)
  the two profiles are of different devices: /device:TPU:6 before, /device:TPU:32 now
where the time goes in v5:
time: 67.7 us; the launch traced here: 67.5 us
  Pallas kernels  32.8 us (48%)
  starting transfers between devices  24.6 us (36%)
  waiting for transfers between devices  7.55 us (11%)
  local copies, waits for them, and re-layouts  1.7 us (3%)
  between operations  0.91 us (1%)
    pallas_call x1, Pallas kernels, body(): pl.pallas_call(rest_kernel, out_shape=(shape((3, images, atoms)), shape((...  20.2 us
    ppermute x6, starting transfers between devices, body(): lax.ppermute(shares, 'space', [(i, i ^ stride * d) for i in range(16)])  17.1 us
    pallas_call x1, Pallas kernels, body(): pl.pallas_call(own_kernel, out_shape=(shape((images * tiles_ext, TILE, TI...  10.1 us
    ppermute x6, waiting for transfers between devices, body(): lax.ppermute(shares, 'space', [(i, i ^ stride * d) for i in range(16)])  7.54 us
    ppermute x1, starting transfers between devices, body(): nxt = lax.ppermute(first, 'image', ring('image', -1))  3.85 us
    ppermute x1, starting transfers between devices, body(): above = lax.ppermute(feats, 'space', ring('space', -1))  2.82 us
    pallas_call x1, Pallas kernels, body(): pl.pallas_call(band_kernel, out_shape=(shape((3, images, atoms)), shape((...  1.84 us
    unnamed x16, local copies, waits for them, and re-layouts  1.7 us
  transfers between devices with their start and end apart: 10, of which 2 were waited for; matrix products, arithmetic and copies ran while one was open for 0% of the time, Pallas kernels for 15%

profile of v5, /device:TPU:32, one launch (start us, length us, event | category | flops | bytes accessed | tf_op | source)
XLA Modules:
  0.0 67.5 jit_solution(15021544952596807434)
XLA Ops:
  0.6 0.9 %copy-done.6 = f32[2,3,8192]{2,0,1:T(2,128)S(1)} copy-done((f32[2,3,8192]{2,0,1:T(2,128)S(1)}, f32[2,3,8192]{2,0,1:T(2,128)}, u32[]{:S(2)}) %copy-start.6) | copy-done | bytes 196632
  1.6 0.8 %copy-done.7 = s32[8192]{0:T(1024)S(1)} copy-done((s32[8192]{0:T(1024)S(1)}, s32[8192]{0:T(1024)}, u32[]{:S(2)}) %copy-start.7) | copy-done | bytes 32792
  2.3 0.6 prep.1
  3.0 2.8 %collective-permute-start.1 = (f32[4,2,8192]{2,1,0:T(2,128)S(1)}, f32[4,2,8192]{2,1,0:T(2,128)S(1)}, u32[]{:S(2)}, u32[]{:S(2)}) collective-permute-start(f32[4,2,8192]{2,1,0:T(2,128)S(1)} %get-tuple-element.19.coords), channel_id=1, source_target_pairs={{0,15},{1,0},{2,1},{3,2},{4,3},{5,4},{6,5},{7,6},{8,7},{9,8},{10,9... | collective-permute-start | bytes 786440 | tf_op jit(solution)/shard_map/ppermute | solution.py:375
  5.8 0.8 %collective-permute-start = (f32[4,2,8192]{2,1,0:T(2,128)S(1)}, f32[4,2,8192]{2,1,0:T(2,128)S(1)}, u32[]{:S(2)}, u32[]{:S(2)}) collective-permute-start(f32[4,2,8192]{2,1,0:T(2,128)S(1)} %get-tuple-element.19.coords), channel_id=1, source_target_pairs={{0,1},{1,2},{2,3},{3,4},{4,5},{5,6},{6,7},{7,8},{8,9},{9,10},{10,1... | collective-permute-start | bytes 786440 | tf_op jit(solution)/shard_map/ppermute | solution.py:374
  6.6 0.0 collective-permute-start.2
  6.6 3.9 %collective-permute-start.3 = (f32[3,1,8192]{2,1,0:T(1,128)S(1)}, f32[3,1,8192]{2,1,0:T(1,128)S(1)}, u32[]{:S(2)}, u32[]{:S(2)}) collective-permute-start(f32[3,1,8192]{2,1,0:T(1,128)S(1)} %get-tuple-element.24), channel_id=1, source_target_pairs={{0,240},{16,0},{32,16},{48,32},{64,48},{80,64},{96,80},{112,96},{1... | collective-permute-start | bytes 294920 | tf_op jit(solution)/shard_map/ppermute | solution.py:377
  10.4 0.0 copy-start.1
  10.5 0.0 copy-start.2
  10.5 10.1 %own.1 = (bf16[160,128,128]{2,1,0:T(8,128)(2,1)S(1)}, bf16[128,128,256]{2,1,0:T(8,128)(2,1)S(1)}, bf16[160,16,128]{2,1,0:T(8,128)(2,1)S(1)}, f32[128,8,128]{2,1,...) custom-call(s32[2,4,64]{2,1,0:T(4,128)S(1)} %copy-done.3, ...), custom_call_target="tpu_custom_call" | custom-call | flops 60000002048 | bytes 1000000 | tf_op jit(solution)/shard_map/own/pallas_call | solution.py:379
  20.6 0.0 collective-permute-done.2.prev
  20.6 0.0 collective-permute-done.3.nxt
  20.7 0.0 collective-permute-done.below
  20.7 20.2 %rest.1 = (f32[3,2,8192]{2,1,0:T(2,128)S(1)}, f32[1,16]{1,0:T(1,128)S(1)}, bf16[160,128,128]{2,1,0:T(8,128)(2,1)S(1)}, bf16[160,16,128]{2,1,0:T(8,128)(2,1)S(1)}, f32[128,8,128]{2,1,0:T(8,128)S(1)}) custom-call(s32[2,4,64]{2,1,0:T(4,128)S(1)} %copy-done.3, ...), custom_call_target="tpu_custom_call", output_to_operand_aliasing={{2}: (17, {}), {3}: (18, {}), {4}: (19, {})} | custom-call | tf_op jit(solution)/shard_map/rest/pallas_call | solution.py:401
  40.9 3.6 %collective-permute-start.6 = (f32[1,16]{1,0:T(1,128)S(1)}, f32[1,16]{1,0:T(1,128)S(1)}, u32[]{:S(2)}, u32[]{:S(2)}) collective-permute-start(f32[1,16]{1,0:T(1,128)S(1)} %get-tuple-element.30), channel_id=1, source_target_pairs={{0,3},{1,2},{2,1},{3,0},{4,7},{5,6},{6,5},{7,4},{8,11},{9,10},{10,... | collective-permute-start | bytes 200 | tf_op jit(solution)/shard_map/ppermute | solution.py:427
  44.5 1.9 %collective-permute-start.5 = (f32[1,16]{1,0:T(1,128)S(1)}, f32[1,16]{1,0:T(1,128)S(1)}, u32[]{:S(2)}, u32[]{:S(2)}) collective-permute-start(f32[1,16]{1,0:T(1,128)S(1)} %get-tuple-element.30), channel_id=1, source_target_pairs={{0,2},{1,3},{2,0},{3,1},{4,6},{5,7},{6,4},{7,5},{8,10},{9,11},{10,... | collective-permute-start | bytes 200 | tf_op jit(solution)/shard_map/ppermute | solution.py:427
  46.4 2.5 %collective-permute-start.4 = (f32[1,16]{1,0:T(1,128)S(1)}, f32[1,16]{1,0:T(1,128)S(1)}, u32[]{:S(2)}, u32[]{:S(2)}) collective-permute-start(f32[1,16]{1,0:T(1,128)S(1)} %get-tuple-element.30), channel_id=1, source_target_pairs={{0,1},{1,0},{2,3},{3,2},{4,5},{5,4},{6,7},{7,6},{8,9},{9,8},{10,11... | collective-permute-start | bytes 200 | tf_op jit(solution)/shard_map/ppermute | solution.py:427
  48.9 2.5 %collective-permute-done.4 = f32[1,16]{1,0:T(1,128)S(1)} collective-permute-done((f32[1,16]{1,0:T(1,128)S(1)}, f32[1,16]{1,0:T(1,128)S(1)}, u32[]{:S(2)}, u32[]{:S(2)}) %collective-permute-start.4) | collective-permute-done | bytes 96 | tf_op jit(solution)/shard_map/ppermute | solution.py:427
  51.4 6.6 %collective-permute-start.9 = (f32[1,16]{1,0:T(1,128)S(1)}, f32[1,16]{1,0:T(1,128)S(1)}, u32[]{:S(2)}, u32[]{:S(2)}) collective-permute-start(f32[1,16]{1,0:T(1,128)S(1)} %add_add_fusion.1), channel_id=1, source_target_pairs={{0,12},{1,13},{2,14},{3,15},{4,8},{5,9},{6,10},{7,11},{8,4},{9,5},... | collective-permute-start | bytes 200 | tf_op jit(solution)/shard_map/ppermute | solution.py:427
  58.1 1.5 %collective-permute-start.8 = (f32[1,16]{1,0:T(1,128)S(1)}, f32[1,16]{1,0:T(1,128)S(1)}, u32[]{:S(2)}, u32[]{:S(2)}) collective-permute-start(f32[1,16]{1,0:T(1,128)S(1)} %add_add_fusion.1), channel_id=1, source_target_pairs={{0,8},{1,9},{2,10},{3,11},{4,12},{5,13},{6,14},{7,15},{8,0},{9,1},... | collective-permute-start | bytes 200 | tf_op jit(solution)/shard_map/ppermute | solution.py:427
  59.6 0.9 %collective-permute-start.7 = (f32[1,16]{1,0:T(1,128)S(1)}, f32[1,16]{1,0:T(1,128)S(1)}, u32[]{:S(2)}, u32[]{:S(2)}) collective-permute-start(f32[1,16]{1,0:T(1,128)S(1)} %add_add_fusion.1), channel_id=1, source_target_pairs={{0,4},{1,5},{2,6},{3,7},{4,0},{5,1},{6,2},{7,3},{8,12},{9,13},{10,... | collective-permute-start | bytes 200 | tf_op jit(solution)/shard_map/ppermute | solution.py:427
  60.5 0.0 collective-permute-done.9
  60.5 5.0 %collective-permute-done.8 = f32[1,16]{1,0:T(1,128)S(1)} collective-permute-done((f32[1,16]{1,0:T(1,128)S(1)}, f32[1,16]{1,0:T(1,128)S(1)}, u32[]{:S(2)}, u32[]{:S(2)}) %collective-permute-start.8) | collective-permute-done | bytes 96 | tf_op jit(solution)/shard_map/ppermute | solution.py:427
  65.5 1.8 %band.1 = (f32[3,2,8192]{2,1,0:T(2,128)}, f32[2]{0:T(128)}) custom-call(s32[4]{0:T(128)S(1)} %get-tuple-element.18.place, f32[1,16]{1,0:T(1,128)S(1)} %add_add_fusion.shares, f32[3,2,8192]{2,1,0:T(2,128)S(1)} %get-tuple-element.31.force, f32[4,2,8192]{2,1,0:T(2,128)S(1)} %get-tuple-element.19.coords, f32[3,1,8192]{2,1,0:T(1,128)S(1)} %collective-permute-done.2.prev, ...), custom_call_target="tpu_custom_call" | custom-call | tf_op jit(solution)/shard_map/band/pallas_call | solution.py:431
  (18 shorter events, 0.0 us)
Async XLA Ops:
  0.6 0.9 %copy-start.6 = (f32[2,3,8192]{2,0,1:T(2,128)S(1)}, f32[2,3,8192]{2,0,1:T(2,128)}, u32[]{:S(2)}) copy-start(f32[2,3,8192]{2,0,1:T(2,128)} %param.8) | copy-start | bytes 589828
  1.6 0.8 %copy-start.7 = (s32[8192]{0:T(1024)S(1)}, s32[8192]{0:T(1024)}, u32[]{:S(2)}) copy-start(s32[8192]{0:T(1024)} %param.11) | copy-start | bytes 98308
  2.3 8.1 %copy-start.3 = (s32[2,4,64]{2,1,0:T(4,128)S(1)}, s32[2,4,64]{2,1,0:T(4,128)}, u32[]{:S(2)}) copy-start(s32[2,4,64]{2,1,0:T(4,128)} %lists.3) | copy-start | bytes 6148
  2.3 8.1 %copy-start.4 = (f32[64]{0:T(128)S(1)}, f32[64]{0:T(128)}, u32[]{:S(2)}) copy-start(f32[64]{0:T(128)} %param.12) | copy-start | bytes 772
  2.3 8.1 %copy-start.5 = (f32[64]{0:T(128)S(1)}, f32[64]{0:T(128)}, u32[]{:S(2)}) copy-start(f32[64]{0:T(128)} %param.13) | copy-start | bytes 772
  3.0 17.7 %collective-permute-start.1 = (f32[4,2,8192]{2,1,0:T(2,128)S(1)}, f32[4,2,8192]{2,1,0:T(2,128)S(1)}, u32[]{:S(2)}, u32[]{:S(2)}) collective-permute-start(f32[4,2,8192]{2,1,0:T(2,128)S(1)} %get-tuple-element.19.coords), channel_id=1, source_target_pairs={{0,15},{1,0},{2,1},{3,2},{4,3},{5,4},{6,5},{7,6},{8,7},{9,8},{10,9... | collective-permute-start | bytes 786440 | tf_op jit(solution)/shard_map/ppermute | solution.py:375
  5.8 14.9 %collective-permute-start = (f32[4,2,8192]{2,1,0:T(2,128)S(1)}, f32[4,2,8192]{2,1,0:T(2,128)S(1)}, u32[]{:S(2)}, u32[]{:S(2)}) collective-permute-start(f32[4,2,8192]{2,1,0:T(2,128)S(1)} %get-tuple-element.19.coords), channel_id=1, source_target_pairs={{0,1},{1,2},{2,3},{3,4},{4,5},{5,6},{6,7},{7,8},{8,9},{9,10},{10,1... | collective-permute-start | bytes 786440 | tf_op jit(solution)/shard_map/ppermute | solution.py:374
  6.6 14.1 %collective-permute-start.2 = (f32[3,1,8192]{2,1,0:T(1,128)S(1)}, f32[3,1,8192]{2,1,0:T(1,128)S(1)}, u32[]{:S(2)}, u32[]{:S(2)}) collective-permute-start(f32[3,1,8192]{2,1,0:T(1,128)S(1)} %get-tuple-element.23), channel_id=1, source_target_pairs={{0,16},{16,32},{32,48},{48,64},{64,80},{80,96},{96,112},{112,128},... | collective-permute-start | bytes 294920 | tf_op jit(solution)/shard_map/ppermute | solution.py:376
  6.6 14.1 %collective-permute-start.3 = (f32[3,1,8192]{2,1,0:T(1,128)S(1)}, f32[3,1,8192]{2,1,0:T(1,128)S(1)}, u32[]{:S(2)}, u32[]{:S(2)}) collective-permute-start(f32[3,1,8192]{2,1,0:T(1,128)S(1)} %get-tuple-element.24), channel_id=1, source_target_pairs={{0,240},{16,0},{32,16},{48,32},{64,48},{80,64},{96,80},{112,96},{1... | collective-permute-start | bytes 294920 | tf_op jit(solution)/shard_map/ppermute | solution.py:377
  10.4 10.2 %copy-start = (f32[3,8192]{1,0:T(4,128)S(1)}, f32[3,8192]{1,0:T(4,128)}, u32[]{:S(2)}) copy-start(f32[3,8192]{1,0:T(4,128)} %ref.1) | copy-start | bytes 294916
  10.4 10.2 %copy-start.1 = (f32[8192]{0:T(1024)S(1)}, f32[8192]{0:T(1024)}, u32[]{:S(2)}) copy-start(f32[8192]{0:T(1024)} %param.10) | copy-start | bytes 98308
  10.5 10.2 %copy-start.2 = (s32[2,2,1024]{2,1,0:T(2,128)S(1)}, s32[2,2,1024]{2,1,0:T(2,128)}, u32[]{:S(2)}) copy-start(s32[2,2,1024]{2,1,0:T(2,128)} %hidx.1) | copy-start | bytes 49156
  40.9 8.0 %collective-permute-start.6 = (f32[1,16]{1,0:T(1,128)S(1)}, f32[1,16]{1,0:T(1,128)S(1)}, u32[]{:S(2)}, u32[]{:S(2)}) collective-permute-start(f32[1,16]{1,0:T(1,128)S(1)} %get-tuple-element.30), channel_id=1, source_target_pairs={{0,3},{1,2},{2,1},{3,0},{4,7},{5,6},{6,5},{7,4},{8,11},{9,10},{10,... | collective-permute-start | bytes 200 | tf_op jit(solution)/shard_map/ppermute | solution.py:427
  44.5 4.4 %collective-permute-start.5 = (f32[1,16]{1,0:T(1,128)S(1)}, f32[1,16]{1,0:T(1,128)S(1)}, u32[]{:S(2)}, u32[]{:S(2)}) collective-permute-start(f32[1,16]{1,0:T(1,128)S(1)} %get-tuple-element.30), channel_id=1, source_target_pairs={{0,2},{1,3},{2,0},{3,1},{4,6},{5,7},{6,4},{7,5},{8,10},{9,11},{10,... | collective-permute-start | bytes 200 | tf_op jit(solution)/shard_map/ppermute | solution.py:427
  46.4 5.0 %collective-permute-start.4 = (f32[1,16]{1,0:T(1,128)S(1)}, f32[1,16]{1,0:T(1,128)S(1)}, u32[]{:S(2)}, u32[]{:S(2)}) collective-permute-start(f32[1,16]{1,0:T(1,128)S(1)} %get-tuple-element.30), channel_id=1, source_target_pairs={{0,1},{1,0},{2,3},{3,2},{4,5},{5,4},{6,7},{7,6},{8,9},{9,8},{10,11... | collective-permute-start | bytes 200 | tf_op jit(solution)/shard_map/ppermute | solution.py:427
  51.4 9.1 %collective-permute-start.9 = (f32[1,16]{1,0:T(1,128)S(1)}, f32[1,16]{1,0:T(1,128)S(1)}, u32[]{:S(2)}, u32[]{:S(2)}) collective-permute-start(f32[1,16]{1,0:T(1,128)S(1)} %add_add_fusion.1), channel_id=1, source_target_pairs={{0,12},{1,13},{2,14},{3,15},{4,8},{5,9},{6,10},{7,11},{8,4},{9,5},... | collective-permute-start | bytes 200 | tf_op jit(solution)/shard_map/ppermute | solution.py:427
  58.1 7.4 %collective-permute-start.8 = (f32[1,16]{1,0:T(1,128)S(1)}, f32[1,16]{1,0:T(1,128)S(1)}, u32[]{:S(2)}, u32[]{:S(2)}) collective-permute-start(f32[1,16]{1,0:T(1,128)S(1)} %add_add_fusion.1), channel_id=1, source_target_pairs={{0,8},{1,9},{2,10},{3,11},{4,12},{5,13},{6,14},{7,15},{8,0},{9,1},... | collective-permute-start | bytes 200 | tf_op jit(solution)/shard_map/ppermute | solution.py:427
  59.6 5.9 %collective-permute-start.7 = (f32[1,16]{1,0:T(1,128)S(1)}, f32[1,16]{1,0:T(1,128)S(1)}, u32[]{:S(2)}, u32[]{:S(2)}) collective-permute-start(f32[1,16]{1,0:T(1,128)S(1)} %add_add_fusion.1), channel_id=1, source_target_pairs={{0,4},{1,5},{2,6},{3,7},{4,0},{5,1},{6,2},{7,3},{8,12},{9,13},{10,... | collective-permute-start | bytes 200 | tf_op jit(solution)/shard_map/ppermute | solution.py:427

commit v6 on v4

--- a/solution.py
+++ b/solution.py
@@ -40,7 +40,7 @@
     cut = pieces(jnp.concatenate([x3, radius, norm, norm, rr, rr], axis=0))
     ones = [jnp.where((row == 5) | (row == 7), 1.0, c) for c in cut]
     streamed = jnp.concatenate([ones[a] for a, _ in GROUPS], axis=0).astype(bf16)
-    streamed = jnp.concatenate([streamed, jnp.zeros((80, TILE), bf16)], axis=0)
+    streamed = jnp.concatenate([streamed, jnp.zeros((16, TILE), bf16)], axis=0)
     moved = jnp.concatenate([depth, depth * x3], axis=0)
     p1, p2, p3 = pieces(jnp.concatenate([moved, moved], axis=0))
     weights = jnp.concatenate(
@@ -61,18 +61,22 @@
         reach = cut[b] * scale_r + jnp.where(row == 6, other, 0.0)
         blocks.append(jnp.concatenate([dist, reach], axis=1))
     held = jnp.concatenate(blocks, axis=0).astype(bf16)
-    return jnp.concatenate([held, jnp.zeros((80, 2 * TILE), bf16)], axis=0)
+    rest = jnp.zeros((16, 2 * TILE), bf16)
+    return jnp.concatenate([held, rest, held, rest], axis=0)
 
 
 def store_tiles(a_out, p_out, first, made):
     eye = (rows_of((TILE, TILE)) == lax.broadcasted_iota(jnp.int32, (TILE, TILE), 1)).astype(bf16)
-    for n in range(0, len(made), 2):
-        pair = jnp.concatenate([made[n][1], made[n + 1][1]], axis=0)
+    upper = lax.broadcasted_iota(jnp.int32, (TILE, TILE), 1) >= TILE // 2
+    for n in range(0, len(made), 4):
+        four = jnp.concatenate([made[n + h][1] for h in range(4)], axis=0)
         turned = lax.dot_general(
-            eye, pair, (((1,), (1,)), ((), ())), preferred_element_type=f32
-        ).astype(bf16)
-        for h in range(2):
-            a_out[first + n + h] = turned[:, h * TILE : (h + 1) * TILE]
+            eye, four, (((1,), (1,)), ((), ())), preferred_element_type=f32
+        )
+        for h in range(4):
+            block = turned[:, (h // 2) * TILE : (h // 2 + 1) * TILE]
+            block = jnp.where(upper, block, 0.0) if h % 2 else jnp.where(upper, 0.0, block)
+            a_out[first + n + h] = block.astype(bf16)
             p_out[first + n + h] = made[n + h][2]
 
 
@@ -203,7 +207,7 @@
 def rest_kernel(
     lists, place, order, count, coords, below, above, own_depth, well, radius, hidx, ref, restr, prev, nxt,
     center, b, a_in, p_in, join_in,
-    force, sums, a, p, join,
+    force, slope, bending, sums, a, p, join,
     halo_x, depth_s, radius_s,
 ):
     images = coords.shape[1]
@@ -265,8 +269,8 @@
 
     def finish(n, carry):
         carry = list(carry)
-        for h in range(4):
-            t = 4 * n + h
+        for h in range(8):
+            t = 8 * n + h
             at = lanes(t)
             depth = own_depth[pl.ds(t, 1)]
             stiff = restr[:, at]
@@ -285,6 +289,8 @@
                 after = jnp.concatenate([x[1:2], nxt[c, :, at]], axis=0)
                 ahead, behind = after - x, x - before
                 both_ways, bend = ahead + behind, ahead - behind
+                slope[c, :, at] = both_ways
+                bending[c, :, at] = bend
                 carry[0] += both_ways * both_ways
                 carry[1] += both_ways * bend
                 carry[2] += bend * bend
@@ -294,7 +300,7 @@
         return tuple(carry)
 
     zero = jnp.zeros((images, TILE), f32)
-    line = lax.fori_loop(0, own_tiles // 4, finish, (zero,) * 6)
+    line = lax.fori_loop(0, own_tiles // 8, finish, (zero,) * 6)
     line = jnp.concatenate(list(line) + [jnp.zeros((16 - 6 * images, TILE), f32)], axis=0)
     row, lane = rows_of((16, 16)), lax.broadcasted_iota(jnp.int32, (16, 16), 1)
     totals = jnp.sum(line, axis=1, keepdims=True)
@@ -302,9 +308,9 @@
     sums[...] = jnp.broadcast_to(totals, (16, 16))
 
 
-def band_kernel(place, shares, force, coords, prev, nxt, out, energies):
+def band_kernel(place, shares, force, slope, bending, out, energies):
     total = jnp.sum(shares[...], axis=0, keepdims=True)
-    images, atoms = coords.shape[1], coords.shape[2]
+    images, atoms = force.shape[1], force.shape[2]
     parts = []
     for m in range(images):
         s_sq, cross, b_sq, f_s, f_b, energy = [
@@ -329,11 +335,7 @@
     for t in range(atoms // TILE):
         at = slice(t * TILE, (t + 1) * TILE)
         for c in range(3):
-            x = coords[c, :, at]
-            before = jnp.concatenate([prev[c, :, at], x[0:1]], axis=0)
-            after = jnp.concatenate([x[1:2], nxt[c, :, at]], axis=0)
-            ahead, behind = after - x, x - before
-            out[c, :, at] = force[c, :, at] + for_s * (ahead + behind) + for_b * (ahead - behind)
+            out[c, :, at] = force[c, :, at] + for_s * slope[c, :, at] + for_b * bending[c, :, at]
 
 
 def ring(axis, step):
@@ -398,9 +400,11 @@
         name="own",
         **params(16),
     )(tile_lists, place, feats, types, well, radius)
-    force, sums, *_ = pl.pallas_call(
+    force, slope, bending, sums, *_ = pl.pallas_call(
         rest_kernel,
         out_shape=(
+            shape((3, images, atoms)),
+            shape((3, images, atoms)),
             shape((3, images, atoms)),
             shape((16, 16)),
             shape(a.shape, bf16),
@@ -408,8 +412,8 @@
             shape(join.shape),
         ),
         in_specs=[SMEM] * 4 + [VMEM] * 16,
-        out_specs=(VMEM,) * 5,
-        input_output_aliases={17: 2, 18: 3, 19: 4},
+        out_specs=(VMEM,) * 7,
+        input_output_aliases={17: 4, 18: 5, 19: 6},
         scratch_shapes=[
             pltpu.VMEM((images, 3, tiles_ext - tiles, TILE), f32),
             pltpu.VMEM((images, tiles_ext - tiles, TILE), f32),
@@ -425,11 +429,11 @@
     out, energies = pl.pallas_call(
         band_kernel,
         out_shape=(shape((3, images, atoms)), shape((images,))),
-        in_specs=[SMEM] + [VMEM] * 5,
+        in_specs=[SMEM] + [VMEM] * 4,
         out_specs=(VMEM, SMEM),
         name="band",
         **params(8),
-    )(place, shares, force, feats, prev, nxt)
+    )(place, shares, force, slope, bending)
     return out.transpose(1, 0, 2), energies
 
 

time: 63.8 us -> 63.5 us (level)
  no operation moved by 1% of the time
where the time goes in v6:
time: 63.5 us; the launch traced here: 63.3 us
  Pallas kernels  32.4 us (51%)
  blocking collectives  17.1 us (27%)
  starting transfers between devices  11.2 us (18%)
  local copies, waits for them, and re-layouts  1.7 us (3%)
  between operations  0.9 us (1%)
    pallas_call x1, Pallas kernels, body(): pl.pallas_call(rest_kernel, out_shape=(shape((3, images, atoms)), shape((...  20.1 us
    all_to_all x1, blocking collectives, body(): shares = lax.all_to_all(sums, 'space', 0, 0, tiled=True)  17.1 us
    pallas_call x1, Pallas kernels, body(): pl.pallas_call(own_kernel, out_shape=(shape((images * tiles_ext, TILE, TI...  9.94 us
    ppermute x1, starting transfers between devices, body(): above = lax.ppermute(feats, 'space', ring('space', -1))  8.56 us
    ppermute x1, starting transfers between devices, body(): nxt = lax.ppermute(first, 'image', ring('image', -1))  2.64 us
    pallas_call x1, Pallas kernels, body(): pl.pallas_call(band_kernel, out_shape=(shape((3, images, atoms)), shape((...  1.76 us
    unnamed x16, local copies, waits for them, and re-layouts  1.7 us
  transfers between devices with their start and end apart: 4, of which 0 were waited for; matrix products, arithmetic and copies ran while one was open for 0% of the time, Pallas kernels for 16%

profile of v6, /device:TPU:6, one launch (start us, length us, event | category | flops | bytes accessed | tf_op | source)
XLA Modules:
  0.0 63.3 jit_solution(7532175848764872244)
XLA Ops:
  0.6 0.0 copy-start.6
  0.6 0.9 %copy-done.6 = f32[2,3,8192]{2,0,1:T(2,128)S(1)} copy-done((f32[2,3,8192]{2,0,1:T(2,128)S(1)}, f32[2,3,8192]{2,0,1:T(2,128)}, u32[]{:S(2)}) %copy-start.6) | copy-done | bytes 196632
  1.6 0.8 %copy-done.7 = s32[8192]{0:T(1024)S(1)} copy-done((s32[8192]{0:T(1024)S(1)}, s32[8192]{0:T(1024)}, u32[]{:S(2)}) %copy-start.7) | copy-done | bytes 32792
  2.3 0.6 %prep.1 = (f32[4,2,8192]{2,1,0:T(2,128)S(1)}, f32[3,1,8192]{2,1,0:T(1,128)S(1)}, f32[3,1,8192]{2,1,0:T(1,128)S(1)}, s32[4]{0:T(128)S(1)}) custom-call(f32[3,2,8192]{2,1,0:T(2,128)S(1)} %bitcast.17, s32[64,128]{1,0:T(8,128)S(1)} %bitcast.18), custom_call_target="tpu_custom_call" | custom-call | flops 10000000000 | bytes 1000000 | tf_op jit(solution)/shard_map/prep/pallas_call | solution.py:362
  3.0 8.6 %collective-permute-start.1 = (f32[4,2,8192]{2,1,0:T(2,128)S(1)}, f32[4,2,8192]{2,1,0:T(2,128)S(1)}, u32[]{:S(2)}, u32[]{:S(2)}) collective-permute-start(f32[4,2,8192]{2,1,0:T(2,128)S(1)} %get-tuple-element.21.coords), channel_id=1, source_target_pairs={{0,15},{1,0},{2,1},{3,2},{4,3},{5,4},{6,5},{7,6},{8,7},{9,8},{10,9... | collective-permute-start | bytes 786440 | tf_op jit(solution)/shard_map/ppermute | solution.py:377
  11.5 0.0 collective-permute-start
  11.5 0.0 collective-permute-start.2
  11.5 2.6 %collective-permute-start.3 = (f32[3,1,8192]{2,1,0:T(1,128)S(1)}, f32[3,1,8192]{2,1,0:T(1,128)S(1)}, u32[]{:S(2)}, u32[]{:S(2)}) collective-permute-start(f32[3,1,8192]{2,1,0:T(1,128)S(1)} %get-tuple-element.26), channel_id=1, source_target_pairs={{0,240},{16,0},{32,16},{48,32},{64,48},{80,64},{96,80},{112,96},{1... | collective-permute-start | bytes 294920 | tf_op jit(solution)/shard_map/ppermute | solution.py:379
  14.2 0.0 copy-done.3
  14.2 0.0 copy-done.4
  14.2 0.0 copy-done.5
  14.2 0.0 copy-start.1
  14.2 0.0 copy-start.2
  14.2 9.9 %own.1 = (bf16[160,128,128]{2,1,0:T(8,128)(2,1)S(1)}, bf16[128,128,256]{2,1,0:T(8,128)(2,1)S(1)}, bf16[160,16,128]{2,1,0:T(8,128)(2,1)S(1)}, f32[128,8,128]{2,1,...) custom-call(s32[2,4,64]{2,1,0:T(4,128)S(1)} %copy-done.3, ...), custom_call_target="tpu_custom_call" | custom-call | flops 60000002048 | bytes 1000000 | tf_op jit(solution)/shard_map/own/pallas_call | solution.py:381
  24.2 0.0 collective-permute-done.2.prev
  24.2 0.0 collective-permute-done.3.nxt
  24.2 0.0 collective-permute-done.1.above
  24.2 0.0 collective-permute-done.below
  24.2 0.0 copy-done
  24.2 0.0 copy-done.1
  24.2 0.0 copy-done.2
  24.2 20.1 %rest.1 = (f32[3,2,8192]{2,1,0:T(2,128)S(1)}, f32[3,2,8192]{2,1,0:T(2,128)S(1)}, f32[3,2,8192]{2,1,0:T(2,128)S(1)}, f32[16,16]{1,0:T(8,128)S(1)}, bf16[160,128,1...) custom-call(s32[2,4,64]{2,1,0:T(4,128)S(1)} %copy-done.3, ...), custom_call_target="tpu_custom_call", output_to_operand_aliasing={{4}: (17, {}), {5}: (18, {}), {6}: (19, {})} | custom-call | tf_op jit(solution)/shard_map/rest/pallas_call | solution.py:403
  44.3 17.1 %all_to_all.11 = f32[16,1,16]{2,1,0:T(1,128)S(1)} all-to-all(f32[16,1,16]{2,1,0:T(1,128)S(1)} %bitcast.12), channel_id=1, replica_groups=mesh['image'=16,'space'=16] {'space'}, dimensions={0} | all-to-all | bytes 2048 | tf_op jit(solution)/shard_map/all_to_all | solution.py:428
  61.4 1.8 %band.1 = (f32[3,2,8192]{2,1,0:T(2,128)}, f32[2]{0:T(128)}) custom-call(s32[4]{0:T(128)S(1)} %get-tuple-element.20.place, f32[16,16]{1,0:T(8,128)S(1)} %bitcast.11, f32[3,2,8192]{2,1,0:T(2,128)S(1)} %get-tuple-element.33.force, f32[3,2,8192]{2,1,0:T(2,128)S(1)} %get-tuple-element.34.slope, f32[3,2,8192]{2,1,0:T(2,128)S(1)} %get-tuple-element.35.bending), custom_call_target="tpu_custom_call" | custom-call | tf_op jit(solution)/shard_map/band/pallas_call | solution.py:429
  (5 shorter events, 0.0 us)
Async XLA Ops:
  0.6 0.9 %copy-start.6 = (f32[2,3,8192]{2,0,1:T(2,128)S(1)}, f32[2,3,8192]{2,0,1:T(2,128)}, u32[]{:S(2)}) copy-start(f32[2,3,8192]{2,0,1:T(2,128)} %param.8) | copy-start | bytes 589828
  1.6 0.8 %copy-start.7 = (s32[8192]{0:T(1024)S(1)}, s32[8192]{0:T(1024)}, u32[]{:S(2)}) copy-start(s32[8192]{0:T(1024)} %param.11) | copy-start | bytes 98308
  2.3 11.9 %copy-start.3 = (s32[2,4,64]{2,1,0:T(4,128)S(1)}, s32[2,4,64]{2,1,0:T(4,128)}, u32[]{:S(2)}) copy-start(s32[2,4,64]{2,1,0:T(4,128)} %lists.3) | copy-start | bytes 6148
  2.3 11.9 %copy-start.4 = (f32[64]{0:T(128)S(1)}, f32[64]{0:T(128)}, u32[]{:S(2)}) copy-start(f32[64]{0:T(128)} %param.12) | copy-start | bytes 772
  2.3 11.9 %copy-start.5 = (f32[64]{0:T(128)S(1)}, f32[64]{0:T(128)}, u32[]{:S(2)}) copy-start(f32[64]{0:T(128)} %param.13) | copy-start | bytes 772
  3.0 21.2 %collective-permute-start.1 = (f32[4,2,8192]{2,1,0:T(2,128)S(1)}, f32[4,2,8192]{2,1,0:T(2,128)S(1)}, u32[]{:S(2)}, u32[]{:S(2)}) collective-permute-start(f32[4,2,8192]{2,1,0:T(2,128)S(1)} %get-tuple-element.21.coords), channel_id=1, source_target_pairs={{0,15},{1,0},{2,1},{3,2},{4,3},{5,4},{6,5},{7,6},{8,7},{9,8},{10,9... | collective-permute-start | bytes 786440 | tf_op jit(solution)/shard_map/ppermute | solution.py:377
  11.5 12.7 %collective-permute-start = (f32[4,2,8192]{2,1,0:T(2,128)S(1)}, f32[4,2,8192]{2,1,0:T(2,128)S(1)}, u32[]{:S(2)}, u32[]{:S(2)}) collective-permute-start(f32[4,2,8192]{2,1,0:T(2,128)S(1)} %get-tuple-element.21.coords), channel_id=1, source_target_pairs={{0,1},{1,2},{2,3},{3,4},{4,5},{5,6},{6,7},{7,8},{8,9},{9,10},{10,1... | collective-permute-start | bytes 786440 | tf_op jit(solution)/shard_map/ppermute | solution.py:376
  11.5 12.6 %collective-permute-start.2 = (f32[3,1,8192]{2,1,0:T(1,128)S(1)}, f32[3,1,8192]{2,1,0:T(1,128)S(1)}, u32[]{:S(2)}, u32[]{:S(2)}) collective-permute-start(f32[3,1,8192]{2,1,0:T(1,128)S(1)} %get-tuple-element.25), channel_id=1, source_target_pairs={{0,16},{16,32},{32,48},{48,64},{64,80},{80,96},{96,112},{112,128},... | collective-permute-start | bytes 294920 | tf_op jit(solution)/shard_map/ppermute | solution.py:378
  11.5 12.6 %collective-permute-start.3 = (f32[3,1,8192]{2,1,0:T(1,128)S(1)}, f32[3,1,8192]{2,1,0:T(1,128)S(1)}, u32[]{:S(2)}, u32[]{:S(2)}) collective-permute-start(f32[3,1,8192]{2,1,0:T(1,128)S(1)} %get-tuple-element.26), channel_id=1, source_target_pairs={{0,240},{16,0},{32,16},{48,32},{64,48},{80,64},{96,80},{112,96},{1... | collective-permute-start | bytes 294920 | tf_op jit(solution)/shard_map/ppermute | solution.py:379
  14.2 10.0 %copy-start = (f32[3,8192]{1,0:T(4,128)S(1)}, f32[3,8192]{1,0:T(4,128)}, u32[]{:S(2)}) copy-start(f32[3,8192]{1,0:T(4,128)} %ref.1) | copy-start | bytes 294916
  14.2 10.0 %copy-start.1 = (f32[8192]{0:T(1024)S(1)}, f32[8192]{0:T(1024)}, u32[]{:S(2)}) copy-start(f32[8192]{0:T(1024)} %param.10) | copy-start | bytes 98308
  14.2 10.0 %copy-start.2 = (s32[2,2,1024]{2,1,0:T(2,128)S(1)}, s32[2,2,1024]{2,1,0:T(2,128)}, u32[]{:S(2)}) copy-start(s32[2,2,1024]{2,1,0:T(2,128)} %hidx.1) | copy-start | bytes 49156

commit v7 on v6

--- a/solution.py
+++ b/solution.py
@@ -7,7 +7,7 @@
 
 TILE = 128
 PARTNERS = 4
-UNROLL = 32
+BLOCK = 16
 BUILD = 16
 spring_k = 2.0
 small_eps = 1e-06
@@ -32,21 +32,26 @@
     return lax.broadcasted_iota(jnp.int32, shape, 0)
 
 
-def streamed_features(x3, depth, radius):
+def streamed_features(x, y, z, depth, radius):
     row = rows_of((8, TILE))
-    squares = x3 * x3
     rr = radius * radius
-    norm = squares[0:1] + squares[1:2] + squares[2:3] + rr
-    cut = pieces(jnp.concatenate([x3, radius, norm, norm, rr, rr], axis=0))
+    norm = x * x + y * y + z * z + rr
+    base = jnp.where(row == 3, radius, jnp.where(row < 6, norm, rr))
+    cut = pieces(jnp.where(row == 0, x, jnp.where(row == 1, y, jnp.where(row == 2, z, base))))
     ones = [jnp.where((row == 5) | (row == 7), 1.0, c) for c in cut]
     streamed = jnp.concatenate([ones[a] for a, _ in GROUPS], axis=0).astype(bf16)
     streamed = jnp.concatenate([streamed, jnp.zeros((16, TILE), bf16)], axis=0)
-    moved = jnp.concatenate([depth, depth * x3], axis=0)
-    p1, p2, p3 = pieces(jnp.concatenate([moved, moved], axis=0))
+    quarter = row & 3
+    moved = jnp.where(quarter == 0, 1.0, jnp.where(quarter == 1, x, jnp.where(quarter == 2, y, z)))
+    p1, p2, p3 = pieces(depth * moved)
     weights = jnp.concatenate(
         [jnp.where(row < 4, p1, p2), jnp.where(row < 4, p3, 0.0)], axis=0
     ).astype(bf16)
     return cut, streamed, weights
+
+
+def repeated(row):
+    return jnp.broadcast_to(row, (8, TILE))
 
 
 def held_features(cut):
@@ -84,10 +89,10 @@
     return jnp.take_along_axis(src, idx, axis=1, mode="promise_in_bounds")
 
 
-def pair_sums(order, steps, lists, a, b, p, join, own_tiles, tiles_ext):
-    def step(n, carry):
-        for h in range(UNROLL):
-            u = order[n * UNROLL + h]
+def pair_sums(order, blocks, lists, a, b, p, join, own_tiles, tiles_ext):
+    def step(first, tiles, carry):
+        for h in range(tiles):
+            u = order[first + h]
             m = u // own_tiles
             t = u - m * own_tiles
             held = b[u]
@@ -116,7 +121,9 @@
             join[u] = jnp.concatenate([joined[:, :TILE], joined[:, TILE:]], axis=0)
         return carry
 
-    lax.fori_loop(0, steps, step, 0)
+    pairs = blocks // 2
+    lax.fori_loop(0, pairs, lambda n, c: step(n * (2 * BLOCK), 2 * BLOCK, c), 0)
+    lax.fori_loop(2 * pairs, blocks, lambda n, c: step(n * BLOCK, BLOCK, c), 0)
 
 
 def table(values):
@@ -168,7 +175,7 @@
 
     n_near, n_far = jnp.int32(0), jnp.int32(0)
     for m in range(images):
-        middle = center[m, 0:3]
+        middle = [repeated(center[m, c : c + 1]) for c in range(3)]
 
         def build(n, carry):
             n_near, n_far = carry
@@ -176,9 +183,11 @@
             for h in range(BUILD):
                 t = BUILD * n + h
                 u = m * own_tiles + t
-                x3 = jnp.concatenate([coords[c, m : m + 1, lanes(t)] for c in range(3)], axis=0)
+                xyz = [repeated(coords[c, m : m + 1, lanes(t)]) - middle[c] for c in range(3)]
                 made.append(
-                    streamed_features(x3 - middle, depth_s[pl.ds(t, 1)], radius_s[pl.ds(t, 1)])
+                    streamed_features(
+                        *xyz, repeated(depth_s[pl.ds(t, 1)]), repeated(radius_s[pl.ds(t, 1)])
+                    )
                 )
                 b[u] = held_features(made[-1][0])
                 last = lists[m, 0, t]
@@ -193,15 +202,15 @@
             return n_near, n_far
 
         n_near, n_far = lax.fori_loop(0, own_tiles // BUILD, build, (n_near, n_far))
-    steps = n_near // UNROLL
+    blocks = n_near // BLOCK
 
     def move(n, n_far):
         order[n_far] = near[n]
         return n_far + 1
 
-    n_far = lax.fori_loop(steps * UNROLL, n_near, move, n_far)
-    count[0] = n_far // UNROLL
-    pair_sums(near, steps, lists, a, b, p, join, own_tiles, tiles_ext)
+    n_far = lax.fori_loop(blocks * BLOCK, n_near, move, n_far)
+    count[0] = n_far // BLOCK
+    pair_sums(near, blocks, lists, a, b, p, join, own_tiles, tiles_ext)
 
 
 def rest_kernel(
@@ -248,16 +257,16 @@
             radius_s[m, spot] = take(radii, kind)
 
     for m in range(images):
-        middle = center[m, 0:3]
+        middle = [repeated(center[m, c : c + 1]) for c in range(3)]
 
         def build(n, carry):
             made = []
             for h in range(BUILD):
                 t = BUILD * n + h
-                x3 = jnp.concatenate([halo_x[m, c, pl.ds(t, 1)] for c in range(3)], axis=0)
+                xyz = [repeated(halo_x[m, c, pl.ds(t, 1)]) - middle[c] for c in range(3)]
                 made.append(
                     streamed_features(
-                        x3 - middle, depth_s[m, pl.ds(t, 1)], radius_s[m, pl.ds(t, 1)]
+                        *xyz, repeated(depth_s[m, pl.ds(t, 1)]), repeated(radius_s[m, pl.ds(t, 1)])
                     )
                 )
             store_tiles(a, p, m * tiles_ext + own_tiles + BUILD * n, made)

time: 63.5 us -> 63.5 us (level)
    pallas_call x1, Pallas kernels: 9.94 us -> 12.2 us  [body(): pl.pallas_call(own_kernel, out_shape=(shape((images * tiles_ext, TILE, TI...]
    pallas_call x1, Pallas kernels: 20.1 us -> 17.8 us  [body(): pl.pallas_call(rest_kernel, out_shape=(shape((3, images, atoms)), shape((...]
  transfers between devices with their start and end apart: 4 -> 4, of which waited for: 0 -> 0; matrix products, arithmetic and copies ran while one was open for 0% -> 0% of each run, Pallas kernels for 16% -> 19%
where the time goes in v7:
time: 63.5 us; the launch traced here: 63.3 us
  Pallas kernels  32.5 us (51%)
  blocking collectives  17 us (27%)
  starting transfers between devices  11.2 us (18%)
  local copies, waits for them, and re-layouts  1.7 us (3%)
  between operations  0.9 us (1%)
    pallas_call x1, Pallas kernels, body(): pl.pallas_call(rest_kernel, out_shape=(shape((3, images, atoms)), shape((...  17.8 us
    all_to_all x1, blocking collectives, body(): shares = lax.all_to_all(sums, 'space', 0, 0, tiled=True)  17 us
    pallas_call x1, Pallas kernels, body(): pl.pallas_call(own_kernel, out_shape=(shape((images * tiles_ext, TILE, TI...  12.2 us
    ppermute x1, starting transfers between devices, body(): above = lax.ppermute(feats, 'space', ring('space', -1))  8.56 us
    ppermute x1, starting transfers between devices, body(): nxt = lax.ppermute(first, 'image', ring('image', -1))  2.64 us
    pallas_call x1, Pallas kernels, body(): pl.pallas_call(band_kernel, out_shape=(shape((3, images, atoms)), shape((...  1.76 us
    unnamed x16, local copies, waits for them, and re-layouts  1.7 us
  transfers between devices with their start and end apart: 4, of which 0 were waited for; matrix products, arithmetic and copies ran while one was open for 0% of the time, Pallas kernels for 19%

profile of v7, /device:TPU:6, one launch (start us, length us, event | category | flops | bytes accessed | tf_op | source)
XLA Modules:
  0.0 63.3 jit_solution(13322882364825588750)
XLA Ops:
  0.6 0.0 copy-start.6
  0.6 0.9 %copy-done.6 = f32[2,3,8192]{2,0,1:T(2,128)S(1)} copy-done((f32[2,3,8192]{2,0,1:T(2,128)S(1)}, f32[2,3,8192]{2,0,1:T(2,128)}, u32[]{:S(2)}) %copy-start.6) | copy-done | bytes 196632
  1.6 0.8 %copy-done.7 = s32[8192]{0:T(1024)S(1)} copy-done((s32[8192]{0:T(1024)S(1)}, s32[8192]{0:T(1024)}, u32[]{:S(2)}) %copy-start.7) | copy-done | bytes 32792
  2.3 0.6 %prep.1 = (f32[4,2,8192]{2,1,0:T(2,128)S(1)}, f32[3,1,8192]{2,1,0:T(1,128)S(1)}, f32[3,1,8192]{2,1,0:T(1,128)S(1)}, s32[4]{0:T(128)S(1)}) custom-call(f32[3,2,8192]{2,1,0:T(2,128)S(1)} %bitcast.17, s32[64,128]{1,0:T(8,128)S(1)} %bitcast.18), custom_call_target="tpu_custom_call" | custom-call | flops 10000000000 | bytes 1000000 | tf_op jit(solution)/shard_map/prep/pallas_call | solution.py:371
  3.0 8.6 %collective-permute-start.1 = (f32[4,2,8192]{2,1,0:T(2,128)S(1)}, f32[4,2,8192]{2,1,0:T(2,128)S(1)}, u32[]{:S(2)}, u32[]{:S(2)}) collective-permute-start(f32[4,2,8192]{2,1,0:T(2,128)S(1)} %get-tuple-element.21.coords), channel_id=1, source_target_pairs={{0,15},{1,0},{2,1},{3,2},{4,3},{5,4},{6,5},{7,6},{8,7},{9,8},{10,9... | collective-permute-start | bytes 786440 | tf_op jit(solution)/shard_map/ppermute | solution.py:386
  11.5 0.0 collective-permute-start
  11.5 0.0 collective-permute-start.2
  11.5 2.6 %collective-permute-start.3 = (f32[3,1,8192]{2,1,0:T(1,128)S(1)}, f32[3,1,8192]{2,1,0:T(1,128)S(1)}, u32[]{:S(2)}, u32[]{:S(2)}) collective-permute-start(f32[3,1,8192]{2,1,0:T(1,128)S(1)} %get-tuple-element.26), channel_id=1, source_target_pairs={{0,240},{16,0},{32,16},{48,32},{64,48},{80,64},{96,80},{112,96},{1... | collective-permute-start | bytes 294920 | tf_op jit(solution)/shard_map/ppermute | solution.py:388
  14.2 0.0 copy-done.3
  14.2 0.0 copy-done.4
  14.2 0.0 copy-done.5
  14.2 0.0 copy-start.1
  14.2 0.0 copy-start.2
  14.2 12.2 %own.1 = (bf16[160,128,128]{2,1,0:T(8,128)(2,1)S(1)}, bf16[128,128,256]{2,1,0:T(8,128)(2,1)S(1)}, bf16[160,16,128]{2,1,0:T(8,128)(2,1)S(1)}, f32[128,8,128]{2,1,...) custom-call(s32[2,4,64]{2,1,0:T(4,128)S(1)} %copy-done.3, ...), custom_call_target="tpu_custom_call" | custom-call | flops 60000002048 | bytes 1000000 | tf_op jit(solution)/shard_map/own/pallas_call | solution.py:390
  26.5 0.0 collective-permute-done.2.prev
  26.5 0.0 collective-permute-done.3.nxt
  26.5 0.0 collective-permute-done.1.above
  26.5 0.0 collective-permute-done.below
  26.5 0.0 copy-done
  26.5 0.0 copy-done.1
  26.5 0.0 copy-done.2
  26.5 17.8 %rest.1 = (f32[3,2,8192]{2,1,0:T(2,128)S(1)}, f32[3,2,8192]{2,1,0:T(2,128)S(1)}, f32[3,2,8192]{2,1,0:T(2,128)S(1)}, f32[16,16]{1,0:T(8,128)S(1)}, bf16[160,128,1...) custom-call(s32[2,4,64]{2,1,0:T(4,128)S(1)} %copy-done.3, ...), custom_call_target="tpu_custom_call", output_to_operand_aliasing={{4}: (17, {}), {5}: (18, {}), {6}: (19, {})} | custom-call | tf_op jit(solution)/shard_map/rest/pallas_call | solution.py:412
  44.4 17.0 %all_to_all.11 = f32[16,1,16]{2,1,0:T(1,128)S(1)} all-to-all(f32[16,1,16]{2,1,0:T(1,128)S(1)} %bitcast.12), channel_id=1, replica_groups=mesh['image'=16,'space'=16] {'space'}, dimensions={0} | all-to-all | bytes 2048 | tf_op jit(solution)/shard_map/all_to_all | solution.py:437
  61.4 1.8 %band.1 = (f32[3,2,8192]{2,1,0:T(2,128)}, f32[2]{0:T(128)}) custom-call(s32[4]{0:T(128)S(1)} %get-tuple-element.20.place, f32[16,16]{1,0:T(8,128)S(1)} %bitcast.11, f32[3,2,8192]{2,1,0:T(2,128)S(1)} %get-tuple-element.33.force, f32[3,2,8192]{2,1,0:T(2,128)S(1)} %get-tuple-element.34.slope, f32[3,2,8192]{2,1,0:T(2,128)S(1)} %get-tuple-element.35.bending), custom_call_target="tpu_custom_call" | custom-call | tf_op jit(solution)/shard_map/band/pallas_call | solution.py:438
  (5 shorter events, 0.0 us)
Async XLA Ops:
  0.6 0.9 %copy-start.6 = (f32[2,3,8192]{2,0,1:T(2,128)S(1)}, f32[2,3,8192]{2,0,1:T(2,128)}, u32[]{:S(2)}) copy-start(f32[2,3,8192]{2,0,1:T(2,128)} %param.8) | copy-start | bytes 589828
  1.6 0.8 %copy-start.7 = (s32[8192]{0:T(1024)S(1)}, s32[8192]{0:T(1024)}, u32[]{:S(2)}) copy-start(s32[8192]{0:T(1024)} %param.11) | copy-start | bytes 98308
  2.3 11.9 %copy-start.3 = (s32[2,4,64]{2,1,0:T(4,128)S(1)}, s32[2,4,64]{2,1,0:T(4,128)}, u32[]{:S(2)}) copy-start(s32[2,4,64]{2,1,0:T(4,128)} %lists.3) | copy-start | bytes 6148
  2.3 11.9 %copy-start.4 = (f32[64]{0:T(128)S(1)}, f32[64]{0:T(128)}, u32[]{:S(2)}) copy-start(f32[64]{0:T(128)} %param.12) | copy-start | bytes 772
  2.3 11.9 %copy-start.5 = (f32[64]{0:T(128)S(1)}, f32[64]{0:T(128)}, u32[]{:S(2)}) copy-start(f32[64]{0:T(128)} %param.13) | copy-start | bytes 772
  3.0 23.5 %collective-permute-start.1 = (f32[4,2,8192]{2,1,0:T(2,128)S(1)}, f32[4,2,8192]{2,1,0:T(2,128)S(1)}, u32[]{:S(2)}, u32[]{:S(2)}) collective-permute-start(f32[4,2,8192]{2,1,0:T(2,128)S(1)} %get-tuple-element.21.coords), channel_id=1, source_target_pairs={{0,15},{1,0},{2,1},{3,2},{4,3},{5,4},{6,5},{7,6},{8,7},{9,8},{10,9... | collective-permute-start | bytes 786440 | tf_op jit(solution)/shard_map/ppermute | solution.py:386
  11.5 15.0 %collective-permute-start = (f32[4,2,8192]{2,1,0:T(2,128)S(1)}, f32[4,2,8192]{2,1,0:T(2,128)S(1)}, u32[]{:S(2)}, u32[]{:S(2)}) collective-permute-start(f32[4,2,8192]{2,1,0:T(2,128)S(1)} %get-tuple-element.21.coords), channel_id=1, source_target_pairs={{0,1},{1,2},{2,3},{3,4},{4,5},{5,6},{6,7},{7,8},{8,9},{9,10},{10,1... | collective-permute-start | bytes 786440 | tf_op jit(solution)/shard_map/ppermute | solution.py:385
  11.5 14.9 %collective-permute-start.2 = (f32[3,1,8192]{2,1,0:T(1,128)S(1)}, f32[3,1,8192]{2,1,0:T(1,128)S(1)}, u32[]{:S(2)}, u32[]{:S(2)}) collective-permute-start(f32[3,1,8192]{2,1,0:T(1,128)S(1)} %get-tuple-element.25), channel_id=1, source_target_pairs={{0,16},{16,32},{32,48},{48,64},{64,80},{80,96},{96,112},{112,128},... | collective-permute-start | bytes 294920 | tf_op jit(solution)/shard_map/ppermute | solution.py:387
  11.5 14.9 %collective-permute-start.3 = (f32[3,1,8192]{2,1,0:T(1,128)S(1)}, f32[3,1,8192]{2,1,0:T(1,128)S(1)}, u32[]{:S(2)}, u32[]{:S(2)}) collective-permute-start(f32[3,1,8192]{2,1,0:T(1,128)S(1)} %get-tuple-element.26), channel_id=1, source_target_pairs={{0,240},{16,0},{32,16},{48,32},{64,48},{80,64},{96,80},{112,96},{1... | collective-permute-start | bytes 294920 | tf_op jit(solution)/shard_map/ppermute | solution.py:388
  14.2 12.3 %copy-start = (f32[3,8192]{1,0:T(4,128)S(1)}, f32[3,8192]{1,0:T(4,128)}, u32[]{:S(2)}) copy-start(f32[3,8192]{1,0:T(4,128)} %ref.1) | copy-start | bytes 294916
  14.2 12.3 %copy-start.1 = (f32[8192]{0:T(1024)S(1)}, f32[8192]{0:T(1024)}, u32[]{:S(2)}) copy-start(f32[8192]{0:T(1024)} %param.10) | copy-start | bytes 98308
  14.2 12.3 %copy-start.2 = (s32[2,2,1024]{2,1,0:T(2,128)S(1)}, s32[2,2,1024]{2,1,0:T(2,128)}, u32[]{:S(2)}) copy-start(s32[2,2,1024]{2,1,0:T(2,128)} %hidx.1) | copy-start | bytes 49156

commit v8 on v7

--- a/solution.py
+++ b/solution.py
@@ -9,6 +9,7 @@
 PARTNERS = 4
 BLOCK = 16
 BUILD = 16
+OWN_BUILD = 32
 spring_k = 2.0
 small_eps = 1e-06
 f32, bf16 = jnp.float32, jnp.bfloat16
@@ -180,8 +181,8 @@
         def build(n, carry):
             n_near, n_far = carry
             made = []
-            for h in range(BUILD):
-                t = BUILD * n + h
+            for h in range(OWN_BUILD):
+                t = OWN_BUILD * n + h
                 u = m * own_tiles + t
                 xyz = [repeated(coords[c, m : m + 1, lanes(t)]) - middle[c] for c in range(3)]
                 made.append(
@@ -198,10 +199,10 @@
                 order[n_far] = u
                 n_near = n_near + inside
                 n_far = n_far + (1 - inside)
-            store_tiles(a, p, m * tiles_ext + BUILD * n, made)
+            store_tiles(a, p, m * tiles_ext + OWN_BUILD * n, made)
             return n_near, n_far
 
-        n_near, n_far = lax.fori_loop(0, own_tiles // BUILD, build, (n_near, n_far))
+        n_near, n_far = lax.fori_loop(0, own_tiles // OWN_BUILD, build, (n_near, n_far))
     blocks = n_near // BLOCK
 
     def move(n, n_far):
@@ -226,35 +227,35 @@
     side_tiles = halo_tiles // 2
     wells, radii = table(well), table(radius)
 
-    for side, source in enumerate((below, above)):
-        low, high = [], []
-        for m in range(images):
-            idx = jnp.concatenate(
-                [hidx[m, side : side + 1, q * TILE : (q + 1) * TILE] for q in range(side_tiles)],
-                axis=0,
-            )
-            low.append(idx & (TILE - 1))
-            high.append(idx >> 7)
-
-        def gather_row(r, carry):
-            out = []
-            for m in range(images):
-                hit = high[m] == r
-                for c in range(4):
-                    wide = jnp.broadcast_to(source[c, m : m + 1, lanes(r)], (8, TILE))
-                    out.append(jnp.where(hit, take(wide, low[m]), carry[4 * m + c]))
-            return tuple(out)
-
-        zero = jnp.zeros((8, TILE), f32)
-        found = lax.fori_loop(0, own_tiles, gather_row, (zero,) * (4 * images), unroll=8)
-        inside = place[side].astype(f32)
+    wanted = [(side, m) for side in range(2) for m in range(images)]
+    low, high = [], []
+    for side, m in wanted:
+        idx = jnp.concatenate(
+            [hidx[m, side : side + 1, q * TILE : (q + 1) * TILE] for q in range(side_tiles)],
+            axis=0,
+        )
+        low.append(idx & (TILE - 1))
+        high.append(idx >> 7)
+
+    def gather_row(r, carry):
+        out = []
+        for n, (side, m) in enumerate(wanted):
+            source = above if side else below
+            hit = high[n] == r
+            for c in range(4):
+                wide = jnp.broadcast_to(source[c, m : m + 1, lanes(r)], (8, TILE))
+                out.append(jnp.where(hit, take(wide, low[n]), carry[4 * n + c]))
+        return tuple(out)
+
+    zero = jnp.zeros((8, TILE), f32)
+    found = lax.fori_loop(0, own_tiles, gather_row, (zero,) * (8 * images), unroll=16)
+    for n, (side, m) in enumerate(wanted):
         spot = slice(side * side_tiles, (side + 1) * side_tiles)
-        for m in range(images):
-            for c in range(3):
-                halo_x[m, c, spot] = found[4 * m + c]
-            kind = found[4 * m + 3].astype(jnp.int32)
-            depth_s[m, spot] = take(wells, kind) * inside
-            radius_s[m, spot] = take(radii, kind)
+        for c in range(3):
+            halo_x[m, c, spot] = found[4 * n + c]
+        kind = found[4 * n + 3].astype(jnp.int32)
+        depth_s[m, spot] = take(wells, kind) * place[side].astype(f32)
+        radius_s[m, spot] = take(radii, kind)
 
     for m in range(images):
         middle = [repeated(center[m, c : c + 1]) for c in range(3)]
@@ -278,8 +279,8 @@
 
     def finish(n, carry):
         carry = list(carry)
-        for h in range(8):
-            t = 8 * n + h
+        for h in range(16):
+            t = 16 * n + h
             at = lanes(t)
             depth = own_depth[pl.ds(t, 1)]
             stiff = restr[:, at]
@@ -309,7 +310,7 @@
         return tuple(carry)
 
     zero = jnp.zeros((images, TILE), f32)
-    line = lax.fori_loop(0, own_tiles // 8, finish, (zero,) * 6)
+    line = lax.fori_loop(0, own_tiles // 16, finish, (zero,) * 6)
     line = jnp.concatenate(list(line) + [jnp.zeros((16 - 6 * images, TILE), f32)], axis=0)
     row, lane = rows_of((16, 16)), lax.broadcasted_iota(jnp.int32, (16, 16), 1)
     totals = jnp.sum(line, axis=1, keepdims=True)

time: 63.5 us -> 62.4 us (0.983)
  Pallas kernels: 32.5 us -> 31.1 us
    pallas_call x1, Pallas kernels: 12.2 us -> 9.61 us  [body(): pl.pallas_call(own_kernel, out_shape=(shape((images * tiles_ext, TILE, TI...]
    pallas_call x1, Pallas kernels: 17.8 us -> 19.1 us  [body(): pl.pallas_call(rest_kernel, out_shape=(shape((3, images, atoms)), shape((...]
  transfers between devices with their start and end apart: 4 -> 4, of which waited for: 0 -> 0; matrix products, arithmetic and copies ran while one was open for 0% -> 0% of each run, Pallas kernels for 19% -> 15%
where the time goes in v8:
time: 62.4 us; the launch traced here: 62 us
  Pallas kernels  31.1 us (50%)
  blocking collectives  17.1 us (27%)
  starting transfers between devices  11.2 us (18%)
  local copies, waits for them, and re-layouts  1.7 us (3%)
  between operations  0.9 us (1%)
    pallas_call x1, Pallas kernels, body(): pl.pallas_call(rest_kernel, out_shape=(shape((3, images, atoms)), shape((...  19.1 us
    all_to_all x1, blocking collectives, body(): shares = lax.all_to_all(sums, 'space', 0, 0, tiled=True)  17.1 us
    pallas_call x1, Pallas kernels, body(): pl.pallas_call(own_kernel, out_shape=(shape((images * tiles_ext, TILE, TI...  9.61 us
    ppermute x1, starting transfers between devices, body(): above = lax.ppermute(feats, 'space', ring('space', -1))  8.56 us
    ppermute x1, starting transfers between devices, body(): nxt = lax.ppermute(first, 'image', ring('image', -1))  2.64 us
    pallas_call x1, Pallas kernels, body(): pl.pallas_call(band_kernel, out_shape=(shape((3, images, atoms)), shape((...  1.76 us
    unnamed x16, local copies, waits for them, and re-layouts  1.7 us
  transfers between devices with their start and end apart: 4, of which 0 were waited for; matrix products, arithmetic and copies ran while one was open for 0% of the time, Pallas kernels for 15%

profile of v8, /device:TPU:6, one launch (start us, length us, event | category | flops | bytes accessed | tf_op | source)
XLA Modules:
  0.0 62.0 jit_solution(6625417914554097030)
XLA Ops:
  0.6 0.0 copy-start.6
  0.6 0.9 %copy-done.6 = f32[2,3,8192]{2,0,1:T(2,128)S(1)} copy-done((f32[2,3,8192]{2,0,1:T(2,128)S(1)}, f32[2,3,8192]{2,0,1:T(2,128)}, u32[]{:S(2)}) %copy-start.6) | copy-done | bytes 196632
  1.6 0.8 %copy-done.7 = s32[8192]{0:T(1024)S(1)} copy-done((s32[8192]{0:T(1024)S(1)}, s32[8192]{0:T(1024)}, u32[]{:S(2)}) %copy-start.7) | copy-done | bytes 32792
  2.3 0.6 %prep.1 = (f32[4,2,8192]{2,1,0:T(2,128)S(1)}, f32[3,1,8192]{2,1,0:T(1,128)S(1)}, f32[3,1,8192]{2,1,0:T(1,128)S(1)}, s32[4]{0:T(128)S(1)}) custom-call(f32[3,2,8192]{2,1,0:T(2,128)S(1)} %bitcast.17, s32[64,128]{1,0:T(8,128)S(1)} %bitcast.18), custom_call_target="tpu_custom_call" | custom-call | flops 10000000000 | bytes 1000000 | tf_op jit(solution)/shard_map/prep/pallas_call | solution.py:372
  3.0 8.6 %collective-permute-start.1 = (f32[4,2,8192]{2,1,0:T(2,128)S(1)}, f32[4,2,8192]{2,1,0:T(2,128)S(1)}, u32[]{:S(2)}, u32[]{:S(2)}) collective-permute-start(f32[4,2,8192]{2,1,0:T(2,128)S(1)} %get-tuple-element.21.coords), channel_id=1, source_target_pairs={{0,15},{1,0},{2,1},{3,2},{4,3},{5,4},{6,5},{7,6},{8,7},{9,8},{10,9... | collective-permute-start | bytes 786440 | tf_op jit(solution)/shard_map/ppermute | solution.py:387
  11.5 0.0 collective-permute-start
  11.5 0.0 collective-permute-start.2
  11.5 2.6 %collective-permute-start.3 = (f32[3,1,8192]{2,1,0:T(1,128)S(1)}, f32[3,1,8192]{2,1,0:T(1,128)S(1)}, u32[]{:S(2)}, u32[]{:S(2)}) collective-permute-start(f32[3,1,8192]{2,1,0:T(1,128)S(1)} %get-tuple-element.26), channel_id=1, source_target_pairs={{0,240},{16,0},{32,16},{48,32},{64,48},{80,64},{96,80},{112,96},{1... | collective-permute-start | bytes 294920 | tf_op jit(solution)/shard_map/ppermute | solution.py:389
  14.2 0.0 copy-done.3
  14.2 0.0 copy-done.4
  14.2 0.0 copy-done.5
  14.2 0.0 copy-start.1
  14.2 0.0 copy-start.2
  14.2 9.6 %own.1 = (bf16[160,128,128]{2,1,0:T(8,128)(2,1)S(1)}, bf16[128,128,256]{2,1,0:T(8,128)(2,1)S(1)}, bf16[160,16,128]{2,1,0:T(8,128)(2,1)S(1)}, f32[128,8,128]{2,1,...) custom-call(s32[2,4,64]{2,1,0:T(4,128)S(1)} %copy-done.3, ...), custom_call_target="tpu_custom_call" | custom-call | flops 60000002048 | bytes 1000000 | tf_op jit(solution)/shard_map/own/pallas_call | solution.py:391
  23.8 0.0 collective-permute-done.2.prev
  23.8 0.0 collective-permute-done.3.nxt
  23.9 0.0 collective-permute-done.1.above
  23.9 0.0 collective-permute-done.below
  23.9 0.0 copy-done
  23.9 0.0 copy-done.1
  23.9 0.0 copy-done.2
  23.9 19.1 %rest.1 = (f32[3,2,8192]{2,1,0:T(2,128)S(1)}, f32[3,2,8192]{2,1,0:T(2,128)S(1)}, f32[3,2,8192]{2,1,0:T(2,128)S(1)}, f32[16,16]{1,0:T(8,128)S(1)}, bf16[160,128,1...) custom-call(s32[2,4,64]{2,1,0:T(4,128)S(1)} %copy-done.3, ...), custom_call_target="tpu_custom_call", output_to_operand_aliasing={{4}: (17, {}), {5}: (18, {}), {6}: (19, {})} | custom-call | tf_op jit(solution)/shard_map/rest/pallas_call | solution.py:413
  43.0 17.1 %all_to_all.11 = f32[16,1,16]{2,1,0:T(1,128)S(1)} all-to-all(f32[16,1,16]{2,1,0:T(1,128)S(1)} %bitcast.12), channel_id=1, replica_groups=mesh['image'=16,'space'=16] {'space'}, dimensions={0} | all-to-all | bytes 2048 | tf_op jit(solution)/shard_map/all_to_all | solution.py:438
  60.1 1.8 %band.1 = (f32[3,2,8192]{2,1,0:T(2,128)}, f32[2]{0:T(128)}) custom-call(s32[4]{0:T(128)S(1)} %get-tuple-element.20.place, f32[16,16]{1,0:T(8,128)S(1)} %bitcast.11, f32[3,2,8192]{2,1,0:T(2,128)S(1)} %get-tuple-element.33.force, f32[3,2,8192]{2,1,0:T(2,128)S(1)} %get-tuple-element.34.slope, f32[3,2,8192]{2,1,0:T(2,128)S(1)} %get-tuple-element.35.bending), custom_call_target="tpu_custom_call" | custom-call | tf_op jit(solution)/shard_map/band/pallas_call | solution.py:439
  (5 shorter events, 0.0 us)
Async XLA Ops:
  0.6 0.9 %copy-start.6 = (f32[2,3,8192]{2,0,1:T(2,128)S(1)}, f32[2,3,8192]{2,0,1:T(2,128)}, u32[]{:S(2)}) copy-start(f32[2,3,8192]{2,0,1:T(2,128)} %param.8) | copy-start | bytes 589828
  1.6 0.8 %copy-start.7 = (s32[8192]{0:T(1024)S(1)}, s32[8192]{0:T(1024)}, u32[]{:S(2)}) copy-start(s32[8192]{0:T(1024)} %param.11) | copy-start | bytes 98308
  2.3 11.9 %copy-start.3 = (s32[2,4,64]{2,1,0:T(4,128)S(1)}, s32[2,4,64]{2,1,0:T(4,128)}, u32[]{:S(2)}) copy-start(s32[2,4,64]{2,1,0:T(4,128)} %lists.3) | copy-start | bytes 6148
  2.3 11.9 %copy-start.4 = (f32[64]{0:T(128)S(1)}, f32[64]{0:T(128)}, u32[]{:S(2)}) copy-start(f32[64]{0:T(128)} %param.12) | copy-start | bytes 772
  2.3 11.9 %copy-start.5 = (f32[64]{0:T(128)S(1)}, f32[64]{0:T(128)}, u32[]{:S(2)}) copy-start(f32[64]{0:T(128)} %param.13) | copy-start | bytes 772
  3.0 20.9 %collective-permute-start.1 = (f32[4,2,8192]{2,1,0:T(2,128)S(1)}, f32[4,2,8192]{2,1,0:T(2,128)S(1)}, u32[]{:S(2)}, u32[]{:S(2)}) collective-permute-start(f32[4,2,8192]{2,1,0:T(2,128)S(1)} %get-tuple-element.21.coords), channel_id=1, source_target_pairs={{0,15},{1,0},{2,1},{3,2},{4,3},{5,4},{6,5},{7,6},{8,7},{9,8},{10,9... | collective-permute-start | bytes 786440 | tf_op jit(solution)/shard_map/ppermute | solution.py:387
  11.5 12.3 %collective-permute-start = (f32[4,2,8192]{2,1,0:T(2,128)S(1)}, f32[4,2,8192]{2,1,0:T(2,128)S(1)}, u32[]{:S(2)}, u32[]{:S(2)}) collective-permute-start(f32[4,2,8192]{2,1,0:T(2,128)S(1)} %get-tuple-element.21.coords), channel_id=1, source_target_pairs={{0,1},{1,2},{2,3},{3,4},{4,5},{5,6},{6,7},{7,8},{8,9},{9,10},{10,1... | collective-permute-start | bytes 786440 | tf_op jit(solution)/shard_map/ppermute | solution.py:386
  11.5 12.3 %collective-permute-start.2 = (f32[3,1,8192]{2,1,0:T(1,128)S(1)}, f32[3,1,8192]{2,1,0:T(1,128)S(1)}, u32[]{:S(2)}, u32[]{:S(2)}) collective-permute-start(f32[3,1,8192]{2,1,0:T(1,128)S(1)} %get-tuple-element.25), channel_id=1, source_target_pairs={{0,16},{16,32},{32,48},{48,64},{64,80},{80,96},{96,112},{112,128},... | collective-permute-start | bytes 294920 | tf_op jit(solution)/shard_map/ppermute | solution.py:388
  11.5 12.3 %collective-permute-start.3 = (f32[3,1,8192]{2,1,0:T(1,128)S(1)}, f32[3,1,8192]{2,1,0:T(1,128)S(1)}, u32[]{:S(2)}, u32[]{:S(2)}) collective-permute-start(f32[3,1,8192]{2,1,0:T(1,128)S(1)} %get-tuple-element.26), channel_id=1, source_target_pairs={{0,240},{16,0},{32,16},{48,32},{64,48},{80,64},{96,80},{112,96},{1... | collective-permute-start | bytes 294920 | tf_op jit(solution)/shard_map/ppermute | solution.py:389
  14.2 9.7 %copy-start = (f32[3,8192]{1,0:T(4,128)S(1)}, f32[3,8192]{1,0:T(4,128)}, u32[]{:S(2)}) copy-start(f32[3,8192]{1,0:T(4,128)} %ref.1) | copy-start | bytes 294916
  14.2 9.7 %copy-start.1 = (f32[8192]{0:T(1024)S(1)}, f32[8192]{0:T(1024)}, u32[]{:S(2)}) copy-start(f32[8192]{0:T(1024)} %param.10) | copy-start | bytes 98308
  14.2 9.7 %copy-start.2 = (s32[2,2,1024]{2,1,0:T(2,128)S(1)}, s32[2,2,1024]{2,1,0:T(2,128)}, u32[]{:S(2)}) copy-start(s32[2,2,1024]{2,1,0:T(2,128)} %hidx.1) | copy-start | bytes 49156

commit v9 on v8

--- a/solution.py
+++ b/solution.py
@@ -9,7 +9,7 @@
 PARTNERS = 4
 BLOCK = 16
 BUILD = 16
-OWN_BUILD = 32
+OWN_BUILD = 64
 spring_k = 2.0
 small_eps = 1e-06
 f32, bf16 = jnp.float32, jnp.bfloat16

time: 62.4 us -> 62.6 us (level)
  blocking collectives: 17.1 us -> 18.3 us
  Pallas kernels: 31.1 us -> 30.2 us
    pallas_call x1, Pallas kernels: 19.1 us -> 16.9 us  [body(): pl.pallas_call(rest_kernel, out_shape=(shape((3, images, atoms)), shape((...]
    pallas_call x1, Pallas kernels: 9.61 us -> 10.9 us  [body(): pl.pallas_call(own_kernel, out_shape=(shape((images * tiles_ext, TILE, TI...]
    all_to_all x1, blocking collectives: 17.1 us -> 18.3 us  [body(): shares = lax.all_to_all(sums, 'space', 0, 0, tiled=True)]
  transfers between devices with their start and end apart: 4 -> 4, of which waited for: 0 -> 0; matrix products, arithmetic and copies ran while one was open for 0% -> 0% of each run, Pallas kernels for 15% -> 18%
where the time goes in v9:
time: 62.6 us; the launch traced here: 62.3 us
  Pallas kernels  30.2 us (48%)
  blocking collectives  18.3 us (29%)
  starting transfers between devices  11.2 us (18%)
  local copies, waits for them, and re-layouts  1.7 us (3%)
  between operations  0.9 us (1%)
    all_to_all x1, blocking collectives, body(): shares = lax.all_to_all(sums, 'space', 0, 0, tiled=True)  18.3 us
    pallas_call x1, Pallas kernels, body(): pl.pallas_call(rest_kernel, out_shape=(shape((3, images, atoms)), shape((...  16.9 us
    pallas_call x1, Pallas kernels, body(): pl.pallas_call(own_kernel, out_shape=(shape((images * tiles_ext, TILE, TI...  10.9 us
    ppermute x1, starting transfers between devices, body(): above = lax.ppermute(feats, 'space', ring('space', -1))  8.56 us
    ppermute x1, starting transfers between devices, body(): nxt = lax.ppermute(first, 'image', ring('image', -1))  2.64 us
    pallas_call x1, Pallas kernels, body(): pl.pallas_call(band_kernel, out_shape=(shape((3, images, atoms)), shape((...  1.76 us
    unnamed x16, local copies, waits for them, and re-layouts  1.7 us
  transfers between devices with their start and end apart: 4, of which 0 were waited for; matrix products, arithmetic and copies ran while one was open for 0% of the time, Pallas kernels for 18%

profile of v9, /device:TPU:6, one launch (start us, length us, event | category | flops | bytes accessed | tf_op | source)
XLA Modules:
  0.0 62.3 jit_solution(7064631452915789401)
XLA Ops:
  0.6 0.0 copy-start.6
  0.6 0.9 %copy-done.6 = f32[2,3,8192]{2,0,1:T(2,128)S(1)} copy-done((f32[2,3,8192]{2,0,1:T(2,128)S(1)}, f32[2,3,8192]{2,0,1:T(2,128)}, u32[]{:S(2)}) %copy-start.6) | copy-done | bytes 196632
  1.6 0.8 %copy-done.7 = s32[8192]{0:T(1024)S(1)} copy-done((s32[8192]{0:T(1024)S(1)}, s32[8192]{0:T(1024)}, u32[]{:S(2)}) %copy-start.7) | copy-done | bytes 32792
  2.3 0.6 %prep.1 = (f32[4,2,8192]{2,1,0:T(2,128)S(1)}, f32[3,1,8192]{2,1,0:T(1,128)S(1)}, f32[3,1,8192]{2,1,0:T(1,128)S(1)}, s32[4]{0:T(128)S(1)}) custom-call(f32[3,2,8192]{2,1,0:T(2,128)S(1)} %bitcast.17, s32[64,128]{1,0:T(8,128)S(1)} %bitcast.18), custom_call_target="tpu_custom_call" | custom-call | flops 10000000000 | bytes 1000000 | tf_op jit(solution)/shard_map/prep/pallas_call | solution.py:372
  3.0 8.6 %collective-permute-start.1 = (f32[4,2,8192]{2,1,0:T(2,128)S(1)}, f32[4,2,8192]{2,1,0:T(2,128)S(1)}, u32[]{:S(2)}, u32[]{:S(2)}) collective-permute-start(f32[4,2,8192]{2,1,0:T(2,128)S(1)} %get-tuple-element.21.coords), channel_id=1, source_target_pairs={{0,15},{1,0},{2,1},{3,2},{4,3},{5,4},{6,5},{7,6},{8,7},{9,8},{10,9... | collective-permute-start | bytes 786440 | tf_op jit(solution)/shard_map/ppermute | solution.py:387
  11.5 0.0 collective-permute-start
  11.5 0.0 collective-permute-start.2
  11.5 2.6 %collective-permute-start.3 = (f32[3,1,8192]{2,1,0:T(1,128)S(1)}, f32[3,1,8192]{2,1,0:T(1,128)S(1)}, u32[]{:S(2)}, u32[]{:S(2)}) collective-permute-start(f32[3,1,8192]{2,1,0:T(1,128)S(1)} %get-tuple-element.26), channel_id=1, source_target_pairs={{0,240},{16,0},{32,16},{48,32},{64,48},{80,64},{96,80},{112,96},{1... | collective-permute-start | bytes 294920 | tf_op jit(solution)/shard_map/ppermute | solution.py:389
  14.2 0.0 copy-done.3
  14.2 0.0 copy-done.4
  14.2 0.0 copy-done.5
  14.2 0.0 copy-start.1
  14.2 0.0 copy-start.2
  14.2 10.9 %own.1 = (bf16[160,128,128]{2,1,0:T(8,128)(2,1)S(1)}, bf16[128,128,256]{2,1,0:T(8,128)(2,1)S(1)}, bf16[160,16,128]{2,1,0:T(8,128)(2,1)S(1)}, f32[128,8,128]{2,1,...) custom-call(s32[2,4,64]{2,1,0:T(4,128)S(1)} %copy-done.3, ...), custom_call_target="tpu_custom_call" | custom-call | flops 60000002048 | bytes 1000000 | tf_op jit(solution)/shard_map/own/pallas_call | solution.py:391
  25.2 0.0 collective-permute-done.2.prev
  25.2 0.0 collective-permute-done.3.nxt
  25.2 0.0 collective-permute-done.1.above
  25.2 0.0 collective-permute-done.below
  25.2 0.0 copy-done
  25.2 0.0 copy-done.1
  25.2 0.0 copy-done.2
  25.3 16.9 %rest.1 = (f32[3,2,8192]{2,1,0:T(2,128)S(1)}, f32[3,2,8192]{2,1,0:T(2,128)S(1)}, f32[3,2,8192]{2,1,0:T(2,128)S(1)}, f32[16,16]{1,0:T(8,128)S(1)}, bf16[160,128,1...) custom-call(s32[2,4,64]{2,1,0:T(4,128)S(1)} %copy-done.3, ...), custom_call_target="tpu_custom_call", output_to_operand_aliasing={{4}: (17, {}), {5}: (18, {}), {6}: (19, {})} | custom-call | tf_op jit(solution)/shard_map/rest/pallas_call | solution.py:413
  42.1 18.3 %all_to_all.11 = f32[16,1,16]{2,1,0:T(1,128)S(1)} all-to-all(f32[16,1,16]{2,1,0:T(1,128)S(1)} %bitcast.12), channel_id=1, replica_groups=mesh['image'=16,'space'=16] {'space'}, dimensions={0} | all-to-all | bytes 2048 | tf_op jit(solution)/shard_map/all_to_all | solution.py:438
  60.4 1.8 %band.1 = (f32[3,2,8192]{2,1,0:T(2,128)}, f32[2]{0:T(128)}) custom-call(s32[4]{0:T(128)S(1)} %get-tuple-element.20.place, f32[16,16]{1,0:T(8,128)S(1)} %bitcast.11, f32[3,2,8192]{2,1,0:T(2,128)S(1)} %get-tuple-element.33.force, f32[3,2,8192]{2,1,0:T(2,128)S(1)} %get-tuple-element.34.slope, f32[3,2,8192]{2,1,0:T(2,128)S(1)} %get-tuple-element.35.bending), custom_call_target="tpu_custom_call" | custom-call | tf_op jit(solution)/shard_map/band/pallas_call | solution.py:439
  (5 shorter events, 0.0 us)
Async XLA Ops:
  0.6 0.9 %copy-start.6 = (f32[2,3,8192]{2,0,1:T(2,128)S(1)}, f32[2,3,8192]{2,0,1:T(2,128)}, u32[]{:S(2)}) copy-start(f32[2,3,8192]{2,0,1:T(2,128)} %param.8) | copy-start | bytes 589828
  1.6 0.8 %copy-start.7 = (s32[8192]{0:T(1024)S(1)}, s32[8192]{0:T(1024)}, u32[]{:S(2)}) copy-start(s32[8192]{0:T(1024)} %param.11) | copy-start | bytes 98308
  2.3 11.9 %copy-start.3 = (s32[2,4,64]{2,1,0:T(4,128)S(1)}, s32[2,4,64]{2,1,0:T(4,128)}, u32[]{:S(2)}) copy-start(s32[2,4,64]{2,1,0:T(4,128)} %lists.3) | copy-start | bytes 6148
  2.3 11.9 %copy-start.4 = (f32[64]{0:T(128)S(1)}, f32[64]{0:T(128)}, u32[]{:S(2)}) copy-start(f32[64]{0:T(128)} %param.12) | copy-start | bytes 772
  2.3 11.9 %copy-start.5 = (f32[64]{0:T(128)S(1)}, f32[64]{0:T(128)}, u32[]{:S(2)}) copy-start(f32[64]{0:T(128)} %param.13) | copy-start | bytes 772
  3.0 22.2 %collective-permute-start.1 = (f32[4,2,8192]{2,1,0:T(2,128)S(1)}, f32[4,2,8192]{2,1,0:T(2,128)S(1)}, u32[]{:S(2)}, u32[]{:S(2)}) collective-permute-start(f32[4,2,8192]{2,1,0:T(2,128)S(1)} %get-tuple-element.21.coords), channel_id=1, source_target_pairs={{0,15},{1,0},{2,1},{3,2},{4,3},{5,4},{6,5},{7,6},{8,7},{9,8},{10,9... | collective-permute-start | bytes 786440 | tf_op jit(solution)/shard_map/ppermute | solution.py:387
  11.5 13.7 %collective-permute-start = (f32[4,2,8192]{2,1,0:T(2,128)S(1)}, f32[4,2,8192]{2,1,0:T(2,128)S(1)}, u32[]{:S(2)}, u32[]{:S(2)}) collective-permute-start(f32[4,2,8192]{2,1,0:T(2,128)S(1)} %get-tuple-element.21.coords), channel_id=1, source_target_pairs={{0,1},{1,2},{2,3},{3,4},{4,5},{5,6},{6,7},{7,8},{8,9},{9,10},{10,1... | collective-permute-start | bytes 786440 | tf_op jit(solution)/shard_map/ppermute | solution.py:386
  11.5 13.6 %collective-permute-start.2 = (f32[3,1,8192]{2,1,0:T(1,128)S(1)}, f32[3,1,8192]{2,1,0:T(1,128)S(1)}, u32[]{:S(2)}, u32[]{:S(2)}) collective-permute-start(f32[3,1,8192]{2,1,0:T(1,128)S(1)} %get-tuple-element.25), channel_id=1, source_target_pairs={{0,16},{16,32},{32,48},{48,64},{64,80},{80,96},{96,112},{112,128},... | collective-permute-start | bytes 294920 | tf_op jit(solution)/shard_map/ppermute | solution.py:388
  11.5 13.7 %collective-permute-start.3 = (f32[3,1,8192]{2,1,0:T(1,128)S(1)}, f32[3,1,8192]{2,1,0:T(1,128)S(1)}, u32[]{:S(2)}, u32[]{:S(2)}) collective-permute-start(f32[3,1,8192]{2,1,0:T(1,128)S(1)} %get-tuple-element.26), channel_id=1, source_target_pairs={{0,240},{16,0},{32,16},{48,32},{64,48},{80,64},{96,80},{112,96},{1... | collective-permute-start | bytes 294920 | tf_op jit(solution)/shard_map/ppermute | solution.py:389
  14.2 11.0 %copy-start = (f32[3,8192]{1,0:T(4,128)S(1)}, f32[3,8192]{1,0:T(4,128)}, u32[]{:S(2)}) copy-start(f32[3,8192]{1,0:T(4,128)} %ref.1) | copy-start | bytes 294916
  14.2 11.0 %copy-start.1 = (f32[8192]{0:T(1024)S(1)}, f32[8192]{0:T(1024)}, u32[]{:S(2)}) copy-start(f32[8192]{0:T(1024)} %param.10) | copy-start | bytes 98308
  14.2 11.0 %copy-start.2 = (s32[2,2,1024]{2,1,0:T(2,128)S(1)}, s32[2,2,1024]{2,1,0:T(2,128)}, u32[]{:S(2)}) copy-start(s32[2,2,1024]{2,1,0:T(2,128)} %hidx.1) | copy-start | bytes 49156
